TPU v7x, 256 devices: a whole 4x4x8 slice. The times are simulated.
256 devices in a mesh: dp: 4 (over x_hi, core), expert: 64 (over x_lo, y, z).
Axes of the slice: x: 4 (x_hi: 2, x_lo: 2; x = x_hi * 2 + x_lo), y: 4, z: 8, core: 2. Of those that a mesh axis runs over, the one named last changes fastest.
Arguments:
- tokens_in: bfloat16 [2, 2048, 2048], P(None, 'expert', 'dp'), may hold values from -6 to 6
- route_ids: int32 [2, 2048, 8], P(None, 'expert'), may hold values from 0 to 127, all different within a row; in each aligned block of 32 rows (0 to 31, 32 to 63, ..., all dimensions but the last counted through in order) at most 4 rows name the same one
- route_gates: float32 [2, 2048, 8], P(None, 'expert'), may hold values from 0.1 to 1
- cotangent: bfloat16 [2, 2048, 2048], P(None, 'expert', 'dp'), may hold values from -0.75 to 0.75
- gate_proj: bfloat16 [128, 1024, 1536], P(None, 'expert', 'dp'), may hold values from -0.125 to 0.125
- up_proj: bfloat16 [128, 1024, 1536], P(None, 'expert', 'dp'), may hold values from -0.125 to 0.125
- down_proj: bfloat16 [128, 1024, 1536], P(None, 'expert', 'dp'), may hold values from -0.21875 to 0.21875
- replica_plan: int32 [2, 64], replicated, may hold values from 0 to 127, as said below
- capacity: int32 [2, 128], replicated, may hold values from 1 to 2, as said below
Outputs:
- y_out: bfloat16 [2, 2048, 2048], P(None, 'expert', 'dp')
- x_grad: bfloat16 [2, 2048, 2048], P(None, 'expert', 'dp')
- gate_grad: bfloat16 [128, 1024, 1536], P(None, 'expert', 'dp')
- up_grad: bfloat16 [128, 1024, 1536], P(None, 'expert', 'dp')
- down_grad: bfloat16 [128, 1024, 1536], P(None, 'expert', 'dp')
Inputs may be any that keep to these rules, and one draw needn't show every extreme that they name: `route_ids`: each token names 8 different experts; among the tokens of one micro-batch on one index of the expert axis (an aligned block of 32), no expert is named more than 2 * 2 times. `replica_plan`: an expert may fill the replica slot of several devices, or of none. Some expert has capacity 2 in every micro-batch.
All inputs are finite; a program needn't handle non-finite values.
Results may differ from a plain program's by a relative error of at most 0.012.
Values may be sent and summed in bfloat16 or wider, within the bound.
No kernel may reach another device: no remote copies, remote signals or barrier semaphores. Data moves between devices by JAX's collectives and lax.ppermute only.
A program may use at most 192 MiB of HBM per device.

v0:
```python
from functools import reduce

import jax
import jax.numpy as jnp
from jax import lax
from jax.sharding import PartitionSpec as P


def sent_together(arrays, axis, split_dim, concat_dim, along):
    both = jnp.concatenate(arrays, axis=along)
    filled, at, done = (
        lax.all_to_all(both, axis, split_axis=split_dim, concat_axis=concat_dim, tiled=True),
        0,
        [],
    )
    for a in arrays:
        done.append(lax.slice_in_dim(filled, at, at + a.shape[along], axis=along))
        at += a.shape[along]
    return tuple(done)


def in_one_piece(arrays, axis, dim, along):
    both = jnp.concatenate(arrays, axis=along)
    filled, at, done = (lax.psum_scatter(both, axis, scatter_dimension=dim, tiled=True), 0, [])
    for a in arrays:
        done.append(lax.slice_in_dim(filled, at, at + a.shape[along], axis=along))
        at += a.shape[along]
    return tuple(done)


def route_slots(batch_ids, batch_plan, batch_caps, source, device_count, row_cap):
    expert_count = batch_caps.shape[0]
    tok_count = batch_ids.shape[0]
    expert_ids = jnp.arange(expert_count, dtype=jnp.int32)
    hosting = (batch_plan[None, :] == expert_ids[:, None]).astype(jnp.int32)
    ranking = jnp.cumsum(hosting, axis=1)
    copies = 1 + ranking[:, -1]
    copy_ids = jnp.arange(device_count + 1, dtype=jnp.int32)
    matched = hosting[:, :, None] * (ranking[:, :, None] == copy_ids[None, None, :]).astype(
        jnp.int32
    )
    replica_dev = jnp.sum(
        matched * jnp.arange(device_count, dtype=jnp.int32)[None, :, None], axis=1
    )
    home_target = 3 * (expert_ids // 2) + expert_ids % 2
    target_table = jnp.where(copy_ids[None, :] == 0, home_target[:, None], 3 * replica_dev + 2)
    matches = (batch_ids[:, :, None] == expert_ids[None, None, :]).astype(jnp.int32)
    copies_route = jnp.sum(matches * copies[None, None, :], axis=2)
    token_ids = source * tok_count + jnp.arange(tok_count, dtype=jnp.int32)
    chosen = token_ids[:, None] % copies_route
    row_table = jnp.sum(matches[:, :, :, None] * target_table[None, None, :, :], axis=2)
    target = jnp.sum(
        row_table * (chosen[:, :, None] == copy_ids[None, None, :]).astype(jnp.int32), axis=2
    )
    limits = jnp.sum(matches * batch_caps[None, None, :], axis=2)
    flat_target = target.reshape(-1)
    slot_ids = jnp.arange(device_count * 3, dtype=jnp.int32)
    onehot = (flat_target[:, None] == slot_ids[None, :]).astype(jnp.int32)
    before = jnp.sum((jnp.cumsum(onehot, axis=0) - onehot) * onehot, axis=1).reshape(target.shape)
    return jnp.where(before < limits, target * row_cap + before, -1)


def slot_blocks(slot_experts, gate_proj, up_proj, down_proj):
    flat_ids = slot_experts.reshape(-1)
    return tuple(
        (
            jnp.take(weights, flat_ids, axis=0).reshape(slot_experts.shape + weights.shape[1:])
            for weights in (gate_proj, up_proj, down_proj)
        )
    )


def split_pairs(weights):
    return weights.reshape(weights.shape[:3] + (2, weights.shape[3] // 2))


def expert_work(rows_in, grads_in, slot_weights, device_count):
    gate_w, up_w, down_w = tuple((split_pairs(blocks) for blocks in slot_weights))
    pair_rows = gate_w.shape[2]
    leading = rows_in.shape[:3]
    rows_split = rows_in.reshape(leading + (device_count, pair_rows, 2))
    grads_split = grads_in.reshape(leading + (device_count, pair_rows, 2))
    pre_gate = jnp.einsum(
        "nscjrh,jsrhf->nscf", rows_split, gate_w, preferred_element_type=jnp.float32
    )
    pre_up = jnp.einsum("nscjrh,jsrhf->nscf", rows_split, up_w, preferred_element_type=jnp.float32)
    logistic = jax.nn.sigmoid(pre_gate)
    swished = pre_gate * logistic
    hidden = (swished * pre_up).astype(jnp.bfloat16)
    partial_value = jnp.einsum(
        "nscf,jsrhf->nscjrh", hidden, down_w, preferred_element_type=jnp.float32
    )
    partial_value = partial_value.astype(jnp.bfloat16).reshape(rows_in.shape)
    hidden_grad = jnp.einsum(
        "nscjrh,jsrhf->nscf", grads_split, down_w, preferred_element_type=jnp.float32
    )
    gate_pre_grad = (hidden_grad * pre_up * logistic * (1.0 + pre_gate * (1.0 - logistic))).astype(
        jnp.bfloat16
    )
    up_pre_grad = (hidden_grad * swished).astype(jnp.bfloat16)
    input_partial = jnp.einsum(
        "nscf,jsrhf->nscjrh", gate_pre_grad, gate_w, preferred_element_type=jnp.float32
    )
    input_partial = input_partial + jnp.einsum(
        "nscf,jsrhf->nscjrh", up_pre_grad, up_w, preferred_element_type=jnp.float32
    )
    input_partial = input_partial.astype(jnp.bfloat16).reshape(rows_in.shape)
    stored_shape = slot_weights[0].shape
    gate_grad = jnp.einsum(
        "nscjrh,nscf->jsrhf", rows_split, gate_pre_grad, preferred_element_type=jnp.float32
    )
    up_grad = jnp.einsum(
        "nscjrh,nscf->jsrhf", rows_split, up_pre_grad, preferred_element_type=jnp.float32
    )
    down_grad = jnp.einsum(
        "nscf,nscjrh->jsrhf", hidden, grads_split, preferred_element_type=jnp.float32
    )
    grads = tuple((member.reshape(stored_shape) for member in (gate_grad, up_grad, down_grad)))
    return (partial_value, input_partial, grads)


def shards(
    tokens_in,
    route_ids,
    route_gates,
    cotangent,
    gate_proj,
    up_proj,
    down_proj,
    replica_plan,
    capacity,
):
    device_count = lax.axis_size("expert")
    source = lax.axis_index("expert")
    expert_count = gate_proj.shape[0]
    micro_count, tok_count, top_count = route_ids.shape
    row_cap = max(2, tok_count * top_count // expert_count)
    buffer_rows = device_count * 3 * row_cap
    devices = jnp.arange(device_count, dtype=jnp.int32)
    home_slots = jnp.stack([2 * devices, 2 * devices + 1], axis=1)
    first_slots = jnp.concatenate([home_slots, replica_plan[0][:, None]], axis=1)
    all_slots = jnp.concatenate([first_slots, replica_plan[1][:, None]], axis=1)
    gate_all, up_all, down_all = slot_blocks(all_slots, gate_proj, up_proj, down_proj)
    arrived = sent_together((gate_all, up_all, down_all), "expert", 0, 0, 1)
    batch_weights = [
        tuple((blocks[:, :3] for blocks in arrived)),
        tuple((jnp.concatenate([blocks[:, :2], blocks[:, 3:]], axis=1) for blocks in arrived)),
    ]
    row_ids = jnp.arange(buffer_rows, dtype=jnp.int32)
    outputs = []
    input_grads = []
    slot_grads = []
    for batch_index in range(micro_count):
        row_slots = route_slots(
            route_ids[batch_index],
            replica_plan[batch_index],
            capacity[batch_index],
            source,
            device_count,
            row_cap,
        )
        select = (row_slots[:, :, None] == row_ids[None, None, :]).astype(jnp.float32)
        placing = jnp.sum(select, axis=1)
        weighting = jnp.sum(select * route_gates[batch_index][:, :, None], axis=1)
        spread = placing.T.astype(jnp.bfloat16)
        rows_out = jnp.dot(
            spread, tokens_in[batch_index], preferred_element_type=jnp.float32
        ).astype(jnp.bfloat16)
        grads_out = jnp.dot(
            weighting.T, cotangent[batch_index].astype(jnp.float32), precision=lax.Precision.HIGHEST
        ).astype(jnp.bfloat16)
        shape_part = (device_count, 3, row_cap, rows_out.shape[1])
        rows_part, grads_part = (
            lax.all_to_all(
                rows_out.reshape(shape_part), "expert", split_axis=0, concat_axis=0, tiled=True
            ),
            lax.all_to_all(
                grads_out.reshape(shape_part), "expert", split_axis=0, concat_axis=0, tiled=True
            ),
        )
        rows_in, grads_in = (
            lax.all_gather(rows_part, "dp", axis=3, tiled=True),
            lax.all_gather(grads_part, "dp", axis=3, tiled=True),
        )
        partial_value, input_partial, grads = expert_work(
            rows_in, grads_in, batch_weights[batch_index], device_count
        )
        output_sum, input_sum = tuple(
            (
                part.astype(jnp.float32)
                for part in in_one_piece((partial_value, input_partial), "dp", 3, 0)
            )
        )
        output_back, input_back = (
            lax.all_to_all(
                output_sum.astype(jnp.bfloat16), "expert", split_axis=0, concat_axis=0, tiled=True
            ),
            lax.all_to_all(
                input_sum.astype(jnp.bfloat16), "expert", split_axis=0, concat_axis=0, tiled=True
            ),
        )
        output_flat = output_back.reshape(buffer_rows, -1).astype(jnp.float32)
        input_flat = input_back.reshape(buffer_rows, -1).astype(jnp.float32)
        outputs.append(
            jnp.dot(weighting, output_flat, precision=lax.Precision.HIGHEST).astype(jnp.bfloat16)
        )
        input_grads.append(
            jnp.dot(placing, input_flat, precision=lax.Precision.HIGHEST).astype(jnp.bfloat16)
        )
        slot_grads.append(grads)
    home_terms = tuple(
        (
            reduce(jnp.add, [grads[member][:, :2] for grads in slot_grads]).astype(jnp.bfloat16)
            for member in range(3)
        )
    )
    replica_terms = tuple(
        (
            jnp.concatenate([grads[member][:, 2:] for grads in slot_grads], axis=1).astype(
                jnp.bfloat16
            )
            for member in range(3)
        )
    )
    send_gate, send_up, send_down = tuple(
        (
            jnp.concatenate([home_part, replica_part], axis=1)
            for home_part, replica_part in zip(home_terms, replica_terms)
        )
    )
    received = (
        lax.all_to_all(send_gate, "expert", split_axis=0, concat_axis=0, tiled=True),
        lax.all_to_all(send_up, "expert", split_axis=0, concat_axis=0, tiled=True),
        lax.all_to_all(send_down, "expert", split_axis=0, concat_axis=0, tiled=True),
    )
    grad_slots = jnp.concatenate([home_slots, replica_plan.T], axis=1).reshape(-1)
    owners = (jnp.arange(expert_count, dtype=jnp.int32)[:, None] == grad_slots[None, :]).astype(
        jnp.bfloat16
    )
    totals = tuple(
        (
            jnp.dot(
                owners, blocks.reshape(grad_slots.shape[0], -1), preferred_element_type=jnp.float32
            )
            .astype(jnp.bfloat16)
            .reshape((expert_count,) + blocks.shape[2:])
            for blocks in received
        )
    )
    return (jnp.stack(outputs), jnp.stack(input_grads), totals[0], totals[1], totals[2])


def solution(mesh):
    in_specs = (
        P(None, "expert", "dp"),
        P(None, "expert", None),
        P(None, "expert", None),
        P(None, "expert", "dp"),
        P(None, "expert", "dp"),
        P(None, "expert", "dp"),
        P(None, "expert", "dp"),
        P(),
        P(),
    )
    out_specs = (
        P(None, "expert", "dp"),
        P(None, "expert", "dp"),
        P(None, "expert", "dp"),
        P(None, "expert", "dp"),
        P(None, "expert", "dp"),
    )
    return jax.shard_map(shards, mesh=mesh, in_specs=in_specs, out_specs=out_specs, check_vma=False)
```

profile of v0, /device:TPU:6, one launch (start us, length us, event | category | flops | bytes accessed | tf_op | source)
XLA Modules:
  0.0 883.7 jit_solution(3002898317803778142)
XLA Ops:
  11.2 35.6 %multiply_reduce_fusion = s32[32,8,65]{1,2,0:T(8,128)S(1)} fusion(s32[128,65]{0,1:T(8,128)S(1)} %get-tuple-element.42, s32[32,8,128]{2,1,0:T(8,128)S(1)} %fusion.116), kind=kLoop, calls=%fused_computation.4 | loop fusion | flops 4243200 | bytes 230912 | tf_op jit(solution)/shard_map/reduce_sum | solution.py:51
  53.1 13.2 %all-to-all-start.4 = ((bf16[64,3,2,512]{3,2,1,0:T(2,128)(2,1)}), bf16[64,3,2,512]{3,2,1,0:T(2,128)(2,1)S(1)}, u32[]{:S(2)}, u32[]{:S(2)}) async-start(bf16[64,3,2,512]{3,2,1,0:T(2,128)(2,1)} %reshape.448), calls=%async_computation.5 | async-start | bytes 786432 | tf_op jit(solution)/shard_map/all_to_all | solution.py:174
  66.5 35.3 %multiply_reduce_fusion.1 = s32[32,8,65]{1,2,0:T(8,128)S(1)} fusion(s32[128,65]{0,1:T(8,128)S(1)} %get-tuple-element.41, s32[32,8,128]{2,1,0:T(8,128)S(1)} %fusion.118), kind=kLoop, calls=%fused_computation.5 | loop fusion | flops 4243200 | bytes 230912 | tf_op jit(solution)/shard_map/reduce_sum | solution.py:51
  105.4 11.3 %all-to-all-start.5 = ((bf16[64,3,2,512]{3,2,1,0:T(2,128)(2,1)}), bf16[64,3,2,512]{3,2,1,0:T(2,128)(2,1)S(1)}, u32[]{:S(2)}, u32[]{:S(2)}) async-start(bf16[64,3,2,512]{3,2,1,0:T(2,128)(2,1)} %reshape.452), calls=%async_computation.6 | async-start | bytes 786432 | tf_op jit(solution)/shard_map/all_to_all | solution.py:177
  119.7 12.5 %all-to-all-done.5 = bf16[64,3,2,512]{3,2,1,0:T(2,128)(2,1)S(1)} async-done(((bf16[64,3,2,512]{3,2,1,0:T(2,128)(2,1)}), bf16[64,3,2,512]{3,2,1,0:T(2,128)(2,1)S(1)}, u32[]{:S(2)}, u32[]{:S(2)}) %all-to-all-start.5) | async-done | bytes 393248 | tf_op jit(solution)/shard_map/all_to_all | solution.py:177
  152.9 11.5 %all-to-all-start.2 = ((bf16[64,3,2,512]{3,2,1,0:T(2,128)(2,1)}), bf16[64,3,2,512]{3,2,1,0:T(2,128)(2,1)}, u32[]{:S(2)}, u32[]{:S(2)}) async-start(bf16[64,3,2,512]{3,2,1,0:T(2,128)(2,1)} %reshape.440), calls=%async_computation.2 | async-start | bytes 786432 | tf_op jit(solution)/shard_map/all_to_all | solution.py:177
  191.4 41.1 %all-gather.9.cloned.1.call-done = bf16[64,3,2,2048]{0,3,2,1:T(8,128)(2,1)} async-done(((bf16[64,3,2,512]{0,3,2,1:T(8,128)(2,1)}), bf16[64,3,2,2048]{0,3,2,1:T(8,128)(2,1)}) %all-gather.9.cloned.1.call-update) | async-done | bytes 1572880 | tf_op jit(solution)/shard_map/all_gather | solution.py:182
  232.5 9.1 %copy.225 = bf16[64,3,2,64,16,2]{3,0,4,5,2,1:T(8,128)(2,1)} copy(bf16[64,3,2,64,16,2]{0,5,4,3,2,1:T(2,128)(2,1)} %bitcast.272) | data formatting | bytes 3145728 | tf_op jit(solution)/shard_map/reshape | solution.py:81
  241.6 69.5 %all-gather.5.cloned.1.call-done = bf16[64,3,2,2048]{0,3,2,1:T(8,128)(2,1)} async-done(((bf16[64,3,2,512]{0,3,2,1:T(8,128)(2,1)}), bf16[64,3,2,2048]{0,3,2,1:T(8,128)(2,1)}) %all-gather.5.cloned.1.call-update) | async-done | bytes 1572880 | tf_op jit(solution)/shard_map/all_gather | solution.py:182
  311.2 9.1 %copy.206 = bf16[64,3,2,64,16,2]{3,0,4,5,2,1:T(8,128)(2,1)} copy(bf16[64,3,2,64,16,2]{0,5,4,3,2,1:T(2,128)(2,1)} %bitcast.275) | data formatting | bytes 3145728 | tf_op jit(solution)/shard_map/reshape | solution.py:81
  320.3 66.4 %all-to-all-done = bf16[64,12,16,384]{3,2,1,0:T(8,128)(2,1)} async-done(((bf16[64,12,16,384]{3,2,1,0:T(8,128)(2,1)}), bf16[64,12,16,384]{3,2,1,0:T(8,128)(2,1)}, u32[]{:S(2)}, u32[]{:S(2)}) %all-to-all-start) | async-done | bytes 9437216 | tf_op jit(solution)/shard_map/all_to_all | solution.py:12
  466.8 9.0 %fusion.103 = (bf16[64,3,2,192,1,1]{3,0,2,5,4,1:T(8,128)(2,1)}, bf16[64,3,2,192]{3,0,2,1:T(8,128)(2,1)S(1)}, bf16[64,3,2,192,1,1]{3,0,2,5,4,1:T(8,128)(2,1)S(1)}) fusion(f32[64,3,2,192]{3,0,2,1:T(8,128)} %fusion.83, f32[64,3,2,192]{3,0,2,1:T(8,128)} %fusion.80, bf16[64,3,2,64,16,2]{0,5,4,3,2,1:T(2,128)(2,1)} %bitcast.304, ...), kind=kOutput, calls=%fused_computation.132 | convolution fusion | flops 303095808 | bytes 4964352 | tf_op jit(solution)/shard_map/nscjrh,jsrhf->nscf/dot_general | solution.py:94
  479.9 10.4 %copy.243 = f32[64,3,16,2,192]{4,3,2,1,0:T(2,128)} copy(f32[64,3,16,2,192]{4,0,3,2,1:T(8,128)} %fusion.49) | data formatting | bytes 9437184 | tf_op jit(solution)/shard_map/nscjrh,nscf->jsrhf/transpose | solution.py:109
  513.1 9.4 %fusion.101 = (bf16[64,3,2,192,1,1]{3,0,2,5,4,1:T(8,128)(2,1)}, bf16[64,3,2,192]{3,0,2,1:T(8,128)(2,1)S(1)}, bf16[64,3,2,192,1,1]{3,0,2,5,4,1:T(8,128)(2,1)S(1)}) fusion(f32[64,3,2,192]{3,0,2,1:T(8,128)} %fusion.72, f32[64,3,2,192]{3,0,2,1:T(8,128)} %fusion.69, bf16[64,3,2,64,16,2]{0,5,4,3,2,1:T(2,128)(2,1)} %bitcast.306, ...), kind=kOutput, calls=%fused_computation.130 | convolution fusion | flops 303095808 | bytes 4964352 | tf_op jit(solution)/shard_map/nscjrh,jsrhf->nscf/dot_general | solution.py:94
  527.3 10.3 %copy.241 = f32[64,3,16,2,192]{4,3,2,1,0:T(2,128)} copy(f32[64,3,16,2,192]{4,0,3,2,1:T(8,128)} %fusion.43) | data formatting | bytes 9437184 | tf_op jit(solution)/shard_map/nscjrh,nscf->jsrhf/transpose | solution.py:109
  553.0 10.6 %all-to-all-start.9 = ((bf16[64,4,16,384]{3,2,1,0:T(8,128)(2,1)}), bf16[64,4,16,384]{3,2,1,0:T(8,128)(2,1)}, u32[]{:S(2)}, u32[]{:S(2)}) async-start(bf16[64,4,16,384]{3,2,1,0:T(8,128)(2,1)} %pad_maximum_fusion.3), calls=%async_computation.11 | async-start | bytes 6291456 | tf_op jit(solution)/shard_map/all_to_all | solution.py:232
  576.7 10.2 %copy.247 = f32[64,3,16,2,192]{4,3,2,1,0:T(2,128)} copy(f32[64,3,16,2,192]{4,0,3,2,1:T(8,128)} %fusion.52) | data formatting | bytes 9437184 | tf_op jit(solution)/shard_map/nscjrh,nscf->jsrhf/transpose | solution.py:112
  602.0 10.2 %copy.245 = f32[64,3,16,2,192]{4,3,2,1,0:T(2,128)} copy(f32[64,3,16,2,192]{4,0,3,2,1:T(8,128)} %fusion.46) | data formatting | bytes 9437184 | tf_op jit(solution)/shard_map/nscjrh,nscf->jsrhf/transpose | solution.py:112
  652.9 9.0 %copy.251 = f32[64,3,16,2,192]{4,3,2,1,0:T(2,128)} copy(f32[64,3,16,2,192]{4,2,3,0,1:T(8,128)S(1)} %fusion.58) | data formatting | bytes 9437184 | tf_op jit(solution)/shard_map/nscf,nscjrh->jsrhf/transpose | solution.py:115
  675.7 8.8 copy.249
  738.0 53.2 %all-to-all-done.11 = bf16[64,4,16,384]{3,2,1,0:T(8,128)(2,1)S(1)} async-done(((bf16[64,4,16,384]{3,2,1,0:T(8,128)(2,1)}), bf16[64,4,16,384]{3,2,1,0:T(8,128)(2,1)S(1)}, u32[]{:S(2)}, u32[]{:S(2)}) %all-to-all-start.11) | async-done | bytes 3145760 | tf_op jit(solution)/shard_map/all_to_all | solution.py:234
  802.8 9.4 %all-to-all-done.6 = bf16[64,3,2,512]{3,2,1,0:T(2,128)(2,1)S(1)} async-done(((bf16[64,3,2,512]{3,2,1,0:T(2,128)(2,1)}), bf16[64,3,2,512]{3,2,1,0:T(2,128)(2,1)S(1)}, u32[]{:S(2)}, u32[]{:S(2)}) %all-to-all-start.6) | async-done | bytes 393248 | tf_op jit(solution)/shard_map/all_to_all | solution.py:195
  819.9 11.4 %all-to-all-done.3 = bf16[64,3,2,512]{3,2,1,0:T(2,128)(2,1)} async-done(((bf16[64,3,2,512]{3,2,1,0:T(2,128)(2,1)}), bf16[64,3,2,512]{3,2,1,0:T(2,128)(2,1)}, u32[]{:S(2)}, u32[]{:S(2)}) %all-to-all-start.3) | async-done | bytes 393248 | tf_op jit(solution)/shard_map/all_to_all | solution.py:195
  849.9 11.0 %all-to-all-start.7 = ((bf16[64,3,2,512]{3,2,1,0:T(2,128)(2,1)}), bf16[64,3,2,512]{3,2,1,0:T(2,128)(2,1)}, u32[]{:S(2)}, u32[]{:S(2)}) async-start(bf16[64,3,2,512]{3,2,1,0:T(2,128)(2,1)} %copy.237), calls=%async_computation.9 | async-start | bytes 786432 | tf_op jit(solution)/shard_map/all_to_all | solution.py:198
  (281 shorter events, 380.8 us)
Async XLA Ops:
  7.2 130.5 %copy-start = (bf16[128,16,384]{2,1,0:T(8,128)(2,1)S(1)}, bf16[128,16,384]{2,1,0:T(8,128)(2,1)}, u32[]{:S(2)}) copy-start(bf16[128,16,384]{2,1,0:T(8,128)(2,1)} %param.15) | copy-start | bytes 4718596
  7.2 43.8 %copy-start.45 = (f32[2,32,8]{1,2,0:T(8,128)S(1)}, f32[2,32,8]{1,2,0:T(8,128)}, u32[]{:S(2)}) copy-start(f32[2,32,8]{1,2,0:T(8,128)} %param.13) | copy-start | bytes 6148
  7.2 44.8 %copy-start.42 = (bf16[2,32,512]{2,1,0:T(8,128)(2,1)S(1)}, bf16[2,32,512]{2,1,0:T(8,128)(2,1)}, u32[]{:S(2)}) copy-start(bf16[2,32,512]{2,1,0:T(8,128)(2,1)} %param.11) | copy-start | bytes 196612
  50.5 51.7 %copy-start.43 = (bf16[2,32,512]{2,1,0:T(8,128)(2,1)S(1)}, bf16[2,32,512]{2,1,0:T(8,128)(2,1)}, u32[]{:S(2)}) copy-start(bf16[2,32,512]{2,1,0:T(8,128)(2,1)} %param.14) | copy-start | bytes 196612
  51.4 52.6 %copy-start.36 = (f32[32,384]{1,0:T(8,128)}, f32[32,384]{1,0:T(8,128)S(1)}, u32[]{:S(2)}) copy-start(f32[32,384]{1,0:T(8,128)S(1)} %get-tuple-element.11) | copy-start | bytes 147460
  53.1 52.0 %all-to-all-start.4 = ((bf16[64,3,2,512]{3,2,1,0:T(2,128)(2,1)}), bf16[64,3,2,512]{3,2,1,0:T(2,128)(2,1)S(1)}, u32[]{:S(2)}, u32[]{:S(2)}) async-start(bf16[64,3,2,512]{3,2,1,0:T(2,128)(2,1)} %reshape.448), calls=%async_computation.5 | async-start | bytes 786432 | tf_op jit(solution)/shard_map/all_to_all | solution.py:174
  105.4 26.8 %all-to-all-start.5 = ((bf16[64,3,2,512]{3,2,1,0:T(2,128)(2,1)}), bf16[64,3,2,512]{3,2,1,0:T(2,128)(2,1)S(1)}, u32[]{:S(2)}, u32[]{:S(2)}) async-start(bf16[64,3,2,512]{3,2,1,0:T(2,128)(2,1)} %reshape.452), calls=%async_computation.6 | async-start | bytes 786432 | tf_op jit(solution)/shard_map/all_to_all | solution.py:177
  132.2 20.7 %all-to-all-start.1 = ((bf16[64,3,2,512]{3,2,1,0:T(2,128)(2,1)}), bf16[64,3,2,512]{3,2,1,0:T(2,128)(2,1)}, u32[]{:S(2)}, u32[]{:S(2)}) async-start(bf16[64,3,2,512]{3,2,1,0:T(2,128)(2,1)} %reshape.436), calls=%async_computation.1 | async-start | bytes 786432 | tf_op jit(solution)/shard_map/all_to_all | solution.py:174
  152.9 25.4 %all-to-all-start.2 = ((bf16[64,3,2,512]{3,2,1,0:T(2,128)(2,1)}), bf16[64,3,2,512]{3,2,1,0:T(2,128)(2,1)}, u32[]{:S(2)}, u32[]{:S(2)}) async-start(bf16[64,3,2,512]{3,2,1,0:T(2,128)(2,1)} %reshape.440), calls=%async_computation.2 | async-start | bytes 786432 | tf_op jit(solution)/shard_map/all_to_all | solution.py:177
  178.4 208.4 %all-to-all-start = ((bf16[64,12,16,384]{3,2,1,0:T(8,128)(2,1)}), bf16[64,12,16,384]{3,2,1,0:T(8,128)(2,1)}, u32[]{:S(2)}, u32[]{:S(2)}) async-start(bf16[64,12,16,384]{3,2,1,0:T(8,128)(2,1)} %pad_maximum_fusion), calls=%async_computation | async-start | bytes 18874368 | tf_op jit(solution)/shard_map/all_to_all | solution.py:12
  184.1 48.4 %all-gather.9.cloned.1.call-start = ((), (), s32[]{:S(2)}) async-start(), calls=%async_computation.17 | async-start | bytes 3932160 | tf_op jit(solution)/shard_map/all_gather | solution.py:182
  185.5 125.7 %all-gather.5.cloned.1.call-start = ((), (), s32[]{:S(2)}) async-start(), calls=%async_computation.14 | async-start | bytes 3932160 | tf_op jit(solution)/shard_map/all_gather | solution.py:182
  187.7 279.2 %all-gather.11.cloned.1.call-start = ((), (), s32[]{:S(2)}) async-start(), calls=%async_computation.18 | async-start | bytes 3932160 | tf_op jit(solution)/shard_map/all_gather | solution.py:183
  189.0 324.1 %all-gather.7.cloned.1.call-start = ((), (), s32[]{:S(2)}) async-start(), calls=%async_computation.15 | async-start | bytes 3932160 | tf_op jit(solution)/shard_map/all_gather | solution.py:183
  553.0 81.7 %all-to-all-start.9 = ((bf16[64,4,16,384]{3,2,1,0:T(8,128)(2,1)}), bf16[64,4,16,384]{3,2,1,0:T(8,128)(2,1)}, u32[]{:S(2)}, u32[]{:S(2)}) async-start(bf16[64,4,16,384]{3,2,1,0:T(8,128)(2,1)} %pad_maximum_fusion.3), calls=%async_computation.11 | async-start | bytes 6291456 | tf_op jit(solution)/shard_map/all_to_all | solution.py:232
  634.8 78.3 %all-to-all-start.10 = ((bf16[64,4,16,384]{3,2,1,0:T(8,128)(2,1)}), bf16[64,4,16,384]{3,2,1,0:T(8,128)(2,1)}, u32[]{:S(2)}, u32[]{:S(2)}) async-start(bf16[64,4,16,384]{3,2,1,0:T(8,128)(2,1)} %pad_maximum_fusion.4), calls=%async_computation.12 | async-start | bytes 6291456 | tf_op jit(solution)/shard_map/all_to_all | solution.py:233
  641.7 91.5 %reduce-scatter.5.cloned.1.call-start = ((), (), s32[]{:S(2)}) async-start(), calls=%async_computation.19 | async-start | bytes 3932160 | tf_op jit(solution)/shard_map/reduce_scatter | solution.py:24
  713.0 78.2 %all-to-all-start.11 = ((bf16[64,4,16,384]{3,2,1,0:T(8,128)(2,1)}), bf16[64,4,16,384]{3,2,1,0:T(8,128)(2,1)S(1)}, u32[]{:S(2)}, u32[]{:S(2)}) async-start(bf16[64,4,16,384]{3,2,1,0:T(8,128)(2,1)} %pad_maximum_fusion.5), calls=%async_computation.13 | async-start | bytes 6291456 | tf_op jit(solution)/shard_map/all_to_all | solution.py:234
  719.8 78.2 %reduce-scatter.3.cloned.1.call-start = ((), (), s32[]{:S(2)}) async-start(), calls=%async_computation.16 | async-start | bytes 3932160 | tf_op jit(solution)/shard_map/reduce_scatter | solution.py:24
  791.2 21.0 %all-to-all-start.6 = ((bf16[64,3,2,512]{3,2,1,0:T(2,128)(2,1)}), bf16[64,3,2,512]{3,2,1,0:T(2,128)(2,1)S(1)}, u32[]{:S(2)}, u32[]{:S(2)}) async-start(bf16[64,3,2,512]{3,2,1,0:T(2,128)(2,1)} %copy.236), calls=%async_computation.8 | async-start | bytes 786432 | tf_op jit(solution)/shard_map/all_to_all | solution.py:195
  797.9 38.8 %copy-start.44 = (s32[64,4]{0,1:T(4,128)S(1)}, s32[64,4]{0,1:T(4,128)}, u32[]{:S(2)}) copy-start(s32[64,4]{0,1:T(4,128)} %get-tuple-element.37) | copy-start | bytes 3076
  812.2 19.0 %all-to-all-start.3 = ((bf16[64,3,2,512]{3,2,1,0:T(2,128)(2,1)}), bf16[64,3,2,512]{3,2,1,0:T(2,128)(2,1)}, u32[]{:S(2)}, u32[]{:S(2)}) async-start(bf16[64,3,2,512]{3,2,1,0:T(2,128)(2,1)} %copy.217), calls=%async_computation.4 | async-start | bytes 786432 | tf_op jit(solution)/shard_map/all_to_all | solution.py:195
  831.3 18.6 %all-to-all-start.8 = ((bf16[64,3,2,512]{3,2,1,0:T(2,128)(2,1)}), bf16[64,3,2,512]{3,2,1,0:T(2,128)(2,1)}, u32[]{:S(2)}, u32[]{:S(2)}) async-start(bf16[64,3,2,512]{3,2,1,0:T(2,128)(2,1)} %copy.238), calls=%async_computation.10 | async-start | bytes 786432 | tf_op jit(solution)/shard_map/all_to_all | solution.py:198
  849.9 24.0 %all-to-all-start.7 = ((bf16[64,3,2,512]{3,2,1,0:T(2,128)(2,1)}), bf16[64,3,2,512]{3,2,1,0:T(2,128)(2,1)}, u32[]{:S(2)}, u32[]{:S(2)}) async-start(bf16[64,3,2,512]{3,2,1,0:T(2,128)(2,1)} %copy.237), calls=%async_computation.9 | async-start | bytes 786432 | tf_op jit(solution)/shard_map/all_to_all | solution.py:198
  (41 other events, 285.0 us)
Sparse Core Ops, SparseCore 0:
  187.3 45.1 all-gather.8
  234.9 76.2 all-gather.4
  313.0 58.6 all-gather.10
  373.4 40.3 all-gather.6
  650.0 62.8 reduce-scatter.4
  733.3 60.6 reduce-scatter.2
where the time goes:
time: 896 us; the launch traced here: 884 us
  waiting for transfers between devices  286 us (32%)
  local copies, waits for them, and re-layouts  272 us (30%)
  other arithmetic  122 us (14%)
  starting transfers between devices  101 us (11%)
  matrix products  86.7 us (10%)
  between operations  15.3 us (2%)
    all_gather x2, waiting for transfers between devices, shards(): lax.all_gather(rows_part, 'dp', axis=3, tiled=True)  111 us
    reduce_sum x2, other arithmetic, route_slots(): jnp.sum(matches[:, :, :, None] * target_table[None, None, :, :], axis=2)  70.9 us
    all_to_all x1, waiting for transfers between devices, sent_together(): lax.all_to_all(both, axis, split_axis=split_dim, concat_axis=concat_dim,...  66.4 us
    all_to_all x1, waiting for transfers between devices, shards(): lax.all_to_all(send_down, 'expert', split_axis=0, concat_axis=0, tiled=True)  53.2 us
    reshape x6, local copies, waits for them, and re-layouts, expert_work(): member.reshape(stored_shape)  50.5 us
    reshape x6, local copies, waits for them, and re-layouts, split_pairs(): return weights.reshape(weights.shape[:3] + (2, weights.shape[3] // 2))  46.8 us
    all_to_all x2, starting transfers between devices, shards(): lax.all_to_all(grads_out.reshape(shape_part), 'expert', split_axis=0, con...  22.8 us
    all_to_all x2, waiting for transfers between devices, shards(): lax.all_to_all(output_sum.astype(jnp.bfloat16), 'expert', split_axis=0, c...  20.8 us
  transfers between devices with their start and end apart: 18, of which 12 were waited for; matrix products, arithmetic and copies ran while one was open for 44% of the time, Pallas kernels for 0%

commit v1 on v0

v1 whole, which is shorter than its diff:
```python
import functools

import jax
import jax.numpy as jnp
from jax import lax
from jax.experimental import pallas as pl
from jax.experimental.pallas import tpu as pltpu
from jax.sharding import Mesh
from jax.sharding import PartitionSpec as P

INTERPRET = False
EXPERT = ("xl", "y", "z")
DP = ("xh", "c")
HOMES = ("xl", "y", "z", "c")
SLOTS = 4
VMEM = pl.BlockSpec(memory_space=pltpu.VMEM)
SMEM = pl.BlockSpec(memory_space=pltpu.SMEM)


def call(kernel, name, in_specs, out_shape, scratch=()):
    return pl.pallas_call(
        kernel,
        name=name,
        in_specs=in_specs,
        out_specs=jax.tree.map(lambda _: VMEM, out_shape),
        out_shape=out_shape,
        scratch_shapes=scratch,
        interpret=INTERPRET,
        compiler_params=pltpu.CompilerParams(vmem_limit_bytes=56 << 20),
    )


def dot(a, b, a_dim, b_dim):
    return lax.dot_general(
        a, b, (((a_dim,), (b_dim,)), ((), ())), preferred_element_type=jnp.float32
    )


def dispatch_kernel(offsets, pick_ref, high_ref, low_ref, own_ref, other_ref, *out_refs):
    micro = pick_ref.shape[0]
    feats = own_ref.shape[-1]
    rows = pick_ref.shape[1] // offsets

    def step(n, carry):
        m, rx = n // 2, n % 2
        at = pl.ds(pl.multiple_of(m * rows, rows), rows)
        for rc, source in enumerate((own_ref, other_ref)):
            x = source[:, rx, 0, m].reshape(-1, feats)
            g = source[:, rx, 1, m].reshape(-1, feats)
            picked = dot(pick_ref[m], x, 1, 0).astype(jnp.bfloat16)
            scaled = dot(high_ref[m], g, 1, 0) + dot(low_ref[m], g, 1, 0)
            scaled = scaled.astype(jnp.bfloat16)
            for o in range(offsets):
                out_refs[o][2 * rc + rx, 0, at] = picked[o * rows : (o + 1) * rows]
                out_refs[o][2 * rc + rx, 1, at] = scaled[o * rows : (o + 1) * rows]
        return carry

    lax.fori_loop(0, 2 * micro, step, 0)


def combine_kernel(offsets, pick_ref, high_ref, low_ref, *refs):
    row_refs, (keep_ref, send_ref) = refs[:offsets], refs[offsets:]
    micro = pick_ref.shape[0]
    rows = pick_ref.shape[1] // offsets
    line, tokens, feats = keep_ref.shape[0], keep_ref.shape[4], keep_ref.shape[5]

    def step(n, carry):
        m, rx = n // 2, n % 2
        at = pl.ds(pl.multiple_of(m * rows, rows), rows)
        for rc, target in enumerate((keep_ref, send_ref)):
            out = jnp.concatenate([r[2 * rc + rx, 0, at] for r in row_refs], axis=0)
            back = jnp.concatenate([r[2 * rc + rx, 1, at] for r in row_refs], axis=0)
            value = dot(high_ref[m], out, 0, 0) + dot(low_ref[m], out, 0, 0)
            grad = dot(pick_ref[m], back, 0, 0)
            shape = (line, tokens, feats)
            target[:, rx, 0, m] = value.reshape(shape).astype(target.dtype)
            target[:, rx, 1, m] = grad.reshape(shape).astype(target.dtype)
        return carry

    lax.fori_loop(0, 2 * micro, step, 0)


def expert_kernel(offsets, quarter_ref, weight_ref, *refs):
    row_refs, refs = refs[:offsets], refs[offsets:]
    grad_ref, refs = refs[0], refs[1:]
    out_refs, refs = refs[:offsets], refs[offsets:]
    w_scr, pre_scr, act_scr = refs
    _, blocks, _, _, pairs, width = weight_ref.shape
    half = width // 2
    depth = blocks * pairs
    rows = row_refs[0].shape[2]

    def swap(lower, upper):
        lane = lax.broadcasted_iota(jnp.int32, lower.shape, 1)
        first = jnp.where(lane < half, lower, pltpu.roll(upper, half, 1))
        second = jnp.where(lane < half, pltpu.roll(lower, half, 1), upper)
        return first, second

    def gather_rows(blk, which):
        return jnp.concatenate([r[blk, which] for r in row_refs], axis=0)

    pre_scr[...] = jnp.zeros_like(pre_scr)

    def first(blk, carry):
        q = quarter_ref[blk]
        x = gather_rows(blk, 0)
        g = gather_rows(blk, 1)
        for k in range(3):
            lower = weight_ref[q, :, 0, k].reshape(depth, width)
            upper = weight_ref[q, :, 1, k].reshape(depth, width)
            even, odd = swap(lower, upper)
            w_scr[k, blk, :depth] = even
            w_scr[k, blk, depth:] = odd
            pre_scr[k] += dot(g if k == 2 else x, w_scr[k, blk], 1, 0)
        return carry

    lax.fori_loop(0, 4, first, 0)
    gate, up, hidden_grad = pre_scr[0], pre_scr[1], pre_scr[2]
    logistic = jax.nn.sigmoid(gate)
    swished = gate * logistic
    act_scr[2] = (swished * up).astype(jnp.bfloat16)
    act_scr[0] = (hidden_grad * up * logistic * (1.0 + gate * (1.0 - logistic))).astype(
        jnp.bfloat16
    )
    act_scr[1] = (hidden_grad * swished).astype(jnp.bfloat16)

    def second(blk, carry):
        q = quarter_ref[blk]
        x = gather_rows(blk, 0)
        g = gather_rows(blk, 1)
        for k in range(3):
            total = dot(g if k == 2 else x, act_scr[k], 0, 0).astype(jnp.bfloat16)
            lower, upper = swap(total[:depth], total[depth:])
            grad_ref[q, :, 0, k] = lower.reshape(blocks, pairs, width)
            grad_ref[q, :, 1, k] = upper.reshape(blocks, pairs, width)
        out = dot(act_scr[2], w_scr[2, blk], 1, 1).astype(jnp.bfloat16)
        back = dot(act_scr[0], w_scr[0, blk], 1, 1) + dot(act_scr[1], w_scr[1, blk], 1, 1)
        back = back.astype(jnp.bfloat16)
        for o in range(offsets):
            out_refs[o][blk, 0] = out[o * rows : (o + 1) * rows]
            out_refs[o][blk, 1] = back[o * rows : (o + 1) * rows]
        return carry

    lax.fori_loop(0, 4, second, 0)


def routing(route_ids, route_gates, expert_ids, replica_plan, capacity):
    line, micro, tokens, _ = route_ids.shape
    offsets = expert_ids.shape[0]
    match = route_ids[:, :, None] == expert_ids[None, None, :, None, None]
    named = jnp.sum(match.astype(jnp.float32), axis=4).transpose(1, 2, 0, 3)
    gates = jnp.sum(jnp.where(match, route_gates[:, :, None], 0.0), axis=4).transpose(1, 2, 0, 3)
    copies = 1 + jnp.sum(
        (replica_plan[:, None, :] == expert_ids[None, :, None]).astype(jnp.int32), axis=2
    )
    all_ids = jnp.arange(capacity.shape[1], dtype=jnp.int32)
    limit = jnp.sum(
        jnp.where(all_ids[None, None, :] == expert_ids[None, :, None], capacity[:, None, :], 0),
        axis=2,
    )
    token_ids = jnp.arange(tokens, dtype=jnp.int32)
    apart = token_ids[None, :] - token_ids[:, None]
    earlier = apart > 0
    rivals = earlier & (apart % copies[:, :, None, None] == 0)
    place = jnp.sum(named[..., None] * rivals[:, :, None].astype(jnp.float32), axis=3)
    count = jnp.sum(named[..., None] * earlier.astype(jnp.float32), axis=3)
    kept = (named > 0) & (place < limit[:, :, None, None].astype(jnp.float32))
    code = jnp.where(kept, count.astype(jnp.int32), -1)
    line_ids = jnp.arange(line, dtype=jnp.int32)
    slot_ids = jnp.arange(SLOTS, dtype=jnp.int32)
    same = line_ids[:, None, None, None] == line_ids[None, None, :, None]
    chosen = (code[:, :, None, None] == slot_ids[None, :, None, None]) & same
    high = lax.reduce_precision(gates, 8, 7)
    low = gates - high
    shape = (micro, offsets * line * SLOTS, line * tokens)

    def spread(values):
        return jnp.where(chosen, values, 0.0).astype(jnp.bfloat16).reshape(shape)

    return spread(1.0), spread(high[:, :, None, None]), spread(low[:, :, None, None])


def shards(
    sizes,
    tokens_in,
    route_ids,
    route_gates,
    cotangent,
    gate_proj,
    up_proj,
    down_proj,
    replica_plan,
    capacity,
):
    nxl, ny, nz = sizes
    micro, tokens, feats = tokens_in.shape
    expert_count, pairs, width = gate_proj.shape
    xh, core = lax.axis_index("xh"), lax.axis_index("c")
    xl, y, z = (lax.axis_index(name) for name in EXPERT)
    steps = [(dx, dy) for dx in range(nxl) for dy in range(ny)]
    offsets = len(steps)
    swap = [(0, 1), (1, 0)]

    weights = jnp.stack([gate_proj, up_proj, down_proj], axis=1)
    weights = lax.all_to_all(weights, HOMES, split_axis=0, concat_axis=0, tiled=True)

    meta = jnp.stack([route_ids.astype(jnp.float32), route_gates])
    meta = lax.all_gather(meta, "z", axis=0)
    lane = jnp.arange(feats, dtype=jnp.int32)
    source = 2 * (lane % (feats // 2)) + lane // (feats // 2)
    halves = (lane[:, None] == source[None, :]).astype(jnp.bfloat16)
    own = jnp.stack([tokens_in, cotangent]).reshape(-1, feats)
    own = jnp.dot(own, halves, preferred_element_type=jnp.float32).astype(jnp.bfloat16)
    across = lax.ppermute(own, "xh", swap)
    line = lax.all_gather(jnp.concatenate([own, across]), "z", axis=0, tiled=True)
    line_shape = (nz, 2, 2, micro, tokens, feats)
    line_other = lax.ppermute(line, "c", swap).reshape(line_shape)
    line = line.reshape(line_shape)

    expert_ids = jnp.stack(
        [((((xl + dx) % nxl) * ny + (y + dy) % ny) * nz + z) * 2 + core for dx, dy in steps]
    )
    selections = routing(
        meta[:, 0].astype(jnp.int32), meta[:, 1], expert_ids, replica_plan, capacity
    )
    chunk_rows = micro * nz * SLOTS
    chunk = jax.ShapeDtypeStruct((4, 2, chunk_rows, feats), jnp.bfloat16)
    sent = call(
        functools.partial(dispatch_kernel, offsets), "dispatch", [VMEM] * 5, (chunk,) * offsets
    )(*selections, line, line_other)

    def moved(pieces, sign):
        done = [pieces[0]]
        for (dx, dy), piece in list(zip(steps, pieces))[1:]:
            pairs_list = [
                (a * ny + b, ((a + sign * dx) % nxl) * ny + (b + sign * dy) % ny)
                for a in range(nxl)
                for b in range(ny)
            ]
            done.append(lax.ppermute(piece, ("xl", "y"), pairs_list))
        return done

    arrived = moved(sent, 1)
    blk = jnp.arange(4, dtype=jnp.int32)
    quarters = (xh ^ (blk % 2)) * 2 + (core ^ (blk // 2))
    rows_all = offsets * chunk_rows
    view = (4, expert_count // 8, 2, 3, pairs, width)
    results = call(
        functools.partial(expert_kernel, offsets),
        "expert",
        [SMEM] + [VMEM] * (1 + offsets),
        (jax.ShapeDtypeStruct(view, jnp.bfloat16),) + (chunk,) * offsets,
        scratch=(
            pltpu.VMEM((3, 4, feats, width), jnp.bfloat16),
            pltpu.VMEM((3, rows_all, width), jnp.float32),
            pltpu.VMEM((3, rows_all, width), jnp.bfloat16),
        ),
    )(quarters, weights.reshape(view), *arrived)
    grads = results[0].reshape(expert_count, 3, pairs, width)
    grads = lax.all_to_all(grads, HOMES, split_axis=0, concat_axis=0, tiled=True)

    returned = moved(results[1:], -1)
    keep, send = call(
        functools.partial(combine_kernel, offsets),
        "combine",
        [VMEM] * (3 + offsets),
        (
            jax.ShapeDtypeStruct(line_shape, jnp.float32),
            jax.ShapeDtypeStruct(line_shape, jnp.bfloat16),
        ),
    )(*selections, *returned)
    keep = (keep + lax.ppermute(send, "c", swap).astype(jnp.float32)).astype(jnp.bfloat16)
    keep = lax.psum_scatter(keep.reshape(-1, feats), "z", scatter_dimension=0, tiled=True)
    keep = keep.reshape(2, -1, feats)
    total = keep[0].astype(jnp.float32) + lax.ppermute(keep[1], "xh", swap).astype(jnp.float32)
    total = jnp.dot(total.astype(jnp.bfloat16), halves.T, preferred_element_type=jnp.float32)
    total = total.astype(jnp.bfloat16).reshape(2, micro, tokens, feats)
    return (total[0], total[1], grads[:, 0], grads[:, 1], grads[:, 2])


def build(devices, sizes):
    mesh = Mesh(devices.reshape((2, 2) + sizes), DP + EXPERT)
    weight = P(None, EXPERT, DP)
    in_specs = (weight, P(None, EXPERT), P(None, EXPERT), weight, weight, weight, weight, P(), P())
    return jax.shard_map(
        functools.partial(shards, sizes),
        mesh=mesh,
        in_specs=in_specs,
        out_specs=(weight,) * 5,
        check_vma=False,
    )


def solution(mesh):
    return build(mesh.devices, (2, 4, 8))
```

time: 896 us -> 482 us (0.54); the launches traced: 884 us -> 481 us
  local copies, waits for them, and re-layouts: 272 us -> 15.9 us
  waiting for transfers between devices: 286 us -> 155 us
  blocking collectives: 0 us -> 123 us
  other arithmetic: 122 us -> 19.1 us
  matrix products: 86.7 us -> 1.59 us
  Pallas kernels: 0 us -> 33.2 us
  starting transfers between devices: 101 us -> 118 us
    all_to_all x12 -> x2, waiting for transfers between devices: 175 us -> 0.01 us  [the longest x1 0.01 us: shards(): lax.all_to_all(weights, HOMES, split_axis=0, concat_axis=0, tiled=True)]
    all_gather x0 -> x1, blocking collectives: none -> 123 us  [shards(): meta = lax.all_gather(meta, 'z', axis=0)]
    reshape x25 -> x0, local copies, waits for them, and re-layouts: 123 us -> none  [the longest x6 50.5 us: expert_work(): member.reshape(stored_shape)]
    ppermute x0 -> x18, waiting for transfers between devices: none -> 113 us  [the longest x14 87.3 us: moved(): done.append(lax.ppermute(piece, ('xl', 'y'), pairs_list))]
    all_gather x4 -> x1, waiting for transfers between devices: 111 us -> 0.02 us  [shards(): lax.all_gather(jnp.concatenate([own, across]), 'z', axis=0, tiled=True)]
    ppermute x0 -> x18, starting transfers between devices: none -> 90 us  [the longest x14 86.7 us: moved(): done.append(lax.ppermute(piece, ('xl', 'y'), pairs_list))]
    dot_general x29 -> x2, matrix products: 86.7 us -> 1.59 us  [the longest x1 1.25 us: shards(): jnp.dot(total.astype(jnp.bfloat16), halves.T, preferred_element_type=jnp....]
    reduce_sum x12 -> x4, other arithmetic: 75.7 us -> 1.87 us  [the longest x1 1.15 us: routing(): jnp.sum(named[..., None] * rivals[:, :, None].astype(jnp.float32), axis=3)]
  transfers between devices with their start and end apart: 18 -> 22, of which waited for: 12 -> 9; matrix products, arithmetic and copies ran while one was open for 44% -> 5% of each run, Pallas kernels for 0% -> 3%
where the time goes in v1:
time: 482 us; the launch traced here: 481 us
  waiting for transfers between devices  155 us (32%)
  blocking collectives  123 us (26%)
  starting transfers between devices  118 us (24%)
  Pallas kernels  33.2 us (7%)
  other arithmetic  19.1 us (4%)
  local copies, waits for them, and re-layouts  15.9 us (3%)
  between operations  14.6 us (3%)
    all_gather x1, blocking collectives, shards(): meta = lax.all_gather(meta, 'z', axis=0)  123 us
    ppermute x14, waiting for transfers between devices, moved(): done.append(lax.ppermute(piece, ('xl', 'y'), pairs_list))  87.3 us
    ppermute x14, starting transfers between devices, moved(): done.append(lax.ppermute(piece, ('xl', 'y'), pairs_list))  86.7 us
    reduce_scatter x1, waiting for transfers between devices, shards(): lax.psum_scatter(keep.reshape(-1, feats), 'z', scatter_dimension=0, tiled...  42.3 us
    pallas_call x1, Pallas kernels, shards(): call(functools.partial(expert_kernel, offsets), 'expert', [SMEM] + [VMEM]...  19.3 us
    ppermute x1, waiting for transfers between devices, shards(): across = lax.ppermute(own, 'xh', swap)  16.3 us
    all_to_all x1, starting transfers between devices, shards(): lax.all_to_all(weights, HOMES, split_axis=0, concat_axis=0, tiled=True)  14.8 us
    all_to_all x1, starting transfers between devices, shards(): lax.all_to_all(grads, HOMES, split_axis=0, concat_axis=0, tiled=True)  13.5 us
  transfers between devices with their start and end apart: 22, of which 9 were waited for; matrix products, arithmetic and copies ran while one was open for 5% of the time, Pallas kernels for 3%

profile of v1, /device:TPU:6, one launch (start us, length us, event | category | flops | bytes accessed | tf_op | source)
XLA Modules:
  0.0 481.3 jit_solution(7036538946815955797)
XLA Ops:
  7.2 5.1 %pad_maximum_fusion = bf16[128,3,16,384]{3,2,1,0:T(8,128)(2,1)} fusion(bf16[128,1,16,384]{3,2,1,0:T(8,128)(2,1)} %bitcast.55, bf16[128,1,16,384]{3,2,1,0:T(8,128)(2,1)} %bitcast.56, bf16[128,1,16,384]{3,2,1,0:T(8,128)(2,1)} %bitcast.57), kind=kLoop, calls=%fused_computation | loop fusion | flops 4718592 | bytes 9437184 | tf_op jit(solution)/shard_map/stack | solution.py:204
  12.3 14.8 %all-to-all-start = ((bf16[128,3,16,384]{3,2,1,0:T(8,128)(2,1)}), bf16[128,3,16,384]{3,2,1,0:T(8,128)(2,1)}, u32[]{:S(2)}, u32[]{:S(2)}) async-start(bf16[128,3,16,384]{3,2,1,0:T(8,128)(2,1)} %pad_maximum_fusion), calls=%async_computation | async-start | bytes 9437184 | tf_op jit(solution)/shard_map/all_to_all | solution.py:205
  29.0 16.3 %collective-permute-done = bf16[128,512]{1,0:T(8,128)(2,1)S(1)} collective-permute-done((bf16[128,512]{1,0:T(8,128)(2,1)S(1)}, bf16[128,512]{1,0:T(8,128)(2,1)S(1)}, u32[]{:S(2)}, u32[]{:S(2)}) %collective-permute-start) | collective-permute-done | bytes 131104 | tf_op jit(solution)/shard_map/ppermute | solution.py:214
  46.5 123.2 %all-gather = f32[16,2,32,8]{2,3,1,0:T(8,128)S(1)} all-gather(f32[2,2,32,8]{2,3,1,0:T(8,128)S(1)} %pad_maximum_fusion.3), channel_id=2, replica_groups=mesh['xh'=2,'c'=2,'xl'=2,'y'=4,'z'=8] {'z'}, dimensions={0}, use_global_device_ids=true | all-gather | bytes 36864 | tf_op jit(solution)/shard_map/all_gather | solution.py:208
  186.9 6.7 %dispatch.1 = (bf16[4,2,64,512]{3,2,1,0:T(8,128)(2,1)}, bf16[4,2,64,512]{3,2,1,0:T(8,128)(2,1)}, bf16[4,2,64,512]{3,2,1,0:T(8,128)(2,1)}, bf16[4,2,64,512]{3,2,1...) custom-call(bf16[2,256,256]{2,1,0:T(8,128)(2,1)} %select_convert_fus, ...), custom_call_target="tpu_custom_call" | custom-call | tf_op jit(solution)/shard_map/dispatch/pallas_call | solution.py:228
  195.2 2.9 collective-permute-start.3
  201.6 7.8 %collective-permute-done.2.refs_1_ = bf16[4,2,64,512]{3,2,1,0:T(8,128)(2,1)S(1)} collective-permute-done((bf16[4,2,64,512]{3,2,1,0:T(8,128)(2,1)}, bf16[4,2,64,512]{3,2,1,0:T(8,128)(2,1)S(1)}, u32[]{:S(2)}, u32[]{:S(2)}) %collective-permute-start.2) | collective-permute-done | bytes 524320 | tf_op jit(solution)/shard_map/ppermute | solution.py:240
  209.4 29.6 %collective-permute-start.7 = (bf16[4,2,64,512]{3,2,1,0:T(8,128)(2,1)}, bf16[4,2,64,512]{3,2,1,0:T(8,128)(2,1)S(1)}, u32[]{:S(2)}, u32[]{:S(2)}) collective-permute-start(bf16[4,2,64,512]{3,2,1,0:T(8,128)(2,1)} %get-tuple-element.30), channel_id=1, source_target_pairs={{0,48},{8,56},{16,32},{24,40},{32,16},{40,24},{48,0},{56,8},{1,49}... | collective-permute-start | bytes 1572872 | tf_op jit(solution)/shard_map/ppermute | solution.py:240
  239.6 11.2 %collective-permute-done.7.refs_6_ = bf16[4,2,64,512]{3,2,1,0:T(8,128)(2,1)S(1)} collective-permute-done((bf16[4,2,64,512]{3,2,1,0:T(8,128)(2,1)}, bf16[4,2,64,512]{3,2,1,0:T(8,128)(2,1)S(1)}, u32[]{:S(2)}, u32[]{:S(2)}) %collective-permute-start.7) | collective-permute-done | bytes 524320 | tf_op jit(solution)/shard_map/ppermute | solution.py:240
  250.8 5.1 %collective-permute-done.8.refs_7_ = bf16[4,2,64,512]{3,2,1,0:T(8,128)(2,1)} collective-permute-done((bf16[4,2,64,512]{3,2,1,0:T(8,128)(2,1)}, bf16[4,2,64,512]{3,2,1,0:T(8,128)(2,1)}, u32[]{:S(2)}, u32[]{:S(2)}) %collective-permute-start.8) | collective-permute-done | bytes 524320 | tf_op jit(solution)/shard_map/ppermute | solution.py:240
  255.9 19.3 %expert.1 = (bf16[4,16,2,3,16,384]{5,4,3,2,1,0:T(8,128)(2,1)}, bf16[4,2,64,512]{3,2,1,0:T(8,128)(2,1)}, bf16[4,2,64,512]{3,2,1,0:T(8,128)(2,1)}, bf16[4,2,64,512...) custom-call(s32[4]{0:T(128)} %fusion.25.quarter_ref, ...), custom_call_target="tpu_custom_call" | custom-call | tf_op jit(solution)/shard_map/expert/pallas_call | solution.py:248
  275.3 13.5 %all-to-all-start.1 = ((bf16[128,3,16,384]{3,2,1,0:T(8,128)(2,1)}), bf16[128,3,16,384]{3,2,1,0:T(8,128)(2,1)}, u32[]{:S(2)}, u32[]{:S(2)}) async-start(bf16[128,3,16,384]{3,2,1,0:T(8,128)(2,1)} %bitcast.52), calls=%async_computation.2 | async-start | bytes 9437184 | tf_op jit(solution)/shard_map/all_to_all | solution.py:260
  288.8 3.1 collective-permute-start.9
  293.6 3.6 collective-permute-start.13
  297.2 45.4 %collective-permute-done.9.refs_1_ = bf16[4,2,64,512]{3,2,1,0:T(8,128)(2,1)S(1)} collective-permute-done((bf16[4,2,64,512]{3,2,1,0:T(8,128)(2,1)}, bf16[4,2,64,512]{3,2,1,0:T(8,128)(2,1)S(1)}, u32[]{:S(2)}, u32[]{:S(2)}) %collective-permute-start.9) | collective-permute-done | bytes 524320 | tf_op jit(solution)/shard_map/ppermute | solution.py:240
  342.6 3.3 collective-permute-start.14
  345.9 37.5 %collective-permute-start.15 = (bf16[4,2,64,512]{3,2,1,0:T(8,128)(2,1)S(1)}, bf16[4,2,64,512]{3,2,1,0:T(8,128)(2,1)S(1)}, u32[]{:S(2)}, u32[]{:S(2)}) collective-permute-start(bf16[4,2,64,512]{3,2,1,0:T(8,128)(2,1)S(1)} %copy-done.20), channel_id=1, source_target_pairs={{0,40},{8,48},{16,56},{24,32},{32,8},{40,16},{48,24},{56,0},{1,41}... | collective-permute-start | bytes 1572872 | tf_op jit(solution)/shard_map/ppermute | solution.py:240
  383.4 17.8 %collective-permute-done.15.refs_7_ = bf16[4,2,64,512]{3,2,1,0:T(8,128)(2,1)S(1)} collective-permute-done((bf16[4,2,64,512]{3,2,1,0:T(8,128)(2,1)S(1)}, bf16[4,2,64,512]{3,2,1,0:T(8,128)(2,1)S(1)}, u32[]{:S(2)}, u32[]{:S(2)}) %collective-permute-start.15) | collective-permute-done | bytes 524320 | tf_op jit(solution)/shard_map/ppermute | solution.py:240
  402.1 7.2 %combine.1 = (f32[8,2,2,2,32,512]{5,4,3,2,1,0:T(8,128)}, bf16[8,2,2,2,32,512]{5,4,3,2,1,0:T(8,128)(2,1)}) custom-call(bf16[2,256,256]{2,1,0:T(8,128)(2,1)} %select_convert_fusion.2.pick_ref, bf16[2,256,256]{2,1,0:T(8,128)(2,1)} %get-tuple-element.51.high_ref, bf16[2,256,256]{2,1,0:T(8,128)(2,1)} %get-tuple-element.50.low_ref, ...), custom_call_target="tpu_custom_call" | custom-call | tf_op jit(solution)/shard_map/combine/pallas_call | solution.py:263
  409.3 4.4 collective-permute-done.16
  413.6 4.4 add_convert_fusion
  418.1 42.3 %reduce-scatter.2.cloned.1.call-done = bf16[256,512]{1,0:T(8,128)(2,1)} async-done(((bf16[2048,512]{1,0:T(8,128)(2,1)}), bf16[256,512]{1,0:T(8,128)(2,1)}) %reduce-scatter.2.cloned.1.call-update) | async-done | bytes 262160 | tf_op jit(solution)/shard_map/reduce_scatter | solution.py:273
  462.8 5.0 %collective-permute-done.17 = bf16[128,512]{1,0:T(8,128)(2,1)S(1)} collective-permute-done((bf16[128,512]{1,0:T(8,128)(2,1)S(1)}, bf16[128,512]{1,0:T(8,128)(2,1)S(1)}, u32[]{:S(2)}, u32[]{:S(2)}) %collective-permute-start.17) | collective-permute-done | bytes 131104 | tf_op jit(solution)/shard_map/ppermute | solution.py:275
  469.8 4.7 slice_bitcast_fusion
  (123 shorter events, 32.6 us)
Async XLA Ops:
  12.3 243.6 %all-to-all-start = ((bf16[128,3,16,384]{3,2,1,0:T(8,128)(2,1)}), bf16[128,3,16,384]{3,2,1,0:T(8,128)(2,1)}, u32[]{:S(2)}, u32[]{:S(2)}) async-start(bf16[128,3,16,384]{3,2,1,0:T(8,128)(2,1)} %pad_maximum_fusion), calls=%async_computation | async-start | bytes 9437184 | tf_op jit(solution)/shard_map/all_to_all | solution.py:205
  27.1 144.7 %copy-start.19 = (s32[2,64]{1,0:T(2,128)S(1)}, s32[2,64]{1,0:T(2,128)}, u32[]{:S(2)}) copy-start(s32[2,64]{1,0:T(2,128)} %param.16) | copy-start | bytes 1540
  27.1 144.4 %all-gather.3.cloned.1.call-start = ((), (), s32[]{:S(2)}) async-start(), calls=%async_computation.3 | async-start | bytes 2359296 | tf_op jit(solution)/shard_map/all_gather | solution.py:215
  27.5 17.8 %collective-permute-start = (bf16[128,512]{1,0:T(8,128)(2,1)S(1)}, bf16[128,512]{1,0:T(8,128)(2,1)S(1)}, u32[]{:S(2)}, u32[]{:S(2)}) collective-permute-start(bf16[128,512]{1,0:T(8,128)(2,1)S(1)} %convolution_convert_fusion.1), channel_id=1, source_target_pairs={{0,128},{128,0},{1,129},{129,1},{2,130},{130,2},{3,131},{131,3},{4... | collective-permute-start | bytes 393224 | tf_op jit(solution)/shard_map/ppermute | solution.py:214
  171.5 14.1 %collective-permute-start.1 = (bf16[2048,512]{1,0:T(8,128)(2,1)}, bf16[2048,512]{1,0:T(8,128)(2,1)S(1)}, u32[]{:S(2)}, u32[]{:S(2)}) collective-permute-start(bf16[2048,512]{1,0:T(8,128)(2,1)} %all-gather.3.cloned.1.call-done), channel_id=1, source_target_pairs={{0,64},{64,0},{1,65},{65,1},{2,66},{66,2},{3,67},{67,3},{4,68},{68... | collective-permute-start | bytes 6291464 | tf_op jit(solution)/shard_map/ppermute | solution.py:217
  193.6 15.8 %collective-permute-start.2 = (bf16[4,2,64,512]{3,2,1,0:T(8,128)(2,1)}, bf16[4,2,64,512]{3,2,1,0:T(8,128)(2,1)S(1)}, u32[]{:S(2)}, u32[]{:S(2)}) collective-permute-start(bf16[4,2,64,512]{3,2,1,0:T(8,128)(2,1)} %get-tuple-element.25), channel_id=1, source_target_pairs={{0,8},{8,16},{16,24},{24,0},{32,40},{40,48},{48,56},{56,32},{1,9},... | collective-permute-start | bytes 1572872 | tf_op jit(solution)/shard_map/ppermute | solution.py:240
  195.2 43.8 %collective-permute-start.3 = (bf16[4,2,64,512]{3,2,1,0:T(8,128)(2,1)}, bf16[4,2,64,512]{3,2,1,0:T(8,128)(2,1)S(1)}, u32[]{:S(2)}, u32[]{:S(2)}) collective-permute-start(bf16[4,2,64,512]{3,2,1,0:T(8,128)(2,1)} %get-tuple-element.26), channel_id=1, source_target_pairs={{0,16},{8,24},{16,0},{24,8},{32,48},{40,56},{48,32},{56,40},{1,17}... | collective-permute-start | bytes 1572872 | tf_op jit(solution)/shard_map/ppermute | solution.py:240
  198.1 41.5 %collective-permute-start.4 = (bf16[4,2,64,512]{3,2,1,0:T(8,128)(2,1)}, bf16[4,2,64,512]{3,2,1,0:T(8,128)(2,1)S(1)}, u32[]{:S(2)}, u32[]{:S(2)}) collective-permute-start(bf16[4,2,64,512]{3,2,1,0:T(8,128)(2,1)} %get-tuple-element.27), channel_id=1, source_target_pairs={{0,24},{8,0},{16,8},{24,16},{32,56},{40,32},{48,40},{56,48},{1,25}... | collective-permute-start | bytes 1572872 | tf_op jit(solution)/shard_map/ppermute | solution.py:240
  199.4 40.1 %collective-permute-start.5 = (bf16[4,2,64,512]{3,2,1,0:T(8,128)(2,1)}, bf16[4,2,64,512]{3,2,1,0:T(8,128)(2,1)S(1)}, u32[]{:S(2)}, u32[]{:S(2)}) collective-permute-start(bf16[4,2,64,512]{3,2,1,0:T(8,128)(2,1)} %get-tuple-element.28), channel_id=1, source_target_pairs={{0,32},{8,40},{16,48},{24,56},{32,0},{40,8},{48,16},{56,24},{1,33}... | collective-permute-start | bytes 1572872 | tf_op jit(solution)/shard_map/ppermute | solution.py:240
  199.6 40.0 %collective-permute-start.6 = (bf16[4,2,64,512]{3,2,1,0:T(8,128)(2,1)}, bf16[4,2,64,512]{3,2,1,0:T(8,128)(2,1)S(1)}, u32[]{:S(2)}, u32[]{:S(2)}) collective-permute-start(bf16[4,2,64,512]{3,2,1,0:T(8,128)(2,1)} %get-tuple-element.29), channel_id=1, source_target_pairs={{0,40},{8,48},{16,56},{24,32},{32,8},{40,16},{48,24},{56,0},{1,41}... | collective-permute-start | bytes 1572872 | tf_op jit(solution)/shard_map/ppermute | solution.py:240
  209.4 41.4 %collective-permute-start.7 = (bf16[4,2,64,512]{3,2,1,0:T(8,128)(2,1)}, bf16[4,2,64,512]{3,2,1,0:T(8,128)(2,1)S(1)}, u32[]{:S(2)}, u32[]{:S(2)}) collective-permute-start(bf16[4,2,64,512]{3,2,1,0:T(8,128)(2,1)} %get-tuple-element.30), channel_id=1, source_target_pairs={{0,48},{8,56},{16,32},{24,40},{32,16},{40,24},{48,0},{56,8},{1,49}... | collective-permute-start | bytes 1572872 | tf_op jit(solution)/shard_map/ppermute | solution.py:240
  239.0 16.9 %collective-permute-start.8 = (bf16[4,2,64,512]{3,2,1,0:T(8,128)(2,1)}, bf16[4,2,64,512]{3,2,1,0:T(8,128)(2,1)}, u32[]{:S(2)}, u32[]{:S(2)}) collective-permute-start(bf16[4,2,64,512]{3,2,1,0:T(8,128)(2,1)} %get-tuple-element.31), channel_id=1, source_target_pairs={{0,56},{8,32},{16,40},{24,48},{32,24},{40,0},{48,8},{56,16},{1,57}... | collective-permute-start | bytes 1572872 | tf_op jit(solution)/shard_map/ppermute | solution.py:240
  275.2 70.6 %copy-start.20 = (bf16[4,2,64,512]{3,2,1,0:T(8,128)(2,1)S(1)}, bf16[4,2,64,512]{3,2,1,0:T(8,128)(2,1)}, u32[]{:S(2)}) copy-start(bf16[4,2,64,512]{3,2,1,0:T(8,128)(2,1)} %get-tuple-element.39) | copy-start | bytes 1572868
  275.3 194.5 %all-to-all-start.1 = ((bf16[128,3,16,384]{3,2,1,0:T(8,128)(2,1)}), bf16[128,3,16,384]{3,2,1,0:T(8,128)(2,1)}, u32[]{:S(2)}, u32[]{:S(2)}) async-start(bf16[128,3,16,384]{3,2,1,0:T(8,128)(2,1)} %bitcast.52), calls=%async_computation.2 | async-start | bytes 9437184 | tf_op jit(solution)/shard_map/all_to_all | solution.py:260
  288.7 171.6 %reduce-scatter.2.cloned.1.call-start = ((), (), s32[]{:S(2)}) async-start(), calls=%async_computation.4 | async-start | bytes 2359296 | tf_op jit(solution)/shard_map/reduce_scatter | solution.py:273
  288.8 53.8 %collective-permute-start.9 = (bf16[4,2,64,512]{3,2,1,0:T(8,128)(2,1)}, bf16[4,2,64,512]{3,2,1,0:T(8,128)(2,1)S(1)}, u32[]{:S(2)}, u32[]{:S(2)}) collective-permute-start(bf16[4,2,64,512]{3,2,1,0:T(8,128)(2,1)} %get-tuple-element.33), channel_id=1, source_target_pairs={{0,24},{8,0},{16,8},{24,16},{32,56},{40,32},{48,40},{56,48},{1,25}... | collective-permute-start | bytes 1572872 | tf_op jit(solution)/shard_map/ppermute | solution.py:240
  291.9 54.0 %collective-permute-start.10 = (bf16[4,2,64,512]{3,2,1,0:T(8,128)(2,1)S(1)}, bf16[4,2,64,512]{3,2,1,0:T(8,128)(2,1)S(1)}, u32[]{:S(2)}, u32[]{:S(2)}) collective-permute-start(bf16[4,2,64,512]{3,2,1,0:T(8,128)(2,1)S(1)} %copy-done.25), channel_id=1, source_target_pairs={{0,16},{8,24},{16,0},{24,8},{32,48},{40,56},{48,32},{56,40},{1,17}... | collective-permute-start | bytes 1572872 | tf_op jit(solution)/shard_map/ppermute | solution.py:240
  292.5 90.9 %collective-permute-start.11 = (bf16[4,2,64,512]{3,2,1,0:T(8,128)(2,1)S(1)}, bf16[4,2,64,512]{3,2,1,0:T(8,128)(2,1)S(1)}, u32[]{:S(2)}, u32[]{:S(2)}) collective-permute-start(bf16[4,2,64,512]{3,2,1,0:T(8,128)(2,1)S(1)} %copy-done.24), channel_id=1, source_target_pairs={{0,8},{8,16},{16,24},{24,0},{32,40},{40,48},{48,56},{56,32},{1,9},... | collective-permute-start | bytes 1572872 | tf_op jit(solution)/shard_map/ppermute | solution.py:240
  293.5 89.9 %collective-permute-start.12 = (bf16[4,2,64,512]{3,2,1,0:T(8,128)(2,1)S(1)}, bf16[4,2,64,512]{3,2,1,0:T(8,128)(2,1)S(1)}, u32[]{:S(2)}, u32[]{:S(2)}) collective-permute-start(bf16[4,2,64,512]{3,2,1,0:T(8,128)(2,1)S(1)} %copy-done.23), channel_id=1, source_target_pairs={{0,32},{8,40},{16,48},{24,56},{32,0},{40,8},{48,16},{56,24},{1,33}... | collective-permute-start | bytes 1572872 | tf_op jit(solution)/shard_map/ppermute | solution.py:240
  293.6 89.8 %collective-permute-start.13 = (bf16[4,2,64,512]{3,2,1,0:T(8,128)(2,1)S(1)}, bf16[4,2,64,512]{3,2,1,0:T(8,128)(2,1)S(1)}, u32[]{:S(2)}, u32[]{:S(2)}) collective-permute-start(bf16[4,2,64,512]{3,2,1,0:T(8,128)(2,1)S(1)} %copy-done.22), channel_id=1, source_target_pairs={{0,56},{8,32},{16,40},{24,48},{32,24},{40,0},{48,8},{56,16},{1,57}... | collective-permute-start | bytes 1572872 | tf_op jit(solution)/shard_map/ppermute | solution.py:240
  342.6 40.8 %collective-permute-start.14 = (bf16[4,2,64,512]{3,2,1,0:T(8,128)(2,1)S(1)}, bf16[4,2,64,512]{3,2,1,0:T(8,128)(2,1)S(1)}, u32[]{:S(2)}, u32[]{:S(2)}) collective-permute-start(bf16[4,2,64,512]{3,2,1,0:T(8,128)(2,1)S(1)} %copy-done.21), channel_id=1, source_target_pairs={{0,48},{8,56},{16,32},{24,40},{32,16},{40,24},{48,0},{56,8},{1,49}... | collective-permute-start | bytes 1572872 | tf_op jit(solution)/shard_map/ppermute | solution.py:240
  345.9 55.4 %collective-permute-start.15 = (bf16[4,2,64,512]{3,2,1,0:T(8,128)(2,1)S(1)}, bf16[4,2,64,512]{3,2,1,0:T(8,128)(2,1)S(1)}, u32[]{:S(2)}, u32[]{:S(2)}) collective-permute-start(bf16[4,2,64,512]{3,2,1,0:T(8,128)(2,1)S(1)} %copy-done.20), channel_id=1, source_target_pairs={{0,40},{8,48},{16,56},{24,32},{32,8},{40,16},{48,24},{56,0},{1,41}... | collective-permute-start | bytes 1572872 | tf_op jit(solution)/shard_map/ppermute | solution.py:240
  409.2 4.4 collective-permute-start.16
  461.3 6.6 %collective-permute-start.17 = (bf16[128,512]{1,0:T(8,128)(2,1)S(1)}, bf16[128,512]{1,0:T(8,128)(2,1)S(1)}, u32[]{:S(2)}, u32[]{:S(2)}) collective-permute-start(bf16[128,512]{1,0:T(8,128)(2,1)S(1)} %slice.43), channel_id=1, source_target_pairs={{0,128},{128,0},{1,129},{129,1},{2,130},{130,2},{3,131},{131,3},{4... | collective-permute-start | bytes 393224 | tf_op jit(solution)/shard_map/ppermute | solution.py:275
  (24 other events, 575.4 us)
Sparse Core Ops, SparseCore 0:
  46.2 87.9 all-gather.2
  418.2 42.1 reduce-scatter.1

commit v2 on v1

v2 whole, which is shorter than its diff:
```python
import functools

import jax
import jax.numpy as jnp
from jax import lax
from jax.experimental import pallas as pl
from jax.experimental.pallas import tpu as pltpu
from jax.sharding import Mesh
from jax.sharding import PartitionSpec as P


INTERPRET = False
EXPERT = ("xl", "y", "z")
DP = ("xh", "c")
HOMES = ("xl", "y", "z", "c")
SLOTS = 4
VMEM = pl.BlockSpec(memory_space=pltpu.VMEM)
SMEM = pl.BlockSpec(memory_space=pltpu.SMEM)


def call(kernel, in_specs, out_shape, scratch=()):
    return pl.pallas_call(
        kernel,
        in_specs=in_specs,
        out_specs=jax.tree.map(lambda _: VMEM, out_shape),
        out_shape=out_shape,
        scratch_shapes=scratch,
        interpret=INTERPRET,
        compiler_params=pltpu.CompilerParams(vmem_limit_bytes=56 << 20),
    )


def dot(a, b, a_dim, b_dim):
    return lax.dot_general(
        a, b, (((a_dim,), (b_dim,)), ((), ())), preferred_element_type=jnp.float32
    )


def dispatch_kernel(offsets, tokens, pick_ref, high_ref, low_ref, own_ref, other_ref, *out_refs):
    micro = pick_ref.shape[0]
    part = own_ref.shape[-1] // 2
    rows = pick_ref.shape[1] // offsets

    def step(n, carry):
        m, rx, lanes = n // 4, n // 2 % 2, pl.ds(pl.multiple_of(n % 2 * part, part), part)
        at = pl.ds(pl.multiple_of(m * rows, rows), rows)
        from_x = pl.ds(pl.multiple_of((2 * rx * micro + m) * tokens, tokens), tokens)
        from_g = pl.ds(pl.multiple_of(((2 * rx + 1) * micro + m) * tokens, tokens), tokens)
        for rc, source in enumerate((own_ref, other_ref)):
            x = source[:, from_x, lanes].reshape(-1, part)
            g = source[:, from_g, lanes].reshape(-1, part)
            picked = dot(pick_ref[m], x, 1, 0).astype(jnp.bfloat16)
            scaled = dot(high_ref[m], g, 1, 0) + dot(low_ref[m], g, 1, 0)
            scaled = scaled.astype(jnp.bfloat16)
            for o in range(offsets):
                out_refs[o][2 * rc + rx, 0, at, lanes] = picked[o * rows : (o + 1) * rows]
                out_refs[o][2 * rc + rx, 1, at, lanes] = scaled[o * rows : (o + 1) * rows]
        return carry

    lax.fori_loop(0, 4 * micro, step, 0)


def combine_kernel(offsets, pick_ref, high_ref, low_ref, *refs):
    row_refs, (keep_ref, send_ref) = refs[:offsets], refs[offsets:]
    micro = pick_ref.shape[0]
    rows = pick_ref.shape[1] // offsets
    line, tokens, part = keep_ref.shape[0], keep_ref.shape[4], keep_ref.shape[5] // 2

    def step(n, carry):
        m, rx, lanes = n // 4, n // 2 % 2, pl.ds(pl.multiple_of(n % 2 * part, part), part)
        at = pl.ds(pl.multiple_of(m * rows, rows), rows)
        for rc, target in enumerate((keep_ref, send_ref)):
            out = jnp.concatenate([r[2 * rc + rx, 0, at, lanes] for r in row_refs], axis=0)
            back = jnp.concatenate([r[2 * rc + rx, 1, at, lanes] for r in row_refs], axis=0)
            value = dot(high_ref[m], out, 0, 0) + dot(low_ref[m], out, 0, 0)
            grad = dot(pick_ref[m], back, 0, 0)
            shape = (line, tokens, part)
            target[:, rx, 0, m, :, lanes] = value.reshape(shape).astype(target.dtype)
            target[:, rx, 1, m, :, lanes] = grad.reshape(shape).astype(target.dtype)
        return carry

    lax.fori_loop(0, 4 * micro, step, 0)


def swap_halves(lower, upper):
    half = lower.shape[1] // 2
    lane = lax.broadcasted_iota(jnp.int32, lower.shape, 1)
    first = jnp.where(lane < half, lower, pltpu.roll(upper, half, 1))
    second = jnp.where(lane < half, pltpu.roll(lower, half, 1), upper)
    return first, second


def expert_kernel(offsets, quarter_ref, fused_ref, down_ref, *refs):
    row_refs, refs = refs[:offsets], refs[offsets:]
    act_ref, refs = refs[0], refs[1:]
    out_refs, (w_scr, pre_scr) = refs[:offsets], refs[offsets:]
    _, blocks, _, pairs, width = down_ref.shape
    depth = blocks * pairs
    rows = row_refs[0].shape[2]
    pre_scr[...] = jnp.zeros_like(pre_scr)

    def first(blk, carry):
        q = quarter_ref[blk]
        x = jnp.concatenate([r[blk, 0] for r in row_refs], axis=0)
        g = jnp.concatenate([r[blk, 1] for r in row_refs], axis=0)

        def unpack(k, lower, upper, source):
            even, odd = swap_halves(lower.reshape(depth, width), upper.reshape(depth, width))
            w_scr[k, blk, :depth] = even
            w_scr[k, blk, depth:] = odd
            pre_scr[k] += dot(source, w_scr[k, blk], 1, 0)

        def ahead(k, carry):
            unpack(k, fused_ref[q, :, 0, k], fused_ref[q, :, 1, k], x)
            return carry

        lax.fori_loop(0, 2, ahead, 0)
        unpack(2, down_ref[q, :, 0], down_ref[q, :, 1], g)
        return carry

    lax.fori_loop(0, 4, first, 0)
    gate, up, hidden_grad = pre_scr[0], pre_scr[1], pre_scr[2]
    logistic = jax.nn.sigmoid(gate)
    swished = gate * logistic
    act_ref[2] = (swished * up).astype(jnp.bfloat16)
    act_ref[0] = (hidden_grad * up * logistic * (1.0 + gate * (1.0 - logistic))).astype(
        jnp.bfloat16
    )
    act_ref[1] = (hidden_grad * swished).astype(jnp.bfloat16)

    def second(n, carry):
        blk, lanes = n // 2, pl.ds(pl.multiple_of(n % 2 * depth, depth), depth)
        out = dot(act_ref[2], w_scr[2, blk, lanes], 1, 1).astype(jnp.bfloat16)
        back = dot(act_ref[0], w_scr[0, blk, lanes], 1, 1)
        back = (back + dot(act_ref[1], w_scr[1, blk, lanes], 1, 1)).astype(jnp.bfloat16)
        for o in range(offsets):
            out_refs[o][blk, 0, :, lanes] = out[o * rows : (o + 1) * rows]
            out_refs[o][blk, 1, :, lanes] = back[o * rows : (o + 1) * rows]
        return carry

    lax.fori_loop(0, 8, second, 0)


def gradient_kernel(offsets, quarter_ref, act_ref, *refs):
    row_refs, grad_ref = refs[:offsets], refs[offsets]
    _, blocks, _, _, pairs, width = grad_ref.shape
    depth = blocks * pairs

    def step(n, carry):
        blk, k = n // 3, n % 3
        q = quarter_ref[blk]
        source = jnp.concatenate([r[blk, k // 2] for r in row_refs], axis=0)
        total = dot(source, act_ref[k], 0, 0).astype(jnp.bfloat16)
        lower, upper = swap_halves(total[:depth], total[depth:])
        grad_ref[q, :, 0, k] = lower.reshape(blocks, pairs, width)
        grad_ref[q, :, 1, k] = upper.reshape(blocks, pairs, width)
        return carry

    lax.fori_loop(0, 12, step, 0)


def routing(route_ids, high, low, expert_ids, replica_plan, capacity):
    line, micro, _, tokens = route_ids.shape
    offsets = expert_ids.shape[0]
    match = route_ids[:, :, None] == expert_ids[None, None, :, None, None]

    def of_expert(values):
        picked = jnp.where(match, values[:, :, None], 0.0)
        return jnp.sum(picked, axis=3).transpose(1, 2, 0, 3)

    named = of_expert(jnp.ones_like(high))
    copies = 1 + jnp.sum(
        (replica_plan[:, None, :] == expert_ids[None, :, None]).astype(jnp.int32), axis=2
    )
    all_ids = jnp.arange(capacity.shape[1], dtype=jnp.int32)
    limit = jnp.sum(
        jnp.where(all_ids[None, None, :] == expert_ids[None, :, None], capacity[:, None, :], 0),
        axis=2,
    )
    token_ids = jnp.arange(tokens, dtype=jnp.int32)
    apart = token_ids[None, :] - token_ids[:, None]
    earlier = apart > 0
    rivals = earlier & (apart % copies[:, :, None, None] == 0)
    place = jnp.sum(named[..., None] * rivals[:, :, None].astype(jnp.float32), axis=3)
    count = jnp.sum(named[..., None] * earlier.astype(jnp.float32), axis=3)
    kept = (named > 0) & (place < limit[:, :, None, None].astype(jnp.float32))
    code = jnp.where(kept, count.astype(jnp.int32), -1)
    line_ids = jnp.arange(line, dtype=jnp.int32)
    slot_ids = jnp.arange(SLOTS, dtype=jnp.int32)
    same = line_ids[:, None, None, None] == line_ids[None, None, :, None]
    chosen = (code[:, :, None, None] == slot_ids[None, :, None, None]) & same
    shape = (micro, offsets * line * SLOTS, line * tokens)

    def spread(values):
        return jnp.where(chosen, values, 0.0).astype(jnp.bfloat16).reshape(shape)

    high, low = of_expert(high), of_expert(low)
    return spread(1.0), spread(high[:, :, None, None]), spread(low[:, :, None, None])


def shards(
    sizes,
    tokens_in,
    route_ids,
    route_gates,
    cotangent,
    gate_proj,
    up_proj,
    down_proj,
    replica_plan,
    capacity,
):
    nxl, ny, nz = sizes
    micro, tokens, feats = tokens_in.shape
    expert_count, pairs, width = gate_proj.shape
    xh, core = lax.axis_index("xh"), lax.axis_index("c")
    xl, y, z = (lax.axis_index(name) for name in EXPERT)
    steps = [(dx, dy) for dx in range(nxl) for dy in range(ny)]
    offsets = len(steps)
    swap = [(0, 1), (1, 0)]

    def to_homes(blocks):
        return lax.all_to_all(blocks, HOMES, split_axis=0, concat_axis=0, tiled=True)

    lane = jnp.arange(feats, dtype=jnp.int32)
    source = 2 * (lane % (feats // 2)) + lane // (feats // 2)
    halves = (lane[:, None] == source[None, :]).astype(jnp.bfloat16)
    own = jnp.stack([tokens_in, cotangent]).reshape(-1, feats)
    own = jnp.dot(own, halves, preferred_element_type=jnp.float32).astype(jnp.bfloat16)
    high = lax.reduce_precision(route_gates, 8, 7)
    meta = jnp.stack([route_ids.astype(jnp.float32), high, route_gates - high])
    meta = meta.transpose(0, 1, 3, 2).reshape(3, -1).astype(jnp.bfloat16)
    routes = meta.shape[1]
    meta = jnp.pad(meta, ((0, 13), (0, feats - routes)))
    across = lax.ppermute(own, "xh", swap)
    down = to_homes(down_proj)
    fused = to_homes(jnp.stack([gate_proj, up_proj], axis=1))
    line = lax.all_gather(jnp.concatenate([own, across, meta]), "z", axis=0)
    line_other = lax.ppermute(line, "c", swap)
    line_shape = (nz, 2, 2, micro, tokens, feats)

    expert_ids = jnp.stack(
        [((((xl + dx) % nxl) * ny + (y + dy) % ny) * nz + z) * 2 + core for dx, dy in steps]
    )
    start = 2 * own.shape[0]
    meta = line[:, start : start + 3, :routes].reshape(nz, 3, micro, -1, tokens)
    meta = meta.astype(jnp.float32)
    selections = routing(
        meta[:, 0].astype(jnp.int32), meta[:, 1], meta[:, 2], expert_ids, replica_plan, capacity
    )
    chunk_rows = micro * nz * SLOTS
    chunk = jax.ShapeDtypeStruct((4, 2, chunk_rows, feats), jnp.bfloat16)
    sent = call(
        functools.partial(dispatch_kernel, offsets, tokens), [VMEM] * 5, (chunk,) * offsets
    )(*selections, line, line_other)

    def moved(pieces, sign):
        done = [pieces[0]]
        for (dx, dy), piece in list(zip(steps, pieces))[1:]:
            pairs_list = [
                (a * ny + b, ((a + sign * dx) % nxl) * ny + (b + sign * dy) % ny)
                for a in range(nxl)
                for b in range(ny)
            ]
            done.append(lax.ppermute(piece, ("xl", "y"), pairs_list))
        return done

    arrived = moved(sent, 1)
    blk = jnp.arange(4, dtype=jnp.int32)
    quarters = (xh ^ (blk % 2)) * 2 + (core ^ (blk // 2))
    rows_all = offsets * chunk_rows
    view = (4, expert_count // 8, 2)
    act = jax.ShapeDtypeStruct((3, rows_all, width), jnp.bfloat16)
    results = call(
        functools.partial(expert_kernel, offsets),
        [SMEM] + [VMEM] * (2 + offsets),
        (act,) + (chunk,) * offsets,
        scratch=(
            pltpu.VMEM((3, 4, feats, width), jnp.bfloat16),
            pltpu.VMEM((3, rows_all, width), jnp.float32),
        ),
    )(
        quarters,
        fused.reshape(view + (2, pairs, width)),
        down.reshape(view + (pairs, width)),
        *arrived,
    )
    returned = moved(results[1:], -1)
    grads = call(
        functools.partial(gradient_kernel, offsets),
        [SMEM] + [VMEM] * (1 + offsets),
        jax.ShapeDtypeStruct(view + (3, pairs, width), jnp.bfloat16),
    )(quarters, results[0], *arrived)
    grads = to_homes(grads.reshape(expert_count, 3, pairs, width))

    keep, send = call(
        functools.partial(combine_kernel, offsets),
        [VMEM] * (3 + offsets),
        (
            jax.ShapeDtypeStruct(line_shape, jnp.bfloat16),
            jax.ShapeDtypeStruct(line_shape, jnp.bfloat16),
        ),
    )(*selections, *returned)
    send = lax.ppermute(send, "c", swap)
    keep = (keep.astype(jnp.float32) + send.astype(jnp.float32)).astype(jnp.bfloat16)
    keep = lax.psum_scatter(keep.reshape(-1, feats), "z", scatter_dimension=0, tiled=True)
    keep = keep.reshape(2, -1, feats)
    total = keep[0].astype(jnp.float32) + lax.ppermute(keep[1], "xh", swap).astype(jnp.float32)
    total = jnp.dot(total.astype(jnp.bfloat16), halves.T, preferred_element_type=jnp.float32)
    total = total.astype(jnp.bfloat16).reshape(2, micro, tokens, feats)
    return (total[0], total[1], grads[:, 0], grads[:, 1], grads[:, 2])


def build(devices, sizes):
    mesh = Mesh(devices.reshape((2, 2) + sizes), DP + EXPERT)
    weight = P(None, EXPERT, DP)
    in_specs = (weight, P(None, EXPERT), P(None, EXPERT), weight, weight, weight, weight, P(), P())

    def step(*args):
        return shards(sizes, *args)

    return jax.shard_map(
        step,
        mesh=mesh,
        in_specs=in_specs,
        out_specs=(weight,) * 5,
        check_vma=False,
    )


def solution(mesh):
    sizes = (2, 4, 8)
    step = build(mesh.devices, sizes)
    return step
```

time: 482 us -> 431 us (0.89)
  blocking collectives: 123 us -> 0 us
  waiting for transfers between devices: 155 us -> 233 us
  starting transfers between devices: 118 us -> 96.1 us
  Pallas kernels: 33.2 us -> 44.8 us
  local copies, waits for them, and re-layouts: 15.9 us -> 21.6 us
    all_gather x1 -> x0, blocking collectives: 123 us -> none  [shards(): meta = lax.all_gather(meta, 'z', axis=0)]
    ppermute x14, waiting for transfers between devices: 87.3 us -> 128 us  [moved(): done.append(lax.ppermute(piece, ('xl', 'y'), pairs_list))]
    all_to_all x2 -> x3, waiting for transfers between devices: 0.01 us -> 30.2 us  [to_homes(): lax.all_to_all(blocks, HOMES, split_axis=0, concat_axis=0, tiled=True)]
    ppermute x14, starting transfers between devices: 86.7 us -> 60.5 us  [moved(): done.append(lax.ppermute(piece, ('xl', 'y'), pairs_list))]
    all_gather x1, waiting for transfers between devices: 0.02 us -> 14.9 us  [shards(): line = lax.all_gather(jnp.concatenate([own, across, meta]), 'z', axis=0)]
    pallas_call x3 -> x4, Pallas kernels: 33.2 us -> 44.8 us  [the longest x1 18.1 us: shards(): call(functools.partial(expert_kernel, offsets), [SMEM] + [VMEM] * (2 + of...]
    ppermute x1, waiting for transfers between devices: 16.3 us -> 7.91 us  [shards(): across = lax.ppermute(own, 'xh', swap)]
    all_to_all x2 -> x3, starting transfers between devices: 28.2 us -> 32.5 us  [to_homes(): lax.all_to_all(blocks, HOMES, split_axis=0, concat_axis=0, tiled=True)]
  transfers between devices with their start and end apart: 22 -> 23, of which waited for: 9 -> 11; matrix products, arithmetic and copies ran while one was open for 5% -> 8% of each run, Pallas kernels for 3% -> 4%
where the time goes in v2:
time: 431 us; the launch traced here: 430 us
  waiting for transfers between devices  233 us (54%)
  starting transfers between devices  96.1 us (22%)
  Pallas kernels  44.8 us (10%)
  local copies, waits for them, and re-layouts  21.6 us (5%)
  other arithmetic  18.8 us (4%)
  between operations  14.5 us (3%)
    ppermute x14, waiting for transfers between devices, moved(): done.append(lax.ppermute(piece, ('xl', 'y'), pairs_list))  128 us
    ppermute x14, starting transfers between devices, moved(): done.append(lax.ppermute(piece, ('xl', 'y'), pairs_list))  60.5 us
    reduce_scatter x1, waiting for transfers between devices, shards(): lax.psum_scatter(keep.reshape(-1, feats), 'z', scatter_dimension=0, tiled...  42.3 us
    all_to_all x3, starting transfers between devices, to_homes(): lax.all_to_all(blocks, HOMES, split_axis=0, concat_axis=0, tiled=True)  32.5 us
    all_to_all x3, waiting for transfers between devices, to_homes(): lax.all_to_all(blocks, HOMES, split_axis=0, concat_axis=0, tiled=True)  30.2 us
    pallas_call x1, Pallas kernels, shards(): call(functools.partial(expert_kernel, offsets), [SMEM] + [VMEM] * (2 + of...  18.1 us
    all_gather x1, waiting for transfers between devices, shards(): line = lax.all_gather(jnp.concatenate([own, across, meta]), 'z', axis=0)  14.9 us
    pallas_call x1, Pallas kernels, shards(): call(functools.partial(gradient_kernel, offsets), [SMEM] + [VMEM] * (1 +...  11.3 us
  transfers between devices with their start and end apart: 23, of which 11 were waited for; matrix products, arithmetic and copies ran while one was open for 8% of the time, Pallas kernels for 4%

profile of v2, /device:TPU:6, one launch (start us, length us, event | category | flops | bytes accessed | tf_op | source)
XLA Modules:
  0.0 430.3 jit_solution(13941431057017715234)
XLA Ops:
  7.2 14.4 %all-to-all-start.1 = ((bf16[128,16,384]{2,1,0:T(8,128)(2,1)}), bf16[128,16,384]{2,1,0:T(8,128)(2,1)S(1)}, u32[]{:S(2)}, u32[]{:S(2)}) async-start(bf16[128,16,384]{2,1,0:T(8,128)(2,1)} %param.15), calls=%async_computation.1 | async-start | bytes 3145728 | tf_op jit(solution)/shard_map/all_to_all | solution.py:223
  23.7 7.9 %collective-permute-done = bf16[128,512]{1,0:T(8,128)(2,1)S(1)} collective-permute-done((bf16[128,512]{1,0:T(8,128)(2,1)S(1)}, bf16[128,512]{1,0:T(8,128)(2,1)S(1)}, u32[]{:S(2)}, u32[]{:S(2)}) %collective-permute-start) | collective-permute-done | bytes 131104 | tf_op jit(solution)/shard_map/ppermute | solution.py:235
  32.3 3.4 pad_maximum_fusion
  35.7 30.2 %all-to-all-done.1 = bf16[128,16,384]{2,1,0:T(8,128)(2,1)S(1)} async-done(((bf16[128,16,384]{2,1,0:T(8,128)(2,1)}), bf16[128,16,384]{2,1,0:T(8,128)(2,1)S(1)}, u32[]{:S(2)}, u32[]{:S(2)}) %all-to-all-start.1) | async-done | bytes 1572896 | tf_op jit(solution)/shard_map/all_to_all | solution.py:223
  67.1 8.7 %all-to-all-start = ((bf16[128,2,16,384]{3,2,1,0:T(8,128)(2,1)}), bf16[128,2,16,384]{3,2,1,0:T(8,128)(2,1)S(1)}, u32[]{:S(2)}, u32[]{:S(2)}) async-start(bf16[128,2,16,384]{3,2,1,0:T(8,128)(2,1)} %pad_maximum_fusion), calls=%async_computation | async-start | bytes 6291456 | tf_op jit(solution)/shard_map/all_to_all | solution.py:223
  76.4 14.9 %all-gather.3.cloned.1.call-done = bf16[2176,512]{1,0:T(8,128)(2,1)} async-done(((bf16[272,512]{1,0:T(8,128)(2,1)}), bf16[2176,512]{1,0:T(8,128)(2,1)}) %all-gather.3.cloned.1.call-update) | async-done | bytes 2228240 | tf_op jit(solution)/shard_map/all_gather | solution.py:238
  114.2 7.6 %shard_map.128 = (bf16[4,2,64,512]{3,2,1,0:T(8,128)(2,1)}, bf16[4,2,64,512]{3,2,1,0:T(8,128)(2,1)}, bf16[4,2,64,512]{3,2,1,0:T(8,128)(2,1)}, bf16[4,2,64,512]{3,...) custom-call(bf16[2,256,256]{2,1,0:T(8,128)(2,1)} %select_convert_fus, ...), custom_call_target="tpu_custom_call" | custom-call | tf_op jit(solution)/shard_map/pallas_call | solution.py:253
  129.9 17.4 %collective-permute-done.2.refs_1_ = bf16[4,2,64,512]{3,2,1,0:T(8,128)(2,1)} collective-permute-done((bf16[4,2,64,512]{3,2,1,0:T(8,128)(2,1)}, bf16[4,2,64,512]{3,2,1,0:T(8,128)(2,1)}, u32[]{:S(2)}, u32[]{:S(2)}) %collective-permute-start.2) | collective-permute-done | bytes 524320 | tf_op jit(solution)/shard_map/ppermute | solution.py:265
  150.4 33.3 %collective-permute-done.3.refs_2_ = bf16[4,2,64,512]{3,2,1,0:T(8,128)(2,1)} collective-permute-done((bf16[4,2,64,512]{3,2,1,0:T(8,128)(2,1)}, bf16[4,2,64,512]{3,2,1,0:T(8,128)(2,1)}, u32[]{:S(2)}, u32[]{:S(2)}) %collective-permute-start.3) | collective-permute-done | bytes 524320 | tf_op jit(solution)/shard_map/ppermute | solution.py:265
  184.2 14.4 %collective-permute-done.8.refs_7_ = bf16[4,2,64,512]{3,2,1,0:T(8,128)(2,1)} collective-permute-done((bf16[4,2,64,512]{3,2,1,0:T(8,128)(2,1)}, bf16[4,2,64,512]{3,2,1,0:T(8,128)(2,1)}, u32[]{:S(2)}, u32[]{:S(2)}) %collective-permute-start.8) | collective-permute-done | bytes 524320 | tf_op jit(solution)/shard_map/ppermute | solution.py:265
  198.7 18.1 %shard_map.129 = (bf16[3,512,384]{2,1,0:T(8,128)(2,1)}, bf16[4,2,64,512]{3,2,1,0:T(8,128)(2,1)}, bf16[4,2,64,512]{3,2,1,0:T(8,128)(2,1)}, bf16[4,2,64,512]{3,2,1...) custom-call(s32[4]{0:T(128)} %fusion.32.quarter_ref, ...), custom_call_target="tpu_custom_call" | custom-call | tf_op jit(solution)/shard_map/pallas_call | solution.py:274
  216.7 11.3 %shard_map.131 = bf16[4,16,2,3,16,384]{5,4,3,2,1,0:T(8,128)(2,1)} custom-call(s32[4]{0:T(128)} %fusion.32.quarter_ref, bf16[3,512,384]{2,1,0:T(8,128)(2,1)} %get-tuple-element.42.act_ref, bf16[4,2,64,512]{3,2,1,0:T(8,128)(2,1)} %get-tuple-element.24.refs_0_, bf16[4,2,64,512]{3,2,1,0:T(8,128)(2,1)} %collective-permute-done.2.refs_1_, ...), custom_call_target="tpu_custom_call" | custom-call | tf_op jit(solution)/shard_map/pallas_call | solution.py:289
  228.1 9.4 %all-to-all-start.2 = ((bf16[128,3,16,384]{3,2,1,0:T(8,128)(2,1)}), bf16[128,3,16,384]{3,2,1,0:T(8,128)(2,1)}, u32[]{:S(2)}, u32[]{:S(2)}) async-start(bf16[128,3,16,384]{3,2,1,0:T(8,128)(2,1)} %bitcast.57), calls=%async_computation.3 | async-start | bytes 9437184 | tf_op jit(solution)/shard_map/all_to_all | solution.py:223
  242.4 3.6 collective-permute-start.13
  246.0 45.4 %collective-permute-done.9.refs_1_ = bf16[4,2,64,512]{3,2,1,0:T(8,128)(2,1)S(1)} collective-permute-done((bf16[4,2,64,512]{3,2,1,0:T(8,128)(2,1)S(1)}, bf16[4,2,64,512]{3,2,1,0:T(8,128)(2,1)S(1)}, u32[]{:S(2)}, u32[]{:S(2)}) %collective-permute-start.9) | collective-permute-done | bytes 524320 | tf_op jit(solution)/shard_map/ppermute | solution.py:265
  291.4 3.3 collective-permute-start.14
  294.7 37.6 %collective-permute-start.15 = (bf16[4,2,64,512]{3,2,1,0:T(8,128)(2,1)}, bf16[4,2,64,512]{3,2,1,0:T(8,128)(2,1)S(1)}, u32[]{:S(2)}, u32[]{:S(2)}) collective-permute-start(bf16[4,2,64,512]{3,2,1,0:T(8,128)(2,1)} %get-tuple-element.39), channel_id=1, source_target_pairs={{0,40},{8,48},{16,56},{24,32},{32,8},{40,16},{48,24},{56,0},{1,41}... | collective-permute-start | bytes 1572872 | tf_op jit(solution)/shard_map/ppermute | solution.py:265
  332.3 17.8 %collective-permute-done.15.refs_7_ = bf16[4,2,64,512]{3,2,1,0:T(8,128)(2,1)S(1)} collective-permute-done((bf16[4,2,64,512]{3,2,1,0:T(8,128)(2,1)}, bf16[4,2,64,512]{3,2,1,0:T(8,128)(2,1)S(1)}, u32[]{:S(2)}, u32[]{:S(2)}) %collective-permute-start.15) | collective-permute-done | bytes 524320 | tf_op jit(solution)/shard_map/ppermute | solution.py:265
  351.0 7.8 %shard_map.130 = (bf16[8,2,2,2,32,512]{5,4,3,2,1,0:T(8,128)(2,1)}, bf16[8,2,2,2,32,512]{5,4,3,2,1,0:T(8,128)(2,1)}) custom-call(bf16[2,256,256]{2,1,0:T(8,128)(2,1)} %select_convert_fusion.2.pick_ref, bf16[2,256,256]{2,1,0:T(8,128)(2,1)} %get-tuple-element.52.high_ref, bf16[2,256,256]{2,1,0:T(8,128)(2,1)} %get-tuple-element.51.low_ref, ...), custom_call_target="tpu_custom_call" | custom-call | tf_op jit(solution)/shard_map/pallas_call | solution.py:296
  358.8 4.4 %collective-permute-done.16 = bf16[8,2,2,2,32,512]{5,4,3,2,1,0:T(8,128)(2,1)S(1)} collective-permute-done((bf16[8,2,2,2,32,512]{5,4,3,2,1,0:T(8,128)(2,1)}, bf16[8,2,2,2,32,512]{5,4,3,2,1,0:T(8,128)(2,1)S(1)}, u32[]{:S(2)}, u32[]{:S(2)}) %collective-permute-start.16) | collective-permute-done | bytes 2097184 | tf_op jit(solution)/shard_map/ppermute | solution.py:304
  363.1 3.9 add_convert_fusion
  367.1 42.3 %reduce-scatter.2.cloned.1.call-done = bf16[256,512]{1,0:T(8,128)(2,1)} async-done(((bf16[2048,512]{1,0:T(8,128)(2,1)}), bf16[256,512]{1,0:T(8,128)(2,1)}) %reduce-scatter.2.cloned.1.call-update) | async-done | bytes 262160 | tf_op jit(solution)/shard_map/reduce_scatter | solution.py:306
  411.8 5.0 %collective-permute-done.17 = bf16[128,512]{1,0:T(8,128)(2,1)S(1)} collective-permute-done((bf16[128,512]{1,0:T(8,128)(2,1)S(1)}, bf16[128,512]{1,0:T(8,128)(2,1)S(1)}, u32[]{:S(2)}, u32[]{:S(2)}) %collective-permute-start.17) | collective-permute-done | bytes 131104 | tf_op jit(solution)/shard_map/ppermute | solution.py:308
  418.7 4.7 %slice_bitcast_fusion = (bf16[128,16,384]{2,1,0:T(8,128)(2,1)}, bf16[128,16,384]{2,1,0:T(8,128)(2,1)}, bf16[128,16,384]{2,1,0:T(8,128)(2,1)}) fusion(bf16[128,3,16,384]{3,2,1,0:T(8,128)(2,1)} %all-to-all-done.2), kind=kLoop, calls=%fused_computation.4 | loop fusion | bytes 9437184 | tf_op jit(solution)/shard_map/squeeze | solution.py:311
  (111 shorter events, 49.0 us)
Async XLA Ops:
  7.2 58.7 %all-to-all-start.1 = ((bf16[128,16,384]{2,1,0:T(8,128)(2,1)}), bf16[128,16,384]{2,1,0:T(8,128)(2,1)S(1)}, u32[]{:S(2)}, u32[]{:S(2)}) async-start(bf16[128,16,384]{2,1,0:T(8,128)(2,1)} %param.15), calls=%async_computation.1 | async-start | bytes 3145728 | tf_op jit(solution)/shard_map/all_to_all | solution.py:223
  21.6 69.7 %all-gather.3.cloned.1.call-start = ((), (), s32[]{:S(2)}) async-start(), calls=%async_computation.5 | async-start | bytes 2506752 | tf_op jit(solution)/shard_map/all_gather | solution.py:238
  22.0 9.5 %collective-permute-start = (bf16[128,512]{1,0:T(8,128)(2,1)S(1)}, bf16[128,512]{1,0:T(8,128)(2,1)S(1)}, u32[]{:S(2)}, u32[]{:S(2)}) collective-permute-start(bf16[128,512]{1,0:T(8,128)(2,1)S(1)} %convolution_convert_fusion.1), channel_id=1, source_target_pairs={{0,128},{128,0},{1,129},{129,1},{2,130},{130,2},{3,131},{131,3},{4... | collective-permute-start | bytes 393224 | tf_op jit(solution)/shard_map/ppermute | solution.py:235
  67.1 117.1 %all-to-all-start = ((bf16[128,2,16,384]{3,2,1,0:T(8,128)(2,1)}), bf16[128,2,16,384]{3,2,1,0:T(8,128)(2,1)S(1)}, u32[]{:S(2)}, u32[]{:S(2)}) async-start(bf16[128,2,16,384]{3,2,1,0:T(8,128)(2,1)} %pad_maximum_fusion), calls=%async_computation | async-start | bytes 6291456 | tf_op jit(solution)/shard_map/all_to_all | solution.py:223
  91.3 22.9 %collective-permute-start.1 = (bf16[8,272,512]{2,1,0:T(8,128)(2,1)}, bf16[8,272,512]{2,1,0:T(8,128)(2,1)}, u32[]{:S(2)}, u32[]{:S(2)}) collective-permute-start(bf16[8,272,512]{2,1,0:T(8,128)(2,1)} %bitcast.61), channel_id=1, source_target_pairs={{0,64},{64,0},{1,65},{65,1},{2,66},{66,2},{3,67},{67,3},{4,68},{68... | collective-permute-start | bytes 6684680 | tf_op jit(solution)/shard_map/ppermute | solution.py:239
  121.8 25.5 %collective-permute-start.2 = (bf16[4,2,64,512]{3,2,1,0:T(8,128)(2,1)}, bf16[4,2,64,512]{3,2,1,0:T(8,128)(2,1)}, u32[]{:S(2)}, u32[]{:S(2)}) collective-permute-start(bf16[4,2,64,512]{3,2,1,0:T(8,128)(2,1)} %get-tuple-element.25), channel_id=1, source_target_pairs={{0,8},{8,16},{16,24},{24,0},{32,40},{40,48},{48,56},{56,32},{1,9},... | collective-permute-start | bytes 1572872 | tf_op jit(solution)/shard_map/ppermute | solution.py:265
  123.4 60.2 %collective-permute-start.3 = (bf16[4,2,64,512]{3,2,1,0:T(8,128)(2,1)}, bf16[4,2,64,512]{3,2,1,0:T(8,128)(2,1)}, u32[]{:S(2)}, u32[]{:S(2)}) collective-permute-start(bf16[4,2,64,512]{3,2,1,0:T(8,128)(2,1)} %get-tuple-element.26), channel_id=1, source_target_pairs={{0,16},{8,24},{16,0},{24,8},{32,48},{40,56},{48,32},{56,40},{1,17}... | collective-permute-start | bytes 1572872 | tf_op jit(solution)/shard_map/ppermute | solution.py:265
  126.4 57.8 %collective-permute-start.4 = (bf16[4,2,64,512]{3,2,1,0:T(8,128)(2,1)}, bf16[4,2,64,512]{3,2,1,0:T(8,128)(2,1)}, u32[]{:S(2)}, u32[]{:S(2)}) collective-permute-start(bf16[4,2,64,512]{3,2,1,0:T(8,128)(2,1)} %get-tuple-element.27), channel_id=1, source_target_pairs={{0,24},{8,0},{16,8},{24,16},{32,56},{40,32},{48,40},{56,48},{1,25}... | collective-permute-start | bytes 1572872 | tf_op jit(solution)/shard_map/ppermute | solution.py:265
  127.7 56.5 %collective-permute-start.5 = (bf16[4,2,64,512]{3,2,1,0:T(8,128)(2,1)}, bf16[4,2,64,512]{3,2,1,0:T(8,128)(2,1)}, u32[]{:S(2)}, u32[]{:S(2)}) collective-permute-start(bf16[4,2,64,512]{3,2,1,0:T(8,128)(2,1)} %get-tuple-element.28), channel_id=1, source_target_pairs={{0,32},{8,40},{16,48},{24,56},{32,0},{40,8},{48,16},{56,24},{1,33}... | collective-permute-start | bytes 1572872 | tf_op jit(solution)/shard_map/ppermute | solution.py:265
  127.7 56.5 %collective-permute-start.6 = (bf16[4,2,64,512]{3,2,1,0:T(8,128)(2,1)}, bf16[4,2,64,512]{3,2,1,0:T(8,128)(2,1)}, u32[]{:S(2)}, u32[]{:S(2)}) collective-permute-start(bf16[4,2,64,512]{3,2,1,0:T(8,128)(2,1)} %get-tuple-element.29), channel_id=1, source_target_pairs={{0,40},{8,48},{16,56},{24,32},{32,8},{40,16},{48,24},{56,0},{1,41}... | collective-permute-start | bytes 1572872 | tf_op jit(solution)/shard_map/ppermute | solution.py:265
  147.3 36.9 %collective-permute-start.7 = (bf16[4,2,64,512]{3,2,1,0:T(8,128)(2,1)}, bf16[4,2,64,512]{3,2,1,0:T(8,128)(2,1)}, u32[]{:S(2)}, u32[]{:S(2)}) collective-permute-start(bf16[4,2,64,512]{3,2,1,0:T(8,128)(2,1)} %get-tuple-element.30), channel_id=1, source_target_pairs={{0,48},{8,56},{16,32},{24,40},{32,16},{40,24},{48,0},{56,8},{1,49}... | collective-permute-start | bytes 1572872 | tf_op jit(solution)/shard_map/ppermute | solution.py:265
  183.7 15.0 %collective-permute-start.8 = (bf16[4,2,64,512]{3,2,1,0:T(8,128)(2,1)}, bf16[4,2,64,512]{3,2,1,0:T(8,128)(2,1)}, u32[]{:S(2)}, u32[]{:S(2)}) collective-permute-start(bf16[4,2,64,512]{3,2,1,0:T(8,128)(2,1)} %get-tuple-element.31), channel_id=1, source_target_pairs={{0,56},{8,32},{16,40},{24,48},{32,24},{40,0},{48,8},{56,16},{1,57}... | collective-permute-start | bytes 1572872 | tf_op jit(solution)/shard_map/ppermute | solution.py:265
  228.1 190.7 %all-to-all-start.2 = ((bf16[128,3,16,384]{3,2,1,0:T(8,128)(2,1)}), bf16[128,3,16,384]{3,2,1,0:T(8,128)(2,1)}, u32[]{:S(2)}, u32[]{:S(2)}) async-start(bf16[128,3,16,384]{3,2,1,0:T(8,128)(2,1)} %bitcast.57), calls=%async_computation.3 | async-start | bytes 9437184 | tf_op jit(solution)/shard_map/all_to_all | solution.py:223
  237.5 171.8 %reduce-scatter.2.cloned.1.call-start = ((), (), s32[]{:S(2)}) async-start(), calls=%async_computation.4 | async-start | bytes 2359296 | tf_op jit(solution)/shard_map/reduce_scatter | solution.py:306
  237.6 53.8 %collective-permute-start.9 = (bf16[4,2,64,512]{3,2,1,0:T(8,128)(2,1)S(1)}, bf16[4,2,64,512]{3,2,1,0:T(8,128)(2,1)S(1)}, u32[]{:S(2)}, u32[]{:S(2)}) collective-permute-start(bf16[4,2,64,512]{3,2,1,0:T(8,128)(2,1)S(1)} %copy-done.16), channel_id=1, source_target_pairs={{0,24},{8,0},{16,8},{24,16},{32,56},{40,32},{48,40},{56,48},{1,25}... | collective-permute-start | bytes 1572872 | tf_op jit(solution)/shard_map/ppermute | solution.py:265
  240.7 54.0 %collective-permute-start.10 = (bf16[4,2,64,512]{3,2,1,0:T(8,128)(2,1)}, bf16[4,2,64,512]{3,2,1,0:T(8,128)(2,1)S(1)}, u32[]{:S(2)}, u32[]{:S(2)}) collective-permute-start(bf16[4,2,64,512]{3,2,1,0:T(8,128)(2,1)} %get-tuple-element.34), channel_id=1, source_target_pairs={{0,16},{8,24},{16,0},{24,8},{32,48},{40,56},{48,32},{56,40},{1,17}... | collective-permute-start | bytes 1572872 | tf_op jit(solution)/shard_map/ppermute | solution.py:265
  241.3 91.0 %collective-permute-start.11 = (bf16[4,2,64,512]{3,2,1,0:T(8,128)(2,1)}, bf16[4,2,64,512]{3,2,1,0:T(8,128)(2,1)S(1)}, u32[]{:S(2)}, u32[]{:S(2)}) collective-permute-start(bf16[4,2,64,512]{3,2,1,0:T(8,128)(2,1)} %get-tuple-element.35), channel_id=1, source_target_pairs={{0,8},{8,16},{16,24},{24,0},{32,40},{40,48},{48,56},{56,32},{1,9},... | collective-permute-start | bytes 1572872 | tf_op jit(solution)/shard_map/ppermute | solution.py:265
  242.3 90.0 %collective-permute-start.12 = (bf16[4,2,64,512]{3,2,1,0:T(8,128)(2,1)}, bf16[4,2,64,512]{3,2,1,0:T(8,128)(2,1)S(1)}, u32[]{:S(2)}, u32[]{:S(2)}) collective-permute-start(bf16[4,2,64,512]{3,2,1,0:T(8,128)(2,1)} %get-tuple-element.36), channel_id=1, source_target_pairs={{0,32},{8,40},{16,48},{24,56},{32,0},{40,8},{48,16},{56,24},{1,33}... | collective-permute-start | bytes 1572872 | tf_op jit(solution)/shard_map/ppermute | solution.py:265
  242.4 89.9 %collective-permute-start.13 = (bf16[4,2,64,512]{3,2,1,0:T(8,128)(2,1)}, bf16[4,2,64,512]{3,2,1,0:T(8,128)(2,1)S(1)}, u32[]{:S(2)}, u32[]{:S(2)}) collective-permute-start(bf16[4,2,64,512]{3,2,1,0:T(8,128)(2,1)} %get-tuple-element.37), channel_id=1, source_target_pairs={{0,56},{8,32},{16,40},{24,48},{32,24},{40,0},{48,8},{56,16},{1,57}... | collective-permute-start | bytes 1572872 | tf_op jit(solution)/shard_map/ppermute | solution.py:265
  291.4 58.8 %copy-start.3 = (bf16[4,2,64,512]{3,2,1,0:T(8,128)(2,1)}, bf16[4,2,64,512]{3,2,1,0:T(8,128)(2,1)S(1)}, u32[]{:S(2)}) copy-start(bf16[4,2,64,512]{3,2,1,0:T(8,128)(2,1)S(1)} %collective-permute-done.9.refs_1_) | copy-start | bytes 1572868
  291.4 40.9 %collective-permute-start.14 = (bf16[4,2,64,512]{3,2,1,0:T(8,128)(2,1)}, bf16[4,2,64,512]{3,2,1,0:T(8,128)(2,1)S(1)}, u32[]{:S(2)}, u32[]{:S(2)}) collective-permute-start(bf16[4,2,64,512]{3,2,1,0:T(8,128)(2,1)} %get-tuple-element.38), channel_id=1, source_target_pairs={{0,48},{8,56},{16,32},{24,40},{32,16},{40,24},{48,0},{56,8},{1,49}... | collective-permute-start | bytes 1572872 | tf_op jit(solution)/shard_map/ppermute | solution.py:265
  294.7 55.5 %collective-permute-start.15 = (bf16[4,2,64,512]{3,2,1,0:T(8,128)(2,1)}, bf16[4,2,64,512]{3,2,1,0:T(8,128)(2,1)S(1)}, u32[]{:S(2)}, u32[]{:S(2)}) collective-permute-start(bf16[4,2,64,512]{3,2,1,0:T(8,128)(2,1)} %get-tuple-element.39), channel_id=1, source_target_pairs={{0,40},{8,48},{16,56},{24,32},{32,8},{40,16},{48,24},{56,0},{1,41}... | collective-permute-start | bytes 1572872 | tf_op jit(solution)/shard_map/ppermute | solution.py:265
  358.8 4.4 %collective-permute-start.16 = (bf16[8,2,2,2,32,512]{5,4,3,2,1,0:T(8,128)(2,1)}, bf16[8,2,2,2,32,512]{5,4,3,2,1,0:T(8,128)(2,1)S(1)}, u32[]{:S(2)}, u32[]{:S(2)}) collective-permute-start(bf16[8,2,2,2,32,512]{5,4,3,2,1,0:T(8,128)(2,1)} %get-tuple-element.41), channel_id=1, source_target_pairs={{0,64},{64,0},{1,65},{65,1},{2,66},{66,2},{3,67},{67,3},{4,68},{68... | collective-permute-start | bytes 6291464 | tf_op jit(solution)/shard_map/ppermute | solution.py:304
  410.3 6.6 %collective-permute-start.17 = (bf16[128,512]{1,0:T(8,128)(2,1)S(1)}, bf16[128,512]{1,0:T(8,128)(2,1)S(1)}, u32[]{:S(2)}, u32[]{:S(2)}) collective-permute-start(bf16[128,512]{1,0:T(8,128)(2,1)S(1)} %slice.53), channel_id=1, source_target_pairs={{0,128},{128,0},{1,129},{129,1},{2,130},{130,2},{3,131},{131,3},{4... | collective-permute-start | bytes 393224 | tf_op jit(solution)/shard_map/ppermute | solution.py:308
  (16 other events, 320.5 us)
Sparse Core Ops, SparseCore 0:
  32.4 58.7 all-gather.2
  367.2 42.0 reduce-scatter.1

commit v3 on v2

v3 whole, which is shorter than its diff:
```python
import functools

import jax
import jax.numpy as jnp
from jax import lax
from jax.experimental import pallas as pl
from jax.experimental.pallas import tpu as pltpu
from jax.sharding import Mesh
from jax.sharding import PartitionSpec as P


INTERPRET = False
EXPERT = ("xl", "y", "z")
DP = ("xh", "c")
HOMES = ("xl", "y", "z", "c")
SLOTS = 4
META_ROWS = 32


def spec(shape, at=None):
    rank = len(shape)
    if at is None:
        return pl.BlockSpec(shape, lambda i, *refs: (0,) * rank)
    return pl.BlockSpec(shape, lambda i, *refs: (at(i, *refs) + (0,) * rank)[:rank])


def call(kernel, grid, in_specs, out_specs, out_shape, scratch=()):
    return pl.pallas_call(
        kernel,
        grid_spec=pltpu.PrefetchScalarGridSpec(
            num_scalar_prefetch=1,
            grid=(grid,),
            in_specs=in_specs,
            out_specs=out_specs,
            scratch_shapes=scratch,
        ),
        out_shape=out_shape,
        interpret=INTERPRET,
        compiler_params=pltpu.CompilerParams(
            dimension_semantics=("arbitrary",), vmem_limit_bytes=56 << 20
        ),
    )


def dot(a, b, a_dim, b_dim):
    return lax.dot_general(
        a, b, (((a_dim,), (b_dim,)), ((), ())), preferred_element_type=jnp.float32
    )


def select_rows(offsets, tokens, top, expert_ref, meta_ref, divides_ref, limit_ref, pick_refs):
    pick_ref, high_ref, low_ref = pick_refs
    micro = pick_ref.shape[0]
    rows = pick_ref.shape[1] // offsets
    columns = pick_ref.shape[2]
    named_rows = jnp.sum(meta_ref[...].astype(jnp.float32), axis=0)
    token = lax.broadcasted_iota(jnp.int32, (offsets, columns), 1) % tokens
    shape = (offsets * rows, columns)
    row = lax.broadcasted_iota(jnp.int32, shape, 0)
    source = lax.broadcasted_iota(jnp.int32, shape, 1) // tokens
    same = (row % rows) // SLOTS == source
    slot = (row % SLOTS).astype(jnp.float32)

    for m in range(micro):
        at = slice(m * top, (m + 1) * top)
        ids = named_rows[at, :columns]
        gates = (
            named_rows[at, columns : 2 * columns],
            named_rows[(micro + m) * top : (micro + m + 1) * top, :columns],
        )
        named, high, low = [], [], []
        for o in range(offsets):
            match = ids == expert_ref[o].astype(jnp.float32)
            named.append(jnp.sum(match.astype(jnp.float32), axis=0, keepdims=True))
            high.append(jnp.sum(jnp.where(match, gates[0], 0.0), axis=0, keepdims=True))
            low.append(jnp.sum(jnp.where(match, gates[1], 0.0), axis=0, keepdims=True))
        named = jnp.concatenate(named, axis=0)
        count = jnp.zeros_like(named)
        place = jnp.zeros_like(named)
        for apart in range(1, tokens):
            prior = jnp.where(token >= apart, pltpu.roll(named, apart, 1), 0.0)
            count += prior
            place += prior * divides_ref[m, :, apart : apart + 1]
        kept = (named > 0.0) & (place < limit_ref[m, :, :1])
        code = jnp.where(kept, count, -1.0)

        def spread(values):
            pieces = [jnp.broadcast_to(v, (rows, columns)) for v in values]
            return jnp.concatenate(pieces, axis=0)

        chosen = same & (spread([code[o : o + 1] for o in range(offsets)]) == slot)
        pick_ref[m] = jnp.where(chosen, 1.0, 0.0).astype(jnp.bfloat16)
        high_ref[m] = jnp.where(chosen, spread(high), 0.0).astype(jnp.bfloat16)
        low_ref[m] = jnp.where(chosen, spread(low), 0.0).astype(jnp.bfloat16)


def dispatch_kernel(
    offsets, tokens, top, expert_ref, divides_ref, limit_ref, meta_ref, own_ref, other_ref, *refs
):
    pick_refs, out_refs = refs[:3], refs[3:]
    pick_ref, high_ref, low_ref = pick_refs
    micro = pick_ref.shape[0]
    feats = own_ref.shape[2]
    rows = pick_ref.shape[1] // offsets

    @pl.when(pl.program_id(0) == 0)
    def _():
        select_rows(offsets, tokens, top, expert_ref, meta_ref, divides_ref, limit_ref, pick_refs)

    for m in range(micro):
        at = slice(m * rows, (m + 1) * rows)
        for rc, source in enumerate((own_ref, other_ref)):
            x = source[:, m * tokens : (m + 1) * tokens].reshape(-1, feats)
            g = source[:, (micro + m) * tokens : (micro + m + 1) * tokens].reshape(-1, feats)
            picked = dot(pick_ref[m], x, 1, 0).astype(jnp.bfloat16)
            scaled = dot(high_ref[m], g, 1, 0) + dot(low_ref[m], g, 1, 0)
            scaled = scaled.astype(jnp.bfloat16)
            for o in range(offsets):
                out_refs[o][rc, 0, 0, at] = picked[o * rows : (o + 1) * rows]
                out_refs[o][rc, 0, 1, at] = scaled[o * rows : (o + 1) * rows]


def combine_kernel(offsets, expert_ref, pick_ref, high_ref, low_ref, *refs):
    row_refs, (keep_ref, send_ref) = refs[:offsets], refs[offsets:]
    micro = pick_ref.shape[0]
    rows = pick_ref.shape[1] // offsets
    shape = (keep_ref.shape[0],) + keep_ref.shape[4:]
    for m in range(micro):
        at = slice(m * rows, (m + 1) * rows)
        for rc, target in enumerate((keep_ref, send_ref)):
            out = jnp.concatenate([r[rc, 0, 0, at] for r in row_refs], axis=0)
            back = jnp.concatenate([r[rc, 0, 1, at] for r in row_refs], axis=0)
            value = dot(high_ref[m], out, 0, 0) + dot(low_ref[m], out, 0, 0)
            grad = dot(pick_ref[m], back, 0, 0)
            target[:, 0, 0, m] = value.astype(target.dtype).reshape(shape)
            target[:, 0, 1, m] = grad.astype(target.dtype).reshape(shape)


def swap_halves(lower, upper):
    half = lower.shape[1] // 2
    lane = lax.broadcasted_iota(jnp.int32, lower.shape, 1)
    first = jnp.where(lane < half, lower, pltpu.roll(upper, half, 1))
    second = jnp.where(lane < half, pltpu.roll(lower, half, 1), upper)
    return first, second


def expert_kernel(offsets, quarter_ref, fused_ref, down_ref, *refs):
    row_refs, refs = refs[:offsets], refs[offsets:]
    act_ref, refs = refs[0], refs[1:]
    out_refs, (w_scr, pre_scr) = refs[:offsets], refs[offsets:]
    _, blocks, _, pairs, width = down_ref.shape
    depth = blocks * pairs
    rows = row_refs[0].shape[3]
    step = pl.program_id(0)

    @pl.when(step == 0)
    def _():
        pre_scr[...] = jnp.zeros_like(pre_scr)

    @pl.when(step < 4)
    def _():
        x = jnp.concatenate([r[0, 0, 0] for r in row_refs], axis=0)
        g = jnp.concatenate([r[0, 0, 1] for r in row_refs], axis=0)
        for k in range(3):
            if k < 2:
                lower, upper = fused_ref[0, :, 0, k], fused_ref[0, :, 1, k]
            else:
                lower, upper = down_ref[0, :, 0], down_ref[0, :, 1]
            even, odd = swap_halves(lower.reshape(depth, width), upper.reshape(depth, width))
            both = jnp.concatenate([even, odd], axis=0)
            w_scr[k, step] = both
            pre_scr[k] += dot(g if k == 2 else x, both, 1, 0)

    @pl.when(step == 3)
    def _():
        gate, up, hidden_grad = pre_scr[0], pre_scr[1], pre_scr[2]
        logistic = jax.nn.sigmoid(gate)
        swished = gate * logistic
        act_ref[2] = (swished * up).astype(jnp.bfloat16)
        act_ref[0] = (hidden_grad * up * logistic * (1.0 + gate * (1.0 - logistic))).astype(
            jnp.bfloat16
        )
        act_ref[1] = (hidden_grad * swished).astype(jnp.bfloat16)

    @pl.when(step >= 4)
    def _():
        blk = step - 4
        out = dot(act_ref[2], w_scr[2, blk], 1, 1).astype(jnp.bfloat16)
        back = dot(act_ref[0], w_scr[0, blk], 1, 1)
        back = (back + dot(act_ref[1], w_scr[1, blk], 1, 1)).astype(jnp.bfloat16)
        for o in range(offsets):
            out_refs[o][0, 0, 0] = out[o * rows : (o + 1) * rows]
            out_refs[o][0, 0, 1] = back[o * rows : (o + 1) * rows]


def gradient_kernel(offsets, quarter_ref, act_ref, *refs):
    row_refs, grad_ref = refs[:offsets], refs[offsets]
    _, blocks, _, members, pairs, width = grad_ref.shape
    depth = blocks * pairs
    source = jnp.concatenate([r[0, 0, 0] for r in row_refs], axis=0)
    for k in range(members):
        total = dot(source, act_ref[k], 0, 0).astype(jnp.bfloat16)
        lower, upper = swap_halves(total[:depth], total[depth:])
        grad_ref[0, :, 0, k] = lower.reshape(blocks, pairs, width)
        grad_ref[0, :, 1, k] = upper.reshape(blocks, pairs, width)


def shards(
    sizes,
    tokens_in,
    route_ids,
    route_gates,
    cotangent,
    gate_proj,
    up_proj,
    down_proj,
    replica_plan,
    capacity,
):
    nxl, ny, nz = sizes
    micro, tokens, feats = tokens_in.shape
    expert_count, pairs, width = gate_proj.shape
    xh, core = lax.axis_index("xh"), lax.axis_index("c")
    xl, y, z = (lax.axis_index(name) for name in EXPERT)
    steps = [(dx, dy) for dx in range(nxl) for dy in range(ny)]
    offsets = len(steps)
    swap = [(0, 1), (1, 0)]

    def to_homes(blocks):
        return lax.all_to_all(blocks, HOMES, split_axis=0, concat_axis=0, tiled=True)

    lane = jnp.arange(feats, dtype=jnp.int32)
    source = 2 * (lane % (feats // 2)) + lane // (feats // 2)
    halves = (lane[:, None] == source[None, :]).astype(jnp.bfloat16)
    own = jnp.stack([tokens_in, cotangent]).reshape(-1, feats)
    own = jnp.dot(own, halves, preferred_element_type=jnp.float32).astype(jnp.bfloat16)
    columns = nz * tokens
    routes = micro * route_ids.shape[2]
    high = lax.reduce_precision(route_gates, 8, 7)
    meta = jnp.stack([route_ids.astype(jnp.float32), high, route_gates - high])
    meta = meta.transpose(0, 1, 3, 2).astype(jnp.bfloat16).reshape(3, routes, tokens)
    mine = jnp.arange(columns, dtype=jnp.int32) // tokens == z
    meta = jnp.where(mine, jnp.tile(meta, (1, 1, nz)), 0)
    meta = jnp.concatenate(
        [
            jnp.concatenate([meta[0], meta[1]], axis=1),
            jnp.concatenate([meta[2], jnp.zeros_like(meta[2])], axis=1),
        ]
    )
    meta = jnp.pad(meta, ((0, META_ROWS - 2 * routes), (0, feats - 2 * columns)))
    across = lax.ppermute(own, "xh", swap)
    down = to_homes(down_proj)
    fused = to_homes(jnp.stack([gate_proj, up_proj], axis=1))
    line = lax.all_gather(jnp.concatenate([own, across, meta]), "z", axis=0)
    line_other = lax.ppermute(line, "c", swap)
    line_shape = (nz, 2, 2, micro, tokens, feats)

    expert_ids = jnp.stack(
        [((((xl + dx) % nxl) * ny + (y + dy) % ny) * nz + z) * 2 + core for dx, dy in steps]
    )
    copies = 1 + jnp.sum(
        (replica_plan[:, None, :] == expert_ids[None, :, None]).astype(jnp.int32), axis=2
    )
    all_ids = jnp.arange(expert_count, dtype=jnp.int32)
    limit = jnp.sum(
        jnp.where(all_ids[None, None, :] == expert_ids[None, :, None], capacity[:, None, :], 0),
        axis=2,
    )
    apart = jnp.arange(128, dtype=jnp.int32)
    divides = (apart % copies[:, :, None] == 0).astype(jnp.float32)
    limit = jnp.broadcast_to(limit[:, :, None].astype(jnp.float32), divides.shape)
    chunk_rows = micro * nz * SLOTS
    chunk = jax.ShapeDtypeStruct((2, 2, 2, chunk_rows, feats), jnp.bfloat16)
    chunk_pair = spec((2, 1, 2, chunk_rows, feats), lambda i, *refs: (0, i))
    pick_shape = (micro, offsets * nz * SLOTS, columns)
    pick = jax.ShapeDtypeStruct(pick_shape, jnp.bfloat16)
    line_rows = 2 * micro * tokens
    line_spec = spec((nz, line_rows, feats), lambda i, *refs: (0, i))
    sent = call(
        functools.partial(dispatch_kernel, offsets, tokens, route_ids.shape[2]),
        2,
        [spec(divides.shape), spec(limit.shape)]
        + [spec((nz, META_ROWS, feats), lambda i, *refs: (0, 2 * line_rows // META_ROWS))]
        + [line_spec] * 2,
        [spec(pick_shape)] * 3 + [chunk_pair] * offsets,
        [pick] * 3 + [chunk] * offsets,
    )(expert_ids, divides, limit, line, line, line_other)
    selections, sent = sent[:3], sent[3:]

    def moved(pieces, sign):
        done = [pieces[0]]
        for (dx, dy), piece in list(zip(steps, pieces))[1:]:
            pairs_list = [
                (a * ny + b, ((a + sign * dx) % nxl) * ny + (b + sign * dy) % ny)
                for a in range(nxl)
                for b in range(ny)
            ]
            done.append(lax.ppermute(piece, ("xl", "y"), pairs_list))
        return done

    arrived = moved(sent, 1)
    blk = jnp.arange(4, dtype=jnp.int32)
    quarters = (xh ^ (blk % 2)) * 2 + (core ^ (blk // 2))
    rows_all = offsets * chunk_rows
    blocks = expert_count // 8
    view = (4, blocks, 2)
    act = jax.ShapeDtypeStruct((3, rows_all, width), jnp.bfloat16)

    def early(i, *refs):
        i = jnp.minimum(i, 3)
        return (i // 2, i % 2)

    def late(i, *refs):
        i = jnp.maximum(i - 4, 0)
        return (i // 2, i % 2)

    results = call(
        functools.partial(expert_kernel, offsets),
        8,
        [
            spec((1, blocks, 2, 2, pairs, width), lambda i, q: (q[jnp.minimum(i, 3)],)),
            spec((1, blocks, 2, pairs, width), lambda i, q: (q[jnp.minimum(i, 3)],)),
        ]
        + [spec((1, 1, 2, chunk_rows, feats), early)] * offsets,
        [spec(act.shape)] + [spec((1, 1, 2, chunk_rows, feats), late)] * offsets,
        [act] + [chunk] * offsets,
        scratch=(
            pltpu.VMEM((3, 4, feats, width), jnp.bfloat16),
            pltpu.VMEM((3, rows_all, width), jnp.float32),
        ),
    )(
        quarters,
        fused.reshape(view + (2, pairs, width)),
        down.reshape(view + (pairs, width)),
        *arrived,
    )
    returned = moved(results[1:], -1)

    def gradient(which, first, members):
        return call(
            functools.partial(gradient_kernel, offsets),
            4,
            [spec((members, rows_all, width), lambda i, *refs: (first // members,))]
            + [spec((1, 1, 1, chunk_rows, feats), lambda i, *refs: (i // 2, i % 2, which))]
            * offsets,
            spec((1, blocks, 2, members, pairs, width), lambda i, q: (q[i],)),
            jax.ShapeDtypeStruct(view + (members, pairs, width), jnp.bfloat16),
        )(quarters, results[0], *arrived)

    fused_grad = to_homes(gradient(0, 0, 2).reshape(expert_count, 2, pairs, width))
    down_grad = to_homes(gradient(1, 2, 1).reshape(expert_count, pairs, width))

    keep, send = call(
        functools.partial(combine_kernel, offsets),
        2,
        [spec(pick_shape)] * 3 + [chunk_pair] * offsets,
        [spec((nz, 1, 2, micro, tokens, feats), lambda i, *refs: (0, i))] * 2,
        [jax.ShapeDtypeStruct(line_shape, jnp.bfloat16)] * 2,
    )(quarters, *selections, *returned)
    send = lax.ppermute(send, "c", swap)
    keep = (keep.astype(jnp.float32) + send.astype(jnp.float32)).astype(jnp.bfloat16)
    keep = lax.psum_scatter(keep.reshape(-1, feats), "z", scatter_dimension=0, tiled=True)
    keep = keep.reshape(2, -1, feats)
    total = keep[0].astype(jnp.float32) + lax.ppermute(keep[1], "xh", swap).astype(jnp.float32)
    total = jnp.dot(total.astype(jnp.bfloat16), halves.T, preferred_element_type=jnp.float32)
    total = total.astype(jnp.bfloat16).reshape(2, micro, tokens, feats)
    return (total[0], total[1], fused_grad[:, 0], fused_grad[:, 1], down_grad)


def build(devices, sizes):
    mesh = Mesh(devices.reshape((2, 2) + sizes), DP + EXPERT)
    weight = P(None, EXPERT, DP)
    in_specs = (weight, P(None, EXPERT), P(None, EXPERT), weight, weight, weight, weight, P(), P())

    def step(*args):
        return shards(sizes, *args)

    return jax.shard_map(
        step,
        mesh=mesh,
        in_specs=in_specs,
        out_specs=(weight,) * 5,
        check_vma=False,
    )


def solution(mesh):
    sizes = (2, 4, 8)
    step = build(mesh.devices, sizes)
    return step
```

time: 431 us -> 437 us (1.014)
  starting transfers between devices: 96.1 us -> 114 us
  waiting for transfers between devices: 233 us -> 247 us
  local copies, waits for them, and re-layouts: 21.6 us -> 8.72 us
  other arithmetic: 18.8 us -> 10.5 us
  Pallas kernels: 44.8 us -> 38.8 us
    reduce_scatter x1, waiting for transfers between devices: 42.3 us -> 85.7 us  [shards(): lax.psum_scatter(keep.reshape(-1, feats), 'z', scatter_dimension=0, tiled...]
    ppermute x14, waiting for transfers between devices: 128 us -> 99.3 us  [moved(): done.append(lax.ppermute(piece, ('xl', 'y'), pairs_list))]
    all_to_all x3 -> x4, starting transfers between devices: 32.5 us -> 48.1 us  [to_homes(): lax.all_to_all(blocks, HOMES, split_axis=0, concat_axis=0, tiled=True)]
    broadcast_in_dim x4 -> x1, local copies, waits for them, and re-layouts: 7.65 us -> 0.67 us  [shards(): jnp.broadcast_to(limit[:, :, None].astype(jnp.float32), divides.shape)]
    convert_element_type x7 -> x2, other arithmetic: 7.01 us -> 0.8 us  [the longest x1 0.79 us: shards(): divides = (apart % copies[:, :, None] == 0).astype(jnp.float32)]
    pallas_call x4 -> x5, Pallas kernels: 44.8 us -> 38.8 us  [the longest x1 14 us: shards(): call(functools.partial(expert_kernel, offsets), 8, [spec((1, blocks, 2, 2...]
    all_to_all x3 -> x4, waiting for transfers between devices: 30.2 us -> 30.2 us  [to_homes(): lax.all_to_all(blocks, HOMES, split_axis=0, concat_axis=0, tiled=True)]
  transfers between devices with their start and end apart: 23 -> 24, of which waited for: 11 -> 11; matrix products, arithmetic and copies ran while one was open for 8% -> 3% of each run, Pallas kernels for 4% -> 4%
where the time goes in v3:
time: 437 us; the launch traced here: 435 us
  waiting for transfers between devices  247 us (57%)
  starting transfers between devices  114 us (26%)
  Pallas kernels  38.8 us (9%)
  between operations  14.4 us (3%)
  other arithmetic  10.5 us (2%)
  local copies, waits for them, and re-layouts  8.72 us (2%)
    ppermute x14, waiting for transfers between devices, moved(): done.append(lax.ppermute(piece, ('xl', 'y'), pairs_list))  99.3 us
    reduce_scatter x1, waiting for transfers between devices, shards(): lax.psum_scatter(keep.reshape(-1, feats), 'z', scatter_dimension=0, tiled...  85.7 us
    ppermute x14, starting transfers between devices, moved(): done.append(lax.ppermute(piece, ('xl', 'y'), pairs_list))  61.8 us
    all_to_all x4, starting transfers between devices, to_homes(): lax.all_to_all(blocks, HOMES, split_axis=0, concat_axis=0, tiled=True)  48.1 us
    all_to_all x4, waiting for transfers between devices, to_homes(): lax.all_to_all(blocks, HOMES, split_axis=0, concat_axis=0, tiled=True)  30.2 us
    all_gather x1, waiting for transfers between devices, shards(): line = lax.all_gather(jnp.concatenate([own, across, meta]), 'z', axis=0)  17.5 us
    pallas_call x1, Pallas kernels, shards(): call(functools.partial(expert_kernel, offsets), 8, [spec((1, blocks, 2, 2...  14 us
    pallas_call x2, Pallas kernels, gradient(): call(functools.partial(gradient_kernel, offsets), 4, [spec((members, rows...  12.7 us
  transfers between devices with their start and end apart: 24, of which 11 were waited for; matrix products, arithmetic and copies ran while one was open for 3% of the time, Pallas kernels for 4%

profile of v3, /device:TPU:6, one launch (start us, length us, event | category | flops | bytes accessed | tf_op | source)
XLA Modules:
  0.0 435.1 jit_solution(4997746420396315954)
XLA Ops:
  7.2 14.4 %all-to-all-start.1 = ((bf16[128,16,384]{2,1,0:T(8,128)(2,1)}), bf16[128,16,384]{2,1,0:T(8,128)(2,1)S(1)}, u32[]{:S(2)}, u32[]{:S(2)}) async-start(bf16[128,16,384]{2,1,0:T(8,128)(2,1)} %param.15), calls=%async_computation.1 | async-start | bytes 3145728 | tf_op jit(solution)/shard_map/all_to_all | solution.py:230
  23.7 7.8 %collective-permute-done = bf16[128,512]{1,0:T(8,128)(2,1)S(1)} collective-permute-done((bf16[128,512]{1,0:T(8,128)(2,1)S(1)}, bf16[128,512]{1,0:T(8,128)(2,1)S(1)}, u32[]{:S(2)}, u32[]{:S(2)}) %collective-permute-start) | collective-permute-done | bytes 131104 | tf_op jit(solution)/shard_map/ppermute | solution.py:251
  32.3 3.4 pad_maximum_fusion
  35.8 30.2 %all-to-all-done.1 = bf16[128,16,384]{2,1,0:T(8,128)(2,1)S(1)} async-done(((bf16[128,16,384]{2,1,0:T(8,128)(2,1)}), bf16[128,16,384]{2,1,0:T(8,128)(2,1)S(1)}, u32[]{:S(2)}, u32[]{:S(2)}) %all-to-all-start.1) | async-done | bytes 1572896 | tf_op jit(solution)/shard_map/all_to_all | solution.py:230
  67.1 8.7 %all-to-all-start = ((bf16[128,2,16,384]{3,2,1,0:T(8,128)(2,1)}), bf16[128,2,16,384]{3,2,1,0:T(8,128)(2,1)S(1)}, u32[]{:S(2)}, u32[]{:S(2)}) async-start(bf16[128,2,16,384]{3,2,1,0:T(8,128)(2,1)} %pad_maximum_fusion), calls=%async_computation | async-start | bytes 6291456 | tf_op jit(solution)/shard_map/all_to_all | solution.py:230
  75.8 17.5 %all-gather.3.cloned.1.call-done = bf16[2304,512]{1,0:T(8,128)(2,1)} async-done(((bf16[288,512]{1,0:T(8,128)(2,1)}), bf16[2304,512]{1,0:T(8,128)(2,1)}) %all-gather.3.cloned.1.call-update) | async-done | bytes 2359312 | tf_op jit(solution)/shard_map/all_gather | solution.py:254
  94.7 3.6 collective-permute-done.1.other_ref
  98.9 6.2 %shard_map.128 = (bf16[2,256,256]{2,1,0:T(8,128)(2,1)}, bf16[2,256,256]{2,1,0:T(8,128)(2,1)}, bf16[2,256,256]{2,1,0:T(8,128)(2,1)}, bf16[2,2,2,64,512]{4,3,2,1,0...) custom-call(s32[8]{0:T(128)} %copy-done.17, ...), custom_call_target="tpu_custom_call" | custom-call | tf_op jit(solution)/shard_map/pallas_call | solution.py:279
  113.3 15.5 %collective-permute-done.2.refs_1_ = bf16[2,2,2,64,512]{4,3,2,1,0:T(8,128)(2,1)} collective-permute-done((bf16[2,2,2,64,512]{4,3,2,1,0:T(8,128)(2,1)}, bf16[2,2,2,64,512]{4,3,2,1,0:T(8,128)(2,1)}, u32[]{:S(2)}, u32[]{:S(2)}) %collective-permute-start.2) | collective-permute-done | bytes 524320 | tf_op jit(solution)/shard_map/ppermute | solution.py:298
  128.8 4.1 collective-permute-start.7
  132.9 41.2 %collective-permute-done.3.refs_2_ = bf16[2,2,2,64,512]{4,3,2,1,0:T(8,128)(2,1)} collective-permute-done((bf16[2,2,2,64,512]{4,3,2,1,0:T(8,128)(2,1)}, bf16[2,2,2,64,512]{4,3,2,1,0:T(8,128)(2,1)}, u32[]{:S(2)}, u32[]{:S(2)}) %collective-permute-start.3) | collective-permute-done | bytes 524320 | tf_op jit(solution)/shard_map/ppermute | solution.py:298
  174.6 13.9 %collective-permute-done.8.refs_7_ = bf16[2,2,2,64,512]{4,3,2,1,0:T(8,128)(2,1)} collective-permute-done((bf16[2,2,2,64,512]{4,3,2,1,0:T(8,128)(2,1)}, bf16[2,2,2,64,512]{4,3,2,1,0:T(8,128)(2,1)}, u32[]{:S(2)}, u32[]{:S(2)}) %collective-permute-start.8) | collective-permute-done | bytes 524320 | tf_op jit(solution)/shard_map/ppermute | solution.py:298
  188.5 14.0 %shard_map.129 = (bf16[3,512,384]{2,1,0:T(8,128)(2,1)}, bf16[2,2,2,64,512]{4,3,2,1,0:T(8,128)(2,1)}, bf16[2,2,2,64,512]{4,3,2,1,0:T(8,128)(2,1)}, bf16[2,2,2,64,...) custom-call(s32[4]{0:T(128)} %fusion.27.quarter_ref.expert_ref, ...), custom_call_target="tpu_custom_call" | custom-call | tf_op jit(solution)/shard_map/pallas_call | solution.py:317
  202.5 5.7 %shard_map.132 = bf16[4,16,2,1,16,384]{5,4,3,2,1,0:T(8,128)(2,1)} custom-call(s32[4]{0:T(128)} %fusion.27.quarter_ref.expert_ref, bf16[3,512,384]{2,1,0:T(8,128)(2,1)} %get-tuple-element.48.act_ref, bf16[2,2,2,64,512]{4,3,2,1,0:T(8,128)(2,1)} %get-tuple-element.30.refs_0_, bf16[2,2,2,64,512]{4,3,2,1,0:T(8,128)(2,1)} %collective-permute-done.2.refs_1_, ...), custom_call_target="tpu_custom_call" | custom-call | tf_op jit(solution)/shard_map/pallas_call | solution.py:340
  208.2 13.1 %all-to-all-start.3 = ((bf16[128,16,384]{2,1,0:T(8,128)(2,1)}), bf16[128,16,384]{2,1,0:T(8,128)(2,1)S(1)}, u32[]{:S(2)}, u32[]{:S(2)}) async-start(bf16[128,16,384]{2,1,0:T(8,128)(2,1)} %bitcast.51), calls=%async_computation.4 | async-start | bytes 3145728 | tf_op jit(solution)/shard_map/all_to_all | solution.py:230
  226.2 3.6 collective-permute-start.13
  229.8 16.2 %collective-permute-done.9.refs_1_ = bf16[2,2,2,64,512]{4,3,2,1,0:T(8,128)(2,1)S(1)} collective-permute-done((bf16[2,2,2,64,512]{4,3,2,1,0:T(8,128)(2,1)}, bf16[2,2,2,64,512]{4,3,2,1,0:T(8,128)(2,1)S(1)}, u32[]{:S(2)}, u32[]{:S(2)}) %collective-permute-start.9) | collective-permute-done | bytes 524320 | tf_op jit(solution)/shard_map/ppermute | solution.py:298
  248.7 38.4 %collective-permute-start.15 = (bf16[2,2,2,64,512]{4,3,2,1,0:T(8,128)(2,1)}, bf16[2,2,2,64,512]{4,3,2,1,0:T(8,128)(2,1)S(1)}, u32[]{:S(2)}, u32[]{:S(2)}) collective-permute-start(bf16[2,2,2,64,512]{4,3,2,1,0:T(8,128)(2,1)} %get-tuple-element.45), channel_id=1, source_target_pairs={{0,40},{8,48},{16,56},{24,32},{32,8},{40,16},{48,24},{56,0},{1,41}... | collective-permute-start | bytes 1572872 | tf_op jit(solution)/shard_map/ppermute | solution.py:298
  287.1 12.5 %collective-permute-done.15.refs_7_ = bf16[2,2,2,64,512]{4,3,2,1,0:T(8,128)(2,1)S(1)} collective-permute-done((bf16[2,2,2,64,512]{4,3,2,1,0:T(8,128)(2,1)}, bf16[2,2,2,64,512]{4,3,2,1,0:T(8,128)(2,1)S(1)}, u32[]{:S(2)}, u32[]{:S(2)}) %collective-permute-start.15) | collective-permute-done | bytes 524320 | tf_op jit(solution)/shard_map/ppermute | solution.py:298
  300.5 5.9 %shard_map.130 = (bf16[8,2,2,2,32,512]{5,4,3,2,1,0:T(8,128)(2,1)}, bf16[8,2,2,2,32,512]{5,4,3,2,1,0:T(8,128)(2,1)}) custom-call(s32[4]{0:T(128)} %fusion.27.quarter_ref.expert_ref, bf16[2,256,256]{2,1,0:T(8,128)(2,1)} %get-tuple-element.27.pick_ref, bf16[2,256,256]{2,1,0:T(8,128)(2,1)} %get-tuple-element.28.high_ref, ...), custom_call_target="tpu_custom_call" | custom-call | tf_op jit(solution)/shard_map/pallas_call | solution.py:353
  306.7 7.0 %shard_map.131 = bf16[4,16,2,2,16,384]{5,4,3,2,1,0:T(8,128)(2,1)} custom-call(s32[4]{0:T(128)} %fusion.27.quarter_ref.expert_ref, bf16[3,512,384]{2,1,0:T(8,128)(2,1)} %get-tuple-element.48.act_ref, bf16[2,2,2,64,512]{4,3,2,1,0:T(8,128)(2,1)} %get-tuple-element.30.refs_0_, bf16[2,2,2,64,512]{4,3,2,1,0:T(8,128)(2,1)} %collective-permute-done.2.refs_1_, ...), custom_call_target="tpu_custom_call" | custom-call | tf_op jit(solution)/shard_map/pallas_call | solution.py:340
  314.8 11.9 %all-to-all-start.2 = ((bf16[128,2,16,384]{3,2,1,0:T(8,128)(2,1)}), bf16[128,2,16,384]{3,2,1,0:T(8,128)(2,1)S(1)}, u32[]{:S(2)}, u32[]{:S(2)}) async-start(bf16[128,2,16,384]{3,2,1,0:T(8,128)(2,1)} %bitcast.45), calls=%async_computation.3 | async-start | bytes 6291456 | tf_op jit(solution)/shard_map/all_to_all | solution.py:230
  326.8 4.6 %add_convert_fusion = bf16[8,2,2,2,32,512]{5,4,3,2,1,0:T(8,128)(2,1)} fusion(bf16[8,2,2,2,32,512]{5,4,3,2,1,0:T(8,128)(2,1)} %collective-permute-done.16, bf16[8,2,2,2,32,512]{5,4,3,2,1,0:T(8,128)(2,1)} %get-tuple-element.46), kind=kLoop, calls=%fused_computation | loop fusion | flops 4194304 | bytes 6291456 | tf_op jit(solution)/shard_map/convert_element_type | solution.py:361
  331.4 85.7 %reduce-scatter.2.cloned.1.call-done = bf16[256,512]{1,0:T(8,128)(2,1)} async-done(((bf16[2048,512]{1,0:T(8,128)(2,1)}), bf16[256,512]{1,0:T(8,128)(2,1)}) %reduce-scatter.2.cloned.1.call-update) | async-done | bytes 262160 | tf_op jit(solution)/shard_map/reduce_scatter | solution.py:362
  (100 shorter events, 35.7 us)
Async XLA Ops:
  7.2 58.7 %all-to-all-start.1 = ((bf16[128,16,384]{2,1,0:T(8,128)(2,1)}), bf16[128,16,384]{2,1,0:T(8,128)(2,1)S(1)}, u32[]{:S(2)}, u32[]{:S(2)}) async-start(bf16[128,16,384]{2,1,0:T(8,128)(2,1)} %param.15), calls=%async_computation.1 | async-start | bytes 3145728 | tf_op jit(solution)/shard_map/all_to_all | solution.py:230
  21.6 71.7 %all-gather.3.cloned.1.call-start = ((), (), s32[]{:S(2)}) async-start(), calls=%async_computation.6 | async-start | bytes 2654208 | tf_op jit(solution)/shard_map/all_gather | solution.py:254
  22.0 9.5 %collective-permute-start = (bf16[128,512]{1,0:T(8,128)(2,1)S(1)}, bf16[128,512]{1,0:T(8,128)(2,1)S(1)}, u32[]{:S(2)}, u32[]{:S(2)}) collective-permute-start(bf16[128,512]{1,0:T(8,128)(2,1)S(1)} %convolution_convert_fusion.1), channel_id=1, source_target_pairs={{0,128},{128,0},{1,129},{129,1},{2,130},{130,2},{3,131},{131,3},{4... | collective-permute-start | bytes 393224 | tf_op jit(solution)/shard_map/ppermute | solution.py:251
  67.1 107.5 %all-to-all-start = ((bf16[128,2,16,384]{3,2,1,0:T(8,128)(2,1)}), bf16[128,2,16,384]{3,2,1,0:T(8,128)(2,1)S(1)}, u32[]{:S(2)}, u32[]{:S(2)}) async-start(bf16[128,2,16,384]{3,2,1,0:T(8,128)(2,1)} %pad_maximum_fusion), calls=%async_computation | async-start | bytes 6291456 | tf_op jit(solution)/shard_map/all_to_all | solution.py:230
  93.3 4.9 %collective-permute-start.1 = (bf16[8,288,512]{2,1,0:T(8,128)(2,1)}, bf16[8,288,512]{2,1,0:T(8,128)(2,1)}, u32[]{:S(2)}, u32[]{:S(2)}) collective-permute-start(bf16[8,288,512]{2,1,0:T(8,128)(2,1)} %bitcast.46), channel_id=1, source_target_pairs={{0,64},{64,0},{1,65},{65,1},{2,66},{66,2},{3,67},{67,3},{4,68},{68... | collective-permute-start | bytes 7077896 | tf_op jit(solution)/shard_map/ppermute | solution.py:255
  105.1 23.7 %collective-permute-start.2 = (bf16[2,2,2,64,512]{4,3,2,1,0:T(8,128)(2,1)}, bf16[2,2,2,64,512]{4,3,2,1,0:T(8,128)(2,1)}, u32[]{:S(2)}, u32[]{:S(2)}) collective-permute-start(bf16[2,2,2,64,512]{4,3,2,1,0:T(8,128)(2,1)} %get-tuple-element.31), channel_id=1, source_target_pairs={{0,8},{8,16},{16,24},{24,0},{32,40},{40,48},{48,56},{56,32},{1,9},... | collective-permute-start | bytes 1572872 | tf_op jit(solution)/shard_map/ppermute | solution.py:298
  107.0 67.1 %collective-permute-start.3 = (bf16[2,2,2,64,512]{4,3,2,1,0:T(8,128)(2,1)}, bf16[2,2,2,64,512]{4,3,2,1,0:T(8,128)(2,1)}, u32[]{:S(2)}, u32[]{:S(2)}) collective-permute-start(bf16[2,2,2,64,512]{4,3,2,1,0:T(8,128)(2,1)} %get-tuple-element.32), channel_id=1, source_target_pairs={{0,16},{8,24},{16,0},{24,8},{32,48},{40,56},{48,32},{56,40},{1,17}... | collective-permute-start | bytes 1572872 | tf_op jit(solution)/shard_map/ppermute | solution.py:298
  109.8 64.8 %collective-permute-start.4 = (bf16[2,2,2,64,512]{4,3,2,1,0:T(8,128)(2,1)}, bf16[2,2,2,64,512]{4,3,2,1,0:T(8,128)(2,1)}, u32[]{:S(2)}, u32[]{:S(2)}) collective-permute-start(bf16[2,2,2,64,512]{4,3,2,1,0:T(8,128)(2,1)} %get-tuple-element.33), channel_id=1, source_target_pairs={{0,24},{8,0},{16,8},{24,16},{32,56},{40,32},{48,40},{56,48},{1,25}... | collective-permute-start | bytes 1572872 | tf_op jit(solution)/shard_map/ppermute | solution.py:298
  111.2 63.4 %collective-permute-start.5 = (bf16[2,2,2,64,512]{4,3,2,1,0:T(8,128)(2,1)}, bf16[2,2,2,64,512]{4,3,2,1,0:T(8,128)(2,1)}, u32[]{:S(2)}, u32[]{:S(2)}) collective-permute-start(bf16[2,2,2,64,512]{4,3,2,1,0:T(8,128)(2,1)} %get-tuple-element.34), channel_id=1, source_target_pairs={{0,32},{8,40},{16,48},{24,56},{32,0},{40,8},{48,16},{56,24},{1,33}... | collective-permute-start | bytes 1572872 | tf_op jit(solution)/shard_map/ppermute | solution.py:298
  111.2 63.4 %collective-permute-start.6 = (bf16[2,2,2,64,512]{4,3,2,1,0:T(8,128)(2,1)}, bf16[2,2,2,64,512]{4,3,2,1,0:T(8,128)(2,1)}, u32[]{:S(2)}, u32[]{:S(2)}) collective-permute-start(bf16[2,2,2,64,512]{4,3,2,1,0:T(8,128)(2,1)} %get-tuple-element.35), channel_id=1, source_target_pairs={{0,40},{8,48},{16,56},{24,32},{32,8},{40,16},{48,24},{56,0},{1,41}... | collective-permute-start | bytes 1572872 | tf_op jit(solution)/shard_map/ppermute | solution.py:298
  128.8 45.8 %collective-permute-start.7 = (bf16[2,2,2,64,512]{4,3,2,1,0:T(8,128)(2,1)}, bf16[2,2,2,64,512]{4,3,2,1,0:T(8,128)(2,1)}, u32[]{:S(2)}, u32[]{:S(2)}) collective-permute-start(bf16[2,2,2,64,512]{4,3,2,1,0:T(8,128)(2,1)} %get-tuple-element.36), channel_id=1, source_target_pairs={{0,48},{8,56},{16,32},{24,40},{32,16},{40,24},{48,0},{56,8},{1,49}... | collective-permute-start | bytes 1572872 | tf_op jit(solution)/shard_map/ppermute | solution.py:298
  174.1 14.5 %collective-permute-start.8 = (bf16[2,2,2,64,512]{4,3,2,1,0:T(8,128)(2,1)}, bf16[2,2,2,64,512]{4,3,2,1,0:T(8,128)(2,1)}, u32[]{:S(2)}, u32[]{:S(2)}) collective-permute-start(bf16[2,2,2,64,512]{4,3,2,1,0:T(8,128)(2,1)} %get-tuple-element.37), channel_id=1, source_target_pairs={{0,56},{8,32},{16,40},{24,48},{32,24},{40,0},{48,8},{56,16},{1,57}... | collective-permute-start | bytes 1572872 | tf_op jit(solution)/shard_map/ppermute | solution.py:298
  208.2 105.4 %all-to-all-start.3 = ((bf16[128,16,384]{2,1,0:T(8,128)(2,1)}), bf16[128,16,384]{2,1,0:T(8,128)(2,1)S(1)}, u32[]{:S(2)}, u32[]{:S(2)}) async-start(bf16[128,16,384]{2,1,0:T(8,128)(2,1)} %bitcast.51), calls=%async_computation.4 | async-start | bytes 3145728 | tf_op jit(solution)/shard_map/all_to_all | solution.py:230
  221.4 24.6 %collective-permute-start.9 = (bf16[2,2,2,64,512]{4,3,2,1,0:T(8,128)(2,1)}, bf16[2,2,2,64,512]{4,3,2,1,0:T(8,128)(2,1)S(1)}, u32[]{:S(2)}, u32[]{:S(2)}) collective-permute-start(bf16[2,2,2,64,512]{4,3,2,1,0:T(8,128)(2,1)} %get-tuple-element.39), channel_id=1, source_target_pairs={{0,24},{8,0},{16,8},{24,16},{32,56},{40,32},{48,40},{56,48},{1,25}... | collective-permute-start | bytes 1572872 | tf_op jit(solution)/shard_map/ppermute | solution.py:298
  224.5 24.2 %collective-permute-start.10 = (bf16[2,2,2,64,512]{4,3,2,1,0:T(8,128)(2,1)}, bf16[2,2,2,64,512]{4,3,2,1,0:T(8,128)(2,1)S(1)}, u32[]{:S(2)}, u32[]{:S(2)}) collective-permute-start(bf16[2,2,2,64,512]{4,3,2,1,0:T(8,128)(2,1)} %get-tuple-element.40), channel_id=1, source_target_pairs={{0,16},{8,24},{16,0},{24,8},{32,48},{40,56},{48,32},{56,40},{1,17}... | collective-permute-start | bytes 1572872 | tf_op jit(solution)/shard_map/ppermute | solution.py:298
  225.1 62.0 %collective-permute-start.11 = (bf16[2,2,2,64,512]{4,3,2,1,0:T(8,128)(2,1)}, bf16[2,2,2,64,512]{4,3,2,1,0:T(8,128)(2,1)S(1)}, u32[]{:S(2)}, u32[]{:S(2)}) collective-permute-start(bf16[2,2,2,64,512]{4,3,2,1,0:T(8,128)(2,1)} %get-tuple-element.41), channel_id=1, source_target_pairs={{0,8},{8,16},{16,24},{24,0},{32,40},{40,48},{48,56},{56,32},{1,9},... | collective-permute-start | bytes 1572872 | tf_op jit(solution)/shard_map/ppermute | solution.py:298
  226.1 61.0 %collective-permute-start.12 = (bf16[2,2,2,64,512]{4,3,2,1,0:T(8,128)(2,1)}, bf16[2,2,2,64,512]{4,3,2,1,0:T(8,128)(2,1)S(1)}, u32[]{:S(2)}, u32[]{:S(2)}) collective-permute-start(bf16[2,2,2,64,512]{4,3,2,1,0:T(8,128)(2,1)} %get-tuple-element.42), channel_id=1, source_target_pairs={{0,32},{8,40},{16,48},{24,56},{32,0},{40,8},{48,16},{56,24},{1,33}... | collective-permute-start | bytes 1572872 | tf_op jit(solution)/shard_map/ppermute | solution.py:298
  226.2 60.9 %collective-permute-start.13 = (bf16[2,2,2,64,512]{4,3,2,1,0:T(8,128)(2,1)}, bf16[2,2,2,64,512]{4,3,2,1,0:T(8,128)(2,1)S(1)}, u32[]{:S(2)}, u32[]{:S(2)}) collective-permute-start(bf16[2,2,2,64,512]{4,3,2,1,0:T(8,128)(2,1)} %get-tuple-element.43), channel_id=1, source_target_pairs={{0,56},{8,32},{16,40},{24,48},{32,24},{40,0},{48,8},{56,16},{1,57}... | collective-permute-start | bytes 1572872 | tf_op jit(solution)/shard_map/ppermute | solution.py:298
  246.0 41.1 %collective-permute-start.14 = (bf16[2,2,2,64,512]{4,3,2,1,0:T(8,128)(2,1)}, bf16[2,2,2,64,512]{4,3,2,1,0:T(8,128)(2,1)S(1)}, u32[]{:S(2)}, u32[]{:S(2)}) collective-permute-start(bf16[2,2,2,64,512]{4,3,2,1,0:T(8,128)(2,1)} %get-tuple-element.44), channel_id=1, source_target_pairs={{0,48},{8,56},{16,32},{24,40},{32,16},{40,24},{48,0},{56,8},{1,49}... | collective-permute-start | bytes 1572872 | tf_op jit(solution)/shard_map/ppermute | solution.py:298
  248.7 51.0 %collective-permute-start.15 = (bf16[2,2,2,64,512]{4,3,2,1,0:T(8,128)(2,1)}, bf16[2,2,2,64,512]{4,3,2,1,0:T(8,128)(2,1)S(1)}, u32[]{:S(2)}, u32[]{:S(2)}) collective-permute-start(bf16[2,2,2,64,512]{4,3,2,1,0:T(8,128)(2,1)} %get-tuple-element.45), channel_id=1, source_target_pairs={{0,40},{8,48},{16,56},{24,32},{32,8},{40,16},{48,24},{56,0},{1,41}... | collective-permute-start | bytes 1572872 | tf_op jit(solution)/shard_map/ppermute | solution.py:298
  306.4 20.4 %collective-permute-start.16 = (bf16[8,2,2,2,32,512]{5,4,3,2,1,0:T(8,128)(2,1)}, bf16[8,2,2,2,32,512]{5,4,3,2,1,0:T(8,128)(2,1)}, u32[]{:S(2)}, u32[]{:S(2)}) collective-permute-start(bf16[8,2,2,2,32,512]{5,4,3,2,1,0:T(8,128)(2,1)} %get-tuple-element.47), channel_id=1, source_target_pairs={{0,64},{64,0},{1,65},{65,1},{2,66},{66,2},{3,67},{67,3},{4,68},{68... | collective-permute-start | bytes 6291464 | tf_op jit(solution)/shard_map/ppermute | solution.py:360
  314.8 105.2 %all-to-all-start.2 = ((bf16[128,2,16,384]{3,2,1,0:T(8,128)(2,1)}), bf16[128,2,16,384]{3,2,1,0:T(8,128)(2,1)S(1)}, u32[]{:S(2)}, u32[]{:S(2)}) async-start(bf16[128,2,16,384]{3,2,1,0:T(8,128)(2,1)} %bitcast.45), calls=%async_computation.3 | async-start | bytes 6291456 | tf_op jit(solution)/shard_map/all_to_all | solution.py:230
  326.8 90.3 %reduce-scatter.2.cloned.1.call-start = ((), (), s32[]{:S(2)}) async-start(), calls=%async_computation.5 | async-start | bytes 2359296 | tf_op jit(solution)/shard_map/reduce_scatter | solution.py:362
  418.0 7.2 %collective-permute-start.17 = (bf16[128,512]{1,0:T(8,128)(2,1)S(1)}, bf16[128,512]{1,0:T(8,128)(2,1)}, u32[]{:S(2)}, u32[]{:S(2)}) collective-permute-start(bf16[128,512]{1,0:T(8,128)(2,1)S(1)} %slice.44), channel_id=1, source_target_pairs={{0,128},{128,0},{1,129},{129,1},{2,130},{130,2},{3,131},{131,3},{4... | collective-permute-start | bytes 393224 | tf_op jit(solution)/shard_map/ppermute | solution.py:364
  (20 other events, 394.3 us)
Sparse Core Ops, SparseCore 0:
  32.4 60.8 all-gather.2
  331.5 85.5 reduce-scatter.1

commit v4 on v3

--- a/solution.py
+++ b/solution.py
@@ -121,19 +121,22 @@
 
 
 def combine_kernel(offsets, expert_ref, pick_ref, high_ref, low_ref, *refs):
-    row_refs, (keep_ref, send_ref) = refs[:offsets], refs[offsets:]
+    row_refs, refs = refs[:offsets], refs[offsets:]
+    target, added = refs[-1], refs[:-1]
     micro = pick_ref.shape[0]
     rows = pick_ref.shape[1] // offsets
-    shape = (keep_ref.shape[0],) + keep_ref.shape[4:]
+    shape = (target.shape[0],) + target.shape[4:]
     for m in range(micro):
         at = slice(m * rows, (m + 1) * rows)
-        for rc, target in enumerate((keep_ref, send_ref)):
-            out = jnp.concatenate([r[rc, 0, 0, at] for r in row_refs], axis=0)
-            back = jnp.concatenate([r[rc, 0, 1, at] for r in row_refs], axis=0)
-            value = dot(high_ref[m], out, 0, 0) + dot(low_ref[m], out, 0, 0)
-            grad = dot(pick_ref[m], back, 0, 0)
-            target[:, 0, 0, m] = value.astype(target.dtype).reshape(shape)
-            target[:, 0, 1, m] = grad.astype(target.dtype).reshape(shape)
+        out = jnp.concatenate([r[0, 0, 0, at] for r in row_refs], axis=0)
+        back = jnp.concatenate([r[0, 0, 1, at] for r in row_refs], axis=0)
+        value = (dot(high_ref[m], out, 0, 0) + dot(low_ref[m], out, 0, 0)).reshape(shape)
+        grad = dot(pick_ref[m], back, 0, 0).reshape(shape)
+        for ref in added:
+            value += ref[:, 0, 0, m].astype(jnp.float32)
+            grad += ref[:, 0, 1, m].astype(jnp.float32)
+        target[:, 0, 0, m] = value.astype(target.dtype)
+        target[:, 0, 1, m] = grad.astype(target.dtype)
 
 
 def swap_halves(lower, upper):
@@ -144,11 +147,11 @@
     return first, second
 
 
-def expert_kernel(offsets, quarter_ref, fused_ref, down_ref, *refs):
+def expert_kernel(offsets, quarter_ref, weight_ref, *refs):
     row_refs, refs = refs[:offsets], refs[offsets:]
-    act_ref, refs = refs[0], refs[1:]
-    out_refs, (w_scr, pre_scr) = refs[:offsets], refs[offsets:]
-    _, blocks, _, pairs, width = down_ref.shape
+    grad_ref, refs = refs[0], refs[1:]
+    out_refs, (w_scr, row_scr, pre_scr, act_scr) = refs[:offsets], refs[offsets:]
+    _, blocks, _, _, pairs, width = weight_ref.shape
     depth = blocks * pairs
     rows = row_refs[0].shape[3]
     step = pl.program_id(0)
@@ -161,13 +164,12 @@
     def _():
         x = jnp.concatenate([r[0, 0, 0] for r in row_refs], axis=0)
         g = jnp.concatenate([r[0, 0, 1] for r in row_refs], axis=0)
+        row_scr[step, 0] = x
+        row_scr[step, 1] = g
         for k in range(3):
-            if k < 2:
-                lower, upper = fused_ref[0, :, 0, k], fused_ref[0, :, 1, k]
-            else:
-                lower, upper = down_ref[0, :, 0], down_ref[0, :, 1]
-            even, odd = swap_halves(lower.reshape(depth, width), upper.reshape(depth, width))
-            both = jnp.concatenate([even, odd], axis=0)
+            lower = weight_ref[0, :, 0, k].reshape(depth, width)
+            upper = weight_ref[0, :, 1, k].reshape(depth, width)
+            both = jnp.concatenate(swap_halves(lower, upper), axis=0)
             w_scr[k, step] = both
             pre_scr[k] += dot(g if k == 2 else x, both, 1, 0)
 
@@ -176,33 +178,26 @@
         gate, up, hidden_grad = pre_scr[0], pre_scr[1], pre_scr[2]
         logistic = jax.nn.sigmoid(gate)
         swished = gate * logistic
-        act_ref[2] = (swished * up).astype(jnp.bfloat16)
-        act_ref[0] = (hidden_grad * up * logistic * (1.0 + gate * (1.0 - logistic))).astype(
+        act_scr[2] = (swished * up).astype(jnp.bfloat16)
+        act_scr[0] = (hidden_grad * up * logistic * (1.0 + gate * (1.0 - logistic))).astype(
             jnp.bfloat16
         )
-        act_ref[1] = (hidden_grad * swished).astype(jnp.bfloat16)
+        act_scr[1] = (hidden_grad * swished).astype(jnp.bfloat16)
 
     @pl.when(step >= 4)
     def _():
         blk = step - 4
-        out = dot(act_ref[2], w_scr[2, blk], 1, 1).astype(jnp.bfloat16)
-        back = dot(act_ref[0], w_scr[0, blk], 1, 1)
-        back = (back + dot(act_ref[1], w_scr[1, blk], 1, 1)).astype(jnp.bfloat16)
+        for k in range(3):
+            total = dot(row_scr[blk, k // 2], act_scr[k], 0, 0).astype(jnp.bfloat16)
+            lower, upper = swap_halves(total[:depth], total[depth:])
+            grad_ref[0, :, 0, k] = lower.reshape(blocks, pairs, width)
+            grad_ref[0, :, 1, k] = upper.reshape(blocks, pairs, width)
+        out = dot(act_scr[2], w_scr[2, blk], 1, 1).astype(jnp.bfloat16)
+        back = dot(act_scr[0], w_scr[0, blk], 1, 1)
+        back = (back + dot(act_scr[1], w_scr[1, blk], 1, 1)).astype(jnp.bfloat16)
         for o in range(offsets):
             out_refs[o][0, 0, 0] = out[o * rows : (o + 1) * rows]
             out_refs[o][0, 0, 1] = back[o * rows : (o + 1) * rows]
-
-
-def gradient_kernel(offsets, quarter_ref, act_ref, *refs):
-    row_refs, grad_ref = refs[:offsets], refs[offsets]
-    _, blocks, _, members, pairs, width = grad_ref.shape
-    depth = blocks * pairs
-    source = jnp.concatenate([r[0, 0, 0] for r in row_refs], axis=0)
-    for k in range(members):
-        total = dot(source, act_ref[k], 0, 0).astype(jnp.bfloat16)
-        lower, upper = swap_halves(total[:depth], total[depth:])
-        grad_ref[0, :, 0, k] = lower.reshape(blocks, pairs, width)
-        grad_ref[0, :, 1, k] = upper.reshape(blocks, pairs, width)
 
 
 def shards(
@@ -249,9 +244,9 @@
     )
     meta = jnp.pad(meta, ((0, META_ROWS - 2 * routes), (0, feats - 2 * columns)))
     across = lax.ppermute(own, "xh", swap)
-    down = to_homes(down_proj)
-    fused = to_homes(jnp.stack([gate_proj, up_proj], axis=1))
+    weights = jnp.stack([gate_proj, up_proj, down_proj], axis=1)
     line = lax.all_gather(jnp.concatenate([own, across, meta]), "z", axis=0)
+    weights = to_homes(weights)
     line_other = lax.ppermute(line, "c", swap)
     line_shape = (nz, 2, 2, micro, tokens, feats)
 
@@ -304,7 +299,6 @@
     rows_all = offsets * chunk_rows
     blocks = expert_count // 8
     view = (4, blocks, 2)
-    act = jax.ShapeDtypeStruct((3, rows_all, width), jnp.bfloat16)
 
     def early(i, *refs):
         i = jnp.minimum(i, 3)
@@ -314,57 +308,44 @@
         i = jnp.maximum(i - 4, 0)
         return (i // 2, i % 2)
 
+    stored = view + (3, pairs, width)
     results = call(
         functools.partial(expert_kernel, offsets),
         8,
-        [
-            spec((1, blocks, 2, 2, pairs, width), lambda i, q: (q[jnp.minimum(i, 3)],)),
-            spec((1, blocks, 2, pairs, width), lambda i, q: (q[jnp.minimum(i, 3)],)),
-        ]
+        [spec((1,) + stored[1:], lambda i, q: (q[jnp.minimum(i, 3)],))]
         + [spec((1, 1, 2, chunk_rows, feats), early)] * offsets,
-        [spec(act.shape)] + [spec((1, 1, 2, chunk_rows, feats), late)] * offsets,
-        [act] + [chunk] * offsets,
+        [spec((1,) + stored[1:], lambda i, q: (q[jnp.maximum(i - 4, 0)],))]
+        + [spec((1, 1, 2, chunk_rows, feats), late)] * offsets,
+        [jax.ShapeDtypeStruct(stored, jnp.bfloat16)] + [chunk] * offsets,
         scratch=(
             pltpu.VMEM((3, 4, feats, width), jnp.bfloat16),
+            pltpu.VMEM((4, 2, rows_all, feats), jnp.bfloat16),
             pltpu.VMEM((3, rows_all, width), jnp.float32),
+            pltpu.VMEM((3, rows_all, width), jnp.bfloat16),
         ),
-    )(
-        quarters,
-        fused.reshape(view + (2, pairs, width)),
-        down.reshape(view + (pairs, width)),
-        *arrived,
-    )
+    )(quarters, weights.reshape(stored), *arrived)
+    grads = to_homes(results[0].reshape(expert_count, 3, pairs, width))
     returned = moved(results[1:], -1)
 
-    def gradient(which, first, members):
+    def combined(rc, *added):
+        half = spec((nz, 1, 2, micro, tokens, feats), lambda i, *refs: (0, i))
         return call(
-            functools.partial(gradient_kernel, offsets),
-            4,
-            [spec((members, rows_all, width), lambda i, *refs: (first // members,))]
-            + [spec((1, 1, 1, chunk_rows, feats), lambda i, *refs: (i // 2, i % 2, which))]
-            * offsets,
-            spec((1, blocks, 2, members, pairs, width), lambda i, q: (q[i],)),
-            jax.ShapeDtypeStruct(view + (members, pairs, width), jnp.bfloat16),
-        )(quarters, results[0], *arrived)
-
-    fused_grad = to_homes(gradient(0, 0, 2).reshape(expert_count, 2, pairs, width))
-    down_grad = to_homes(gradient(1, 2, 1).reshape(expert_count, pairs, width))
-
-    keep, send = call(
-        functools.partial(combine_kernel, offsets),
-        2,
-        [spec(pick_shape)] * 3 + [chunk_pair] * offsets,
-        [spec((nz, 1, 2, micro, tokens, feats), lambda i, *refs: (0, i))] * 2,
-        [jax.ShapeDtypeStruct(line_shape, jnp.bfloat16)] * 2,
-    )(quarters, *selections, *returned)
-    send = lax.ppermute(send, "c", swap)
-    keep = (keep.astype(jnp.float32) + send.astype(jnp.float32)).astype(jnp.bfloat16)
+            functools.partial(combine_kernel, offsets),
+            2,
+            [spec(pick_shape)] * 3
+            + [spec((1, 1, 2, chunk_rows, feats), lambda i, *refs: (rc, i))] * offsets
+            + [half] * len(added),
+            half,
+            jax.ShapeDtypeStruct(line_shape, jnp.bfloat16),
+        )(quarters, *selections, *returned, *added)
+
+    keep = combined(0, lax.ppermute(combined(1), "c", swap))
     keep = lax.psum_scatter(keep.reshape(-1, feats), "z", scatter_dimension=0, tiled=True)
     keep = keep.reshape(2, -1, feats)
     total = keep[0].astype(jnp.float32) + lax.ppermute(keep[1], "xh", swap).astype(jnp.float32)
     total = jnp.dot(total.astype(jnp.bfloat16), halves.T, preferred_element_type=jnp.float32)
     total = total.astype(jnp.bfloat16).reshape(2, micro, tokens, feats)
-    return (total[0], total[1], fused_grad[:, 0], fused_grad[:, 1], down_grad)
+    return (total[0], total[1], grads[:, 0], grads[:, 1], grads[:, 2])
 
 
 def build(devices, sizes):

time: 437 us -> 442 us (1.011)
  waiting for transfers between devices: 247 us -> 256 us
  Pallas kernels: 38.8 us -> 32.9 us
    all_gather x1, waiting for transfers between devices: 17.5 us -> 96.9 us  [shards(): line = lax.all_gather(jnp.concatenate([own, across, meta]), 'z', axis=0)]
    reduce_scatter x1, waiting for transfers between devices: 85.7 us -> 42.3 us  [shards(): lax.psum_scatter(keep.reshape(-1, feats), 'z', scatter_dimension=0, tiled...]
    all_to_all x4 -> x2, waiting for transfers between devices: 30.2 us -> 0.01 us  [to_homes(): lax.all_to_all(blocks, HOMES, split_axis=0, concat_axis=0, tiled=True)]
    ppermute x14, starting transfers between devices: 61.8 us -> 87.3 us  [moved(): done.append(lax.ppermute(piece, ('xl', 'y'), pairs_list))]
    all_to_all x4 -> x2, starting transfers between devices: 48.1 us -> 27.5 us  [to_homes(): lax.all_to_all(blocks, HOMES, split_axis=0, concat_axis=0, tiled=True)]
    ppermute x14, waiting for transfers between devices: 99.3 us -> 88.4 us  [moved(): done.append(lax.ppermute(piece, ('xl', 'y'), pairs_list))]
    ppermute x1, waiting for transfers between devices: 7.82 us -> 16.1 us  [shards(): across = lax.ppermute(own, 'xh', swap)]
    pallas_call x4 -> x3, Pallas kernels: 32.5 us -> 26.7 us  [the longest x1 17.4 us: shards(): call(functools.partial(expert_kernel, offsets), 8, [spec((1,) + stored[1:...]
  transfers between devices with their start and end apart: 24 -> 22, of which waited for: 11 -> 12; matrix products, arithmetic and copies ran while one was open for 3% -> 2% of each run, Pallas kernels for 4% -> 4%
where the time goes in v4:
time: 442 us; the launch traced here: 441 us
  waiting for transfers between devices  256 us (58%)
  starting transfers between devices  118 us (27%)
  Pallas kernels  32.9 us (7%)
  between operations  14.4 us (3%)
  local copies, waits for them, and re-layouts  10.2 us (2%)
  other arithmetic  7.68 us (2%)
    all_gather x1, waiting for transfers between devices, shards(): line = lax.all_gather(jnp.concatenate([own, across, meta]), 'z', axis=0)  96.9 us
    ppermute x14, waiting for transfers between devices, moved(): done.append(lax.ppermute(piece, ('xl', 'y'), pairs_list))  88.4 us
    ppermute x14, starting transfers between devices, moved(): done.append(lax.ppermute(piece, ('xl', 'y'), pairs_list))  87.3 us
    reduce_scatter x1, waiting for transfers between devices, shards(): lax.psum_scatter(keep.reshape(-1, feats), 'z', scatter_dimension=0, tiled...  42.3 us
    all_to_all x2, starting transfers between devices, to_homes(): lax.all_to_all(blocks, HOMES, split_axis=0, concat_axis=0, tiled=True)  27.5 us
    pallas_call x1, Pallas kernels, shards(): call(functools.partial(expert_kernel, offsets), 8, [spec((1,) + stored[1:...  17.4 us
    ppermute x1, waiting for transfers between devices, shards(): across = lax.ppermute(own, 'xh', swap)  16.1 us
    pallas_call x2, Pallas kernels, combined(): call(functools.partial(combine_kernel, offsets), 2, [spec(pick_shape)] *...  9.34 us
  transfers between devices with their start and end apart: 22, of which 12 were waited for; matrix products, arithmetic and copies ran while one was open for 2% of the time, Pallas kernels for 4%

profile of v4, /device:TPU:6, one launch (start us, length us, event | category | flops | bytes accessed | tf_op | source)
XLA Modules:
  0.0 441.3 jit_solution(5462843931974640187)
XLA Ops:
  7.2 5.1 %pad_maximum_fusion = bf16[128,3,16,384]{3,2,1,0:T(8,128)(2,1)} fusion(bf16[128,1,16,384]{3,2,1,0:T(8,128)(2,1)} %bitcast.50, bf16[128,1,16,384]{3,2,1,0:T(8,128)(2,1)} %bitcast.51, bf16[128,1,16,384]{3,2,1,0:T(8,128)(2,1)} %bitcast.52), kind=kLoop, calls=%fused_computation | loop fusion | flops 4718592 | bytes 9437184 | tf_op jit(solution)/shard_map/stack | solution.py:247
  12.3 14.8 %all-to-all-start = ((bf16[128,3,16,384]{3,2,1,0:T(8,128)(2,1)}), bf16[128,3,16,384]{3,2,1,0:T(8,128)(2,1)}, u32[]{:S(2)}, u32[]{:S(2)}) async-start(bf16[128,3,16,384]{3,2,1,0:T(8,128)(2,1)} %pad_maximum_fusion), calls=%async_computation | async-start | bytes 9437184 | tf_op jit(solution)/shard_map/all_to_all | solution.py:225
  29.3 16.1 %collective-permute-done = bf16[128,512]{1,0:T(8,128)(2,1)S(1)} collective-permute-done((bf16[128,512]{1,0:T(8,128)(2,1)S(1)}, bf16[128,512]{1,0:T(8,128)(2,1)S(1)}, u32[]{:S(2)}, u32[]{:S(2)}) %collective-permute-start) | collective-permute-done | bytes 131104 | tf_op jit(solution)/shard_map/ppermute | solution.py:246
  46.1 96.9 %all-gather.3.cloned.1.call-done = bf16[2304,512]{1,0:T(8,128)(2,1)} async-done(((bf16[288,512]{1,0:T(8,128)(2,1)}), bf16[2304,512]{1,0:T(8,128)(2,1)}) %all-gather.3.cloned.1.call-update) | async-done | bytes 2359312 | tf_op jit(solution)/shard_map/all_gather | solution.py:248
  144.3 3.4 collective-permute-done.1.other_ref
  149.2 6.2 %shard_map.128 = (bf16[2,256,256]{2,1,0:T(8,128)(2,1)}, bf16[2,256,256]{2,1,0:T(8,128)(2,1)}, bf16[2,256,256]{2,1,0:T(8,128)(2,1)}, bf16[2,2,2,64,512]{4,3,2,1,0...) custom-call(s32[8]{0:T(128)} %copy-done.19, ...), custom_call_target="tpu_custom_call" | custom-call | tf_op jit(solution)/shard_map/pallas_call | solution.py:274
  163.2 7.7 %collective-permute-done.2.refs_1_ = bf16[2,2,2,64,512]{4,3,2,1,0:T(8,128)(2,1)S(1)} collective-permute-done((bf16[2,2,2,64,512]{4,3,2,1,0:T(8,128)(2,1)}, bf16[2,2,2,64,512]{4,3,2,1,0:T(8,128)(2,1)S(1)}, u32[]{:S(2)}, u32[]{:S(2)}) %collective-permute-start.2) | collective-permute-done | bytes 524320 | tf_op jit(solution)/shard_map/ppermute | solution.py:293
  170.9 30.2 %collective-permute-start.7 = (bf16[2,2,2,64,512]{4,3,2,1,0:T(8,128)(2,1)}, bf16[2,2,2,64,512]{4,3,2,1,0:T(8,128)(2,1)S(1)}, u32[]{:S(2)}, u32[]{:S(2)}) collective-permute-start(bf16[2,2,2,64,512]{4,3,2,1,0:T(8,128)(2,1)} %get-tuple-element.34), channel_id=1, source_target_pairs={{0,48},{8,56},{16,32},{24,40},{32,16},{40,24},{48,0},{56,8},{1,49}... | collective-permute-start | bytes 1572872 | tf_op jit(solution)/shard_map/ppermute | solution.py:293
  203.1 10.6 %collective-permute-done.7.refs_6_ = bf16[2,2,2,64,512]{4,3,2,1,0:T(8,128)(2,1)S(1)} collective-permute-done((bf16[2,2,2,64,512]{4,3,2,1,0:T(8,128)(2,1)}, bf16[2,2,2,64,512]{4,3,2,1,0:T(8,128)(2,1)S(1)}, u32[]{:S(2)}, u32[]{:S(2)}) %collective-permute-start.7) | collective-permute-done | bytes 524320 | tf_op jit(solution)/shard_map/ppermute | solution.py:293
  213.7 5.6 %collective-permute-done.8.refs_7_ = bf16[2,2,2,64,512]{4,3,2,1,0:T(8,128)(2,1)} collective-permute-done((bf16[2,2,2,64,512]{4,3,2,1,0:T(8,128)(2,1)}, bf16[2,2,2,64,512]{4,3,2,1,0:T(8,128)(2,1)}, u32[]{:S(2)}, u32[]{:S(2)}) %collective-permute-start.8) | collective-permute-done | bytes 524320 | tf_op jit(solution)/shard_map/ppermute | solution.py:293
  219.4 17.4 %shard_map.129 = (bf16[4,16,2,3,16,384]{5,4,3,2,1,0:T(8,128)(2,1)}, bf16[2,2,2,64,512]{4,3,2,1,0:T(8,128)(2,1)}, bf16[2,2,2,64,512]{4,3,2,1,0:T(8,128)(2,1)}, bf...) custom-call(s32[4]{0:T(128)} %fusion.27.quarter_ref.expert_ref, ...), custom_call_target="tpu_custom_call" | custom-call | tf_op jit(solution)/shard_map/pallas_call | solution.py:312
  236.8 12.8 %all-to-all-start.1 = ((bf16[128,3,16,384]{3,2,1,0:T(8,128)(2,1)}), bf16[128,3,16,384]{3,2,1,0:T(8,128)(2,1)}, u32[]{:S(2)}, u32[]{:S(2)}) async-start(bf16[128,3,16,384]{3,2,1,0:T(8,128)(2,1)} %bitcast.49), calls=%async_computation.2 | async-start | bytes 9437184 | tf_op jit(solution)/shard_map/all_to_all | solution.py:225
  249.6 3.1 collective-permute-start.9
  254.4 3.6 collective-permute-start.13
  258.0 45.4 %collective-permute-done.9.refs_1_ = bf16[2,2,2,64,512]{4,3,2,1,0:T(8,128)(2,1)S(1)} collective-permute-done((bf16[2,2,2,64,512]{4,3,2,1,0:T(8,128)(2,1)}, bf16[2,2,2,64,512]{4,3,2,1,0:T(8,128)(2,1)S(1)}, u32[]{:S(2)}, u32[]{:S(2)}) %collective-permute-start.9) | collective-permute-done | bytes 524320 | tf_op jit(solution)/shard_map/ppermute | solution.py:293
  303.4 3.3 collective-permute-start.14
  306.7 37.6 %collective-permute-start.15 = (bf16[2,2,2,64,512]{4,3,2,1,0:T(8,128)(2,1)S(1)}, bf16[2,2,2,64,512]{4,3,2,1,0:T(8,128)(2,1)S(1)}, u32[]{:S(2)}, u32[]{:S(2)}) collective-permute-start(bf16[2,2,2,64,512]{4,3,2,1,0:T(8,128)(2,1)S(1)} %copy-done.22), channel_id=1, source_target_pairs={{0,40},{8,48},{16,56},{24,32},{32,8},{40,16},{48,24},{56,0},{1,41}... | collective-permute-start | bytes 1572872 | tf_op jit(solution)/shard_map/ppermute | solution.py:293
  344.4 17.7 %collective-permute-done.15.refs_7_ = bf16[2,2,2,64,512]{4,3,2,1,0:T(8,128)(2,1)S(1)} collective-permute-done((bf16[2,2,2,64,512]{4,3,2,1,0:T(8,128)(2,1)S(1)}, bf16[2,2,2,64,512]{4,3,2,1,0:T(8,128)(2,1)S(1)}, u32[]{:S(2)}, u32[]{:S(2)}) %collective-permute-start.15) | collective-permute-done | bytes 524320 | tf_op jit(solution)/shard_map/ppermute | solution.py:293
  362.9 4.6 %shard_map.130 = bf16[8,2,2,2,32,512]{5,4,3,2,1,0:T(8,128)(2,1)} custom-call(s32[4]{0:T(128)} %fusion.27.quarter_ref.expert_ref, bf16[2,256,256]{2,1,0:T(8,128)(2,1)} %get-tuple-element.25.pick_ref, bf16[2,256,256]{2,1,0:T(8,128)(2,1)} %get-tuple-element.26.high_ref, bf16[2,256,256]{2,1,0:T(8,128)(2,1)} %get-tuple-element.27.low_ref, ...), custom_call_target="tpu_custom_call" | custom-call | tf_op jit(solution)/shard_map/pallas_call | solution.py:332
  367.5 4.4 collective-permute-done.16.refs_8_
  373.2 4.8 %shard_map.131 = bf16[8,2,2,2,32,512]{5,4,3,2,1,0:T(8,128)(2,1)} custom-call(s32[4]{0:T(128)} %fusion.27.quarter_ref.expert_ref, bf16[2,256,256]{2,1,0:T(8,128)(2,1)} %get-tuple-element.25.pick_ref, bf16[2,256,256]{2,1,0:T(8,128)(2,1)} %get-tuple-element.26.high_ref, bf16[2,256,256]{2,1,0:T(8,128)(2,1)} %get-tuple-element.27.low_ref, ...), custom_call_target="tpu_custom_call" | custom-call | tf_op jit(solution)/shard_map/pallas_call | solution.py:332
  378.0 42.3 %reduce-scatter.2.cloned.1.call-done = bf16[256,512]{1,0:T(8,128)(2,1)} async-done(((bf16[2048,512]{1,0:T(8,128)(2,1)}), bf16[256,512]{1,0:T(8,128)(2,1)}) %reduce-scatter.2.cloned.1.call-update) | async-done | bytes 262160 | tf_op jit(solution)/shard_map/reduce_scatter | solution.py:343
  422.8 4.9 %collective-permute-done.17 = bf16[128,512]{1,0:T(8,128)(2,1)S(1)} collective-permute-done((bf16[128,512]{1,0:T(8,128)(2,1)S(1)}, bf16[128,512]{1,0:T(8,128)(2,1)S(1)}, u32[]{:S(2)}, u32[]{:S(2)}) %collective-permute-start.17) | collective-permute-done | bytes 131104 | tf_op jit(solution)/shard_map/ppermute | solution.py:345
  429.7 4.7 %slice_bitcast_fusion = (bf16[128,16,384]{2,1,0:T(8,128)(2,1)}, bf16[128,16,384]{2,1,0:T(8,128)(2,1)}, bf16[128,16,384]{2,1,0:T(8,128)(2,1)}) fusion(bf16[128,3,16,384]{3,2,1,0:T(8,128)(2,1)} %all-to-all-done.1), kind=kLoop, calls=%fused_computation.1 | loop fusion | bytes 9437184 | tf_op jit(solution)/shard_map/squeeze | solution.py:348
  (101 shorter events, 23.7 us)
Async XLA Ops:
  12.3 207.0 %all-to-all-start = ((bf16[128,3,16,384]{3,2,1,0:T(8,128)(2,1)}), bf16[128,3,16,384]{3,2,1,0:T(8,128)(2,1)}, u32[]{:S(2)}, u32[]{:S(2)}) async-start(bf16[128,3,16,384]{3,2,1,0:T(8,128)(2,1)} %pad_maximum_fusion), calls=%async_computation | async-start | bytes 9437184 | tf_op jit(solution)/shard_map/all_to_all | solution.py:225
  27.1 116.1 %copy-start.20 = (s32[2,128]{1,0:T(2,128)S(1)}, s32[2,128]{1,0:T(2,128)}, u32[]{:S(2)}) copy-start(s32[2,128]{1,0:T(2,128)} %param.17) | copy-start | bytes 3076
  27.1 116.2 %copy-start.21 = (s32[2,64]{1,0:T(2,128)S(1)}, s32[2,64]{1,0:T(2,128)}, u32[]{:S(2)}) copy-start(s32[2,64]{1,0:T(2,128)} %param.16) | copy-start | bytes 1540
  27.1 115.9 %all-gather.3.cloned.1.call-start = ((), (), s32[]{:S(2)}) async-start(), calls=%async_computation.4 | async-start | bytes 2654208 | tf_op jit(solution)/shard_map/all_gather | solution.py:248
  27.6 17.8 %collective-permute-start = (bf16[128,512]{1,0:T(8,128)(2,1)S(1)}, bf16[128,512]{1,0:T(8,128)(2,1)S(1)}, u32[]{:S(2)}, u32[]{:S(2)}) collective-permute-start(bf16[128,512]{1,0:T(8,128)(2,1)S(1)} %convolution_convert_fusion.1), channel_id=1, source_target_pairs={{0,128},{128,0},{1,129},{129,1},{2,130},{130,2},{3,131},{131,3},{4... | collective-permute-start | bytes 393224 | tf_op jit(solution)/shard_map/ppermute | solution.py:246
  143.0 4.7 %collective-permute-start.1 = (bf16[8,288,512]{2,1,0:T(8,128)(2,1)}, bf16[8,288,512]{2,1,0:T(8,128)(2,1)S(1)}, u32[]{:S(2)}, u32[]{:S(2)}) collective-permute-start(bf16[8,288,512]{2,1,0:T(8,128)(2,1)} %bitcast.45), channel_id=1, source_target_pairs={{0,64},{64,0},{1,65},{65,1},{2,66},{66,2},{3,67},{67,3},{4,68},{68... | collective-permute-start | bytes 7077896 | tf_op jit(solution)/shard_map/ppermute | solution.py:250
  155.4 15.5 %collective-permute-start.2 = (bf16[2,2,2,64,512]{4,3,2,1,0:T(8,128)(2,1)}, bf16[2,2,2,64,512]{4,3,2,1,0:T(8,128)(2,1)S(1)}, u32[]{:S(2)}, u32[]{:S(2)}) collective-permute-start(bf16[2,2,2,64,512]{4,3,2,1,0:T(8,128)(2,1)} %get-tuple-element.29), channel_id=1, source_target_pairs={{0,8},{8,16},{16,24},{24,0},{32,40},{40,48},{48,56},{56,32},{1,9},... | collective-permute-start | bytes 1572872 | tf_op jit(solution)/shard_map/ppermute | solution.py:293
  157.0 45.5 %collective-permute-start.3 = (bf16[2,2,2,64,512]{4,3,2,1,0:T(8,128)(2,1)}, bf16[2,2,2,64,512]{4,3,2,1,0:T(8,128)(2,1)S(1)}, u32[]{:S(2)}, u32[]{:S(2)}) collective-permute-start(bf16[2,2,2,64,512]{4,3,2,1,0:T(8,128)(2,1)} %get-tuple-element.30), channel_id=1, source_target_pairs={{0,16},{8,24},{16,0},{24,8},{32,48},{40,56},{48,32},{56,40},{1,17}... | collective-permute-start | bytes 1572872 | tf_op jit(solution)/shard_map/ppermute | solution.py:293
  159.7 43.3 %collective-permute-start.4 = (bf16[2,2,2,64,512]{4,3,2,1,0:T(8,128)(2,1)}, bf16[2,2,2,64,512]{4,3,2,1,0:T(8,128)(2,1)S(1)}, u32[]{:S(2)}, u32[]{:S(2)}) collective-permute-start(bf16[2,2,2,64,512]{4,3,2,1,0:T(8,128)(2,1)} %get-tuple-element.31), channel_id=1, source_target_pairs={{0,24},{8,0},{16,8},{24,16},{32,56},{40,32},{48,40},{56,48},{1,25}... | collective-permute-start | bytes 1572872 | tf_op jit(solution)/shard_map/ppermute | solution.py:293
  161.2 41.9 %collective-permute-start.5 = (bf16[2,2,2,64,512]{4,3,2,1,0:T(8,128)(2,1)}, bf16[2,2,2,64,512]{4,3,2,1,0:T(8,128)(2,1)S(1)}, u32[]{:S(2)}, u32[]{:S(2)}) collective-permute-start(bf16[2,2,2,64,512]{4,3,2,1,0:T(8,128)(2,1)} %get-tuple-element.32), channel_id=1, source_target_pairs={{0,32},{8,40},{16,48},{24,56},{32,0},{40,8},{48,16},{56,24},{1,33}... | collective-permute-start | bytes 1572872 | tf_op jit(solution)/shard_map/ppermute | solution.py:293
  162.1 41.0 %collective-permute-start.6 = (bf16[2,2,2,64,512]{4,3,2,1,0:T(8,128)(2,1)}, bf16[2,2,2,64,512]{4,3,2,1,0:T(8,128)(2,1)S(1)}, u32[]{:S(2)}, u32[]{:S(2)}) collective-permute-start(bf16[2,2,2,64,512]{4,3,2,1,0:T(8,128)(2,1)} %get-tuple-element.33), channel_id=1, source_target_pairs={{0,40},{8,48},{16,56},{24,32},{32,8},{40,16},{48,24},{56,0},{1,41}... | collective-permute-start | bytes 1572872 | tf_op jit(solution)/shard_map/ppermute | solution.py:293
  170.9 42.8 %collective-permute-start.7 = (bf16[2,2,2,64,512]{4,3,2,1,0:T(8,128)(2,1)}, bf16[2,2,2,64,512]{4,3,2,1,0:T(8,128)(2,1)S(1)}, u32[]{:S(2)}, u32[]{:S(2)}) collective-permute-start(bf16[2,2,2,64,512]{4,3,2,1,0:T(8,128)(2,1)} %get-tuple-element.34), channel_id=1, source_target_pairs={{0,48},{8,56},{16,32},{24,40},{32,16},{40,24},{48,0},{56,8},{1,49}... | collective-permute-start | bytes 1572872 | tf_op jit(solution)/shard_map/ppermute | solution.py:293
  202.5 16.8 %collective-permute-start.8 = (bf16[2,2,2,64,512]{4,3,2,1,0:T(8,128)(2,1)}, bf16[2,2,2,64,512]{4,3,2,1,0:T(8,128)(2,1)}, u32[]{:S(2)}, u32[]{:S(2)}) collective-permute-start(bf16[2,2,2,64,512]{4,3,2,1,0:T(8,128)(2,1)} %get-tuple-element.35), channel_id=1, source_target_pairs={{0,56},{8,32},{16,40},{24,48},{32,24},{40,0},{48,8},{56,16},{1,57}... | collective-permute-start | bytes 1572872 | tf_op jit(solution)/shard_map/ppermute | solution.py:293
  236.8 192.9 %all-to-all-start.1 = ((bf16[128,3,16,384]{3,2,1,0:T(8,128)(2,1)}), bf16[128,3,16,384]{3,2,1,0:T(8,128)(2,1)}, u32[]{:S(2)}, u32[]{:S(2)}) async-start(bf16[128,3,16,384]{3,2,1,0:T(8,128)(2,1)} %bitcast.49), calls=%async_computation.2 | async-start | bytes 9437184 | tf_op jit(solution)/shard_map/all_to_all | solution.py:225
  249.6 170.7 %reduce-scatter.2.cloned.1.call-start = ((), (), s32[]{:S(2)}) async-start(), calls=%async_computation.3 | async-start | bytes 2359296 | tf_op jit(solution)/shard_map/reduce_scatter | solution.py:343
  249.6 53.8 %collective-permute-start.9 = (bf16[2,2,2,64,512]{4,3,2,1,0:T(8,128)(2,1)}, bf16[2,2,2,64,512]{4,3,2,1,0:T(8,128)(2,1)S(1)}, u32[]{:S(2)}, u32[]{:S(2)}) collective-permute-start(bf16[2,2,2,64,512]{4,3,2,1,0:T(8,128)(2,1)} %get-tuple-element.37), channel_id=1, source_target_pairs={{0,24},{8,0},{16,8},{24,16},{32,56},{40,32},{48,40},{56,48},{1,25}... | collective-permute-start | bytes 1572872 | tf_op jit(solution)/shard_map/ppermute | solution.py:293
  252.7 54.0 %collective-permute-start.10 = (bf16[2,2,2,64,512]{4,3,2,1,0:T(8,128)(2,1)}, bf16[2,2,2,64,512]{4,3,2,1,0:T(8,128)(2,1)S(1)}, u32[]{:S(2)}, u32[]{:S(2)}) collective-permute-start(bf16[2,2,2,64,512]{4,3,2,1,0:T(8,128)(2,1)} %get-tuple-element.38), channel_id=1, source_target_pairs={{0,16},{8,24},{16,0},{24,8},{32,48},{40,56},{48,32},{56,40},{1,17}... | collective-permute-start | bytes 1572872 | tf_op jit(solution)/shard_map/ppermute | solution.py:293
  253.3 91.0 %collective-permute-start.11 = (bf16[2,2,2,64,512]{4,3,2,1,0:T(8,128)(2,1)}, bf16[2,2,2,64,512]{4,3,2,1,0:T(8,128)(2,1)S(1)}, u32[]{:S(2)}, u32[]{:S(2)}) collective-permute-start(bf16[2,2,2,64,512]{4,3,2,1,0:T(8,128)(2,1)} %get-tuple-element.39), channel_id=1, source_target_pairs={{0,8},{8,16},{16,24},{24,0},{32,40},{40,48},{48,56},{56,32},{1,9},... | collective-permute-start | bytes 1572872 | tf_op jit(solution)/shard_map/ppermute | solution.py:293
  254.3 90.0 %collective-permute-start.12 = (bf16[2,2,2,64,512]{4,3,2,1,0:T(8,128)(2,1)}, bf16[2,2,2,64,512]{4,3,2,1,0:T(8,128)(2,1)S(1)}, u32[]{:S(2)}, u32[]{:S(2)}) collective-permute-start(bf16[2,2,2,64,512]{4,3,2,1,0:T(8,128)(2,1)} %get-tuple-element.40), channel_id=1, source_target_pairs={{0,32},{8,40},{16,48},{24,56},{32,0},{40,8},{48,16},{56,24},{1,33}... | collective-permute-start | bytes 1572872 | tf_op jit(solution)/shard_map/ppermute | solution.py:293
  254.4 89.9 %collective-permute-start.13 = (bf16[2,2,2,64,512]{4,3,2,1,0:T(8,128)(2,1)}, bf16[2,2,2,64,512]{4,3,2,1,0:T(8,128)(2,1)S(1)}, u32[]{:S(2)}, u32[]{:S(2)}) collective-permute-start(bf16[2,2,2,64,512]{4,3,2,1,0:T(8,128)(2,1)} %get-tuple-element.41), channel_id=1, source_target_pairs={{0,56},{8,32},{16,40},{24,48},{32,24},{40,0},{48,8},{56,16},{1,57}... | collective-permute-start | bytes 1572872 | tf_op jit(solution)/shard_map/ppermute | solution.py:293
  303.4 40.9 %collective-permute-start.14 = (bf16[2,2,2,64,512]{4,3,2,1,0:T(8,128)(2,1)S(1)}, bf16[2,2,2,64,512]{4,3,2,1,0:T(8,128)(2,1)S(1)}, u32[]{:S(2)}, u32[]{:S(2)}) collective-permute-start(bf16[2,2,2,64,512]{4,3,2,1,0:T(8,128)(2,1)S(1)} %copy-done.23), channel_id=1, source_target_pairs={{0,48},{8,56},{16,32},{24,40},{32,16},{40,24},{48,0},{56,8},{1,49}... | collective-permute-start | bytes 1572872 | tf_op jit(solution)/shard_map/ppermute | solution.py:293
  306.7 55.4 %collective-permute-start.15 = (bf16[2,2,2,64,512]{4,3,2,1,0:T(8,128)(2,1)S(1)}, bf16[2,2,2,64,512]{4,3,2,1,0:T(8,128)(2,1)S(1)}, u32[]{:S(2)}, u32[]{:S(2)}) collective-permute-start(bf16[2,2,2,64,512]{4,3,2,1,0:T(8,128)(2,1)S(1)} %copy-done.22), channel_id=1, source_target_pairs={{0,40},{8,48},{16,56},{24,32},{32,8},{40,16},{48,24},{56,0},{1,41}... | collective-permute-start | bytes 1572872 | tf_op jit(solution)/shard_map/ppermute | solution.py:293
  367.5 4.4 collective-permute-start.16
  421.2 6.6 %collective-permute-start.17 = (bf16[128,512]{1,0:T(8,128)(2,1)S(1)}, bf16[128,512]{1,0:T(8,128)(2,1)S(1)}, u32[]{:S(2)}, u32[]{:S(2)}) collective-permute-start(bf16[128,512]{1,0:T(8,128)(2,1)S(1)} %slice.48), channel_id=1, source_target_pairs={{0,128},{128,0},{1,129},{129,1},{2,130},{130,2},{3,131},{131,3},{4... | collective-permute-start | bytes 393224 | tf_op jit(solution)/shard_map/ppermute | solution.py:345
  (22 other events, 514.0 us)
Sparse Core Ops, SparseCore 0:
  46.2 96.7 all-gather.2
  378.2 42.0 reduce-scatter.1

commit v5 on v4

--- a/solution.py
+++ b/solution.py
@@ -147,11 +147,11 @@
     return first, second
 
 
-def expert_kernel(offsets, quarter_ref, weight_ref, *refs):
+def expert_kernel(offsets, quarter_ref, fused_ref, down_ref, *refs):
     row_refs, refs = refs[:offsets], refs[offsets:]
     grad_ref, refs = refs[0], refs[1:]
     out_refs, (w_scr, row_scr, pre_scr, act_scr) = refs[:offsets], refs[offsets:]
-    _, blocks, _, _, pairs, width = weight_ref.shape
+    _, blocks, _, pairs, width = down_ref.shape
     depth = blocks * pairs
     rows = row_refs[0].shape[3]
     step = pl.program_id(0)
@@ -167,9 +167,12 @@
         row_scr[step, 0] = x
         row_scr[step, 1] = g
         for k in range(3):
-            lower = weight_ref[0, :, 0, k].reshape(depth, width)
-            upper = weight_ref[0, :, 1, k].reshape(depth, width)
-            both = jnp.concatenate(swap_halves(lower, upper), axis=0)
+            if k < 2:
+                lower, upper = fused_ref[0, :, 0, k], fused_ref[0, :, 1, k]
+            else:
+                lower, upper = down_ref[0, :, 0], down_ref[0, :, 1]
+            halves = swap_halves(lower.reshape(depth, width), upper.reshape(depth, width))
+            both = jnp.concatenate(halves, axis=0)
             w_scr[k, step] = both
             pre_scr[k] += dot(g if k == 2 else x, both, 1, 0)
 
@@ -218,6 +221,7 @@
     xh, core = lax.axis_index("xh"), lax.axis_index("c")
     xl, y, z = (lax.axis_index(name) for name in EXPERT)
     steps = [(dx, dy) for dx in range(nxl) for dy in range(ny)]
+    steps = steps[:1] + sorted(steps[1:], key=lambda s: -s[0] - min(s[1], ny - s[1]))
     offsets = len(steps)
     swap = [(0, 1), (1, 0)]
 
@@ -244,9 +248,9 @@
     )
     meta = jnp.pad(meta, ((0, META_ROWS - 2 * routes), (0, feats - 2 * columns)))
     across = lax.ppermute(own, "xh", swap)
-    weights = jnp.stack([gate_proj, up_proj, down_proj], axis=1)
     line = lax.all_gather(jnp.concatenate([own, across, meta]), "z", axis=0)
-    weights = to_homes(weights)
+    down = to_homes(down_proj)
+    fused = to_homes(jnp.stack([gate_proj, up_proj], axis=1))
     line_other = lax.ppermute(line, "c", swap)
     line_shape = (nz, 2, 2, micro, tokens, feats)
 
@@ -312,7 +316,10 @@
     results = call(
         functools.partial(expert_kernel, offsets),
         8,
-        [spec((1,) + stored[1:], lambda i, q: (q[jnp.minimum(i, 3)],))]
+        [
+            spec((1, blocks, 2, 2, pairs, width), lambda i, q: (q[jnp.minimum(i, 3)],)),
+            spec((1, blocks, 2, pairs, width), lambda i, q: (q[jnp.minimum(i, 3)],)),
+        ]
         + [spec((1, 1, 2, chunk_rows, feats), early)] * offsets,
         [spec((1,) + stored[1:], lambda i, q: (q[jnp.maximum(i - 4, 0)],))]
         + [spec((1, 1, 2, chunk_rows, feats), late)] * offsets,
@@ -323,7 +330,12 @@
             pltpu.VMEM((3, rows_all, width), jnp.float32),
             pltpu.VMEM((3, rows_all, width), jnp.bfloat16),
         ),
-    )(quarters, weights.reshape(stored), *arrived)
+    )(
+        quarters,
+        fused.reshape(view + (2, pairs, width)),
+        down.reshape(view + (pairs, width)),
+        *arrived,
+    )
     grads = to_homes(results[0].reshape(expert_count, 3, pairs, width))
     returned = moved(results[1:], -1)
 
@@ -342,10 +354,12 @@
     keep = combined(0, lax.ppermute(combined(1), "c", swap))
     keep = lax.psum_scatter(keep.reshape(-1, feats), "z", scatter_dimension=0, tiled=True)
     keep = keep.reshape(2, -1, feats)
-    total = keep[0].astype(jnp.float32) + lax.ppermute(keep[1], "xh", swap).astype(jnp.float32)
+    across = lax.ppermute(keep[1], "xh", swap)
+    gradients = tuple(grads[:, k] for k in range(3))
+    total = keep[0].astype(jnp.float32) + across.astype(jnp.float32)
     total = jnp.dot(total.astype(jnp.bfloat16), halves.T, preferred_element_type=jnp.float32)
     total = total.astype(jnp.bfloat16).reshape(2, micro, tokens, feats)
-    return (total[0], total[1], grads[:, 0], grads[:, 1], grads[:, 2])
+    return (total[0], total[1], *gradients)
 
 
 def build(devices, sizes):

time: 442 us -> 396 us (0.90)
  starting transfers between devices: 118 us -> 69.5 us
  waiting for transfers between devices: 256 us -> 261 us
    all_gather x1, waiting for transfers between devices: 96.9 us -> 17.5 us  [shards(): line = lax.all_gather(jnp.concatenate([own, across, meta]), 'z', axis=0)]
    ppermute x14, starting transfers between devices: 87.3 us -> 26.9 us  [moved(): done.append(lax.ppermute(piece, ('xl', 'y'), pairs_list))]
    ppermute x14, waiting for transfers between devices: 88.4 us -> 146 us  [moved(): done.append(lax.ppermute(piece, ('xl', 'y'), pairs_list))]
    all_to_all x2 -> x3, waiting for transfers between devices: 0.01 us -> 30.2 us  [to_homes(): lax.all_to_all(blocks, HOMES, split_axis=0, concat_axis=0, tiled=True)]
    all_to_all x2 -> x3, starting transfers between devices: 27.5 us -> 39.8 us  [to_homes(): lax.all_to_all(blocks, HOMES, split_axis=0, concat_axis=0, tiled=True)]
    ppermute x1, waiting for transfers between devices: 16.1 us -> 7.81 us  [shards(): across = lax.ppermute(own, 'xh', swap)]
  transfers between devices with their start and end apart: 22 -> 23, of which waited for: 12 -> 17; matrix products, arithmetic and copies ran while one was open for 2% -> 3% of each run, Pallas kernels for 4% -> 4%
where the time goes in v5:
time: 396 us
  waiting for transfers between devices  261 us (66%)
  starting transfers between devices  69.5 us (18%)
  Pallas kernels  33 us (8%)
  between operations  14.3 us (4%)
  local copies, waits for them, and re-layouts  10.5 us (3%)
  other arithmetic  5.93 us (1%)
    ppermute x14, waiting for transfers between devices, moved(): done.append(lax.ppermute(piece, ('xl', 'y'), pairs_list))  146 us
    reduce_scatter x1, waiting for transfers between devices, shards(): lax.psum_scatter(keep.reshape(-1, feats), 'z', scatter_dimension=0, tiled...  45.6 us
    all_to_all x3, starting transfers between devices, to_homes(): lax.all_to_all(blocks, HOMES, split_axis=0, concat_axis=0, tiled=True)  39.8 us
    all_to_all x3, waiting for transfers between devices, to_homes(): lax.all_to_all(blocks, HOMES, split_axis=0, concat_axis=0, tiled=True)  30.2 us
    ppermute x14, starting transfers between devices, moved(): done.append(lax.ppermute(piece, ('xl', 'y'), pairs_list))  26.9 us
    all_gather x1, waiting for transfers between devices, shards(): line = lax.all_gather(jnp.concatenate([own, across, meta]), 'z', axis=0)  17.5 us
    pallas_call x1, Pallas kernels, shards(): call(functools.partial(expert_kernel, offsets), 8, [spec((1, blocks, 2, 2...  17.3 us
    pallas_call x2, Pallas kernels, combined(): call(functools.partial(combine_kernel, offsets), 2, [spec(pick_shape)] *...  9.47 us
  transfers between devices with their start and end apart: 23, of which 17 were waited for; matrix products, arithmetic and copies ran while one was open for 3% of the time, Pallas kernels for 4%

profile of v5, /device:TPU:6, one launch (start us, length us, event | category | flops | bytes accessed | tf_op | source)
XLA Modules:
  0.0 395.8 jit_solution(895557827031545335)
XLA Ops:
  7.2 14.4 %all-to-all-start.1 = ((bf16[128,16,384]{2,1,0:T(8,128)(2,1)}), bf16[128,16,384]{2,1,0:T(8,128)(2,1)S(1)}, u32[]{:S(2)}, u32[]{:S(2)}) async-start(bf16[128,16,384]{2,1,0:T(8,128)(2,1)} %param.15), calls=%async_computation.1 | async-start | bytes 3145728 | tf_op jit(solution)/shard_map/all_to_all | solution.py:229
  23.7 7.8 %collective-permute-done = bf16[128,512]{1,0:T(8,128)(2,1)S(1)} collective-permute-done((bf16[128,512]{1,0:T(8,128)(2,1)S(1)}, bf16[128,512]{1,0:T(8,128)(2,1)S(1)}, u32[]{:S(2)}, u32[]{:S(2)}) %collective-permute-start) | collective-permute-done | bytes 131104 | tf_op jit(solution)/shard_map/ppermute | solution.py:250
  35.7 30.2 %all-to-all-done.1 = bf16[128,16,384]{2,1,0:T(8,128)(2,1)S(1)} async-done(((bf16[128,16,384]{2,1,0:T(8,128)(2,1)}), bf16[128,16,384]{2,1,0:T(8,128)(2,1)S(1)}, u32[]{:S(2)}, u32[]{:S(2)}) %all-to-all-start.1) | async-done | bytes 1572896 | tf_op jit(solution)/shard_map/all_to_all | solution.py:229
  67.1 8.7 %all-to-all-start = ((bf16[128,2,16,384]{3,2,1,0:T(8,128)(2,1)}), bf16[128,2,16,384]{3,2,1,0:T(8,128)(2,1)S(1)}, u32[]{:S(2)}, u32[]{:S(2)}) async-start(bf16[128,2,16,384]{3,2,1,0:T(8,128)(2,1)} %pad_maximum_fusion), calls=%async_computation | async-start | bytes 6291456 | tf_op jit(solution)/shard_map/all_to_all | solution.py:229
  75.8 17.5 %all-gather.3.cloned.1.call-done = bf16[2304,512]{1,0:T(8,128)(2,1)} async-done(((bf16[288,512]{1,0:T(8,128)(2,1)}), bf16[2304,512]{1,0:T(8,128)(2,1)}) %all-gather.3.cloned.1.call-update) | async-done | bytes 2359312 | tf_op jit(solution)/shard_map/all_gather | solution.py:251
  98.9 6.3 %shard_map.128 = (bf16[2,256,256]{2,1,0:T(8,128)(2,1)}, bf16[2,256,256]{2,1,0:T(8,128)(2,1)}, bf16[2,256,256]{2,1,0:T(8,128)(2,1)}, bf16[2,2,2,64,512]{4,3,2,1,0...) custom-call(s32[8]{0:T(128)} %copy-done.15, ...), custom_call_target="tpu_custom_call" | custom-call | tf_op jit(solution)/shard_map/pallas_call | solution.py:278
  113.0 20.3 %collective-permute-done.2.refs_1_ = bf16[2,2,2,64,512]{4,3,2,1,0:T(8,128)(2,1)} collective-permute-done((bf16[2,2,2,64,512]{4,3,2,1,0:T(8,128)(2,1)}, bf16[2,2,2,64,512]{4,3,2,1,0:T(8,128)(2,1)}, u32[]{:S(2)}, u32[]{:S(2)}) %collective-permute-start.2) | collective-permute-done | bytes 524320 | tf_op jit(solution)/shard_map/ppermute | solution.py:297
  135.0 28.3 %collective-permute-done.3.refs_2_ = bf16[2,2,2,64,512]{4,3,2,1,0:T(8,128)(2,1)} collective-permute-done((bf16[2,2,2,64,512]{4,3,2,1,0:T(8,128)(2,1)}, bf16[2,2,2,64,512]{4,3,2,1,0:T(8,128)(2,1)}, u32[]{:S(2)}, u32[]{:S(2)}) %collective-permute-start.3) | collective-permute-done | bytes 524320 | tf_op jit(solution)/shard_map/ppermute | solution.py:297
  165.5 8.6 %collective-permute-done.6.refs_5_ = bf16[2,2,2,64,512]{4,3,2,1,0:T(8,128)(2,1)} collective-permute-done((bf16[2,2,2,64,512]{4,3,2,1,0:T(8,128)(2,1)}, bf16[2,2,2,64,512]{4,3,2,1,0:T(8,128)(2,1)}, u32[]{:S(2)}, u32[]{:S(2)}) %collective-permute-start.6) | collective-permute-done | bytes 524320 | tf_op jit(solution)/shard_map/ppermute | solution.py:297
  177.4 17.3 %shard_map.129 = (bf16[4,16,2,3,16,384]{5,4,3,2,1,0:T(8,128)(2,1)}, bf16[2,2,2,64,512]{4,3,2,1,0:T(8,128)(2,1)}, bf16[2,2,2,64,512]{4,3,2,1,0:T(8,128)(2,1)}, bf...) custom-call(s32[4]{0:T(128)} %fusion.27.quarter_ref.expert_ref, ...), custom_call_target="tpu_custom_call" | custom-call | tf_op jit(solution)/shard_map/pallas_call | solution.py:316
  194.7 16.7 %all-to-all-start.2 = ((bf16[128,3,16,384]{3,2,1,0:T(8,128)(2,1)}), bf16[128,3,16,384]{3,2,1,0:T(8,128)(2,1)}, u32[]{:S(2)}, u32[]{:S(2)}) async-start(bf16[128,3,16,384]{3,2,1,0:T(8,128)(2,1)} %bitcast.51), calls=%async_computation.3 | async-start | bytes 9437184 | tf_op jit(solution)/shard_map/all_to_all | solution.py:229
  221.8 25.2 %collective-permute-done.9.refs_1_ = bf16[2,2,2,64,512]{4,3,2,1,0:T(8,128)(2,1)S(1)} collective-permute-done((bf16[2,2,2,64,512]{4,3,2,1,0:T(8,128)(2,1)S(1)}, bf16[2,2,2,64,512]{4,3,2,1,0:T(8,128)(2,1)S(1)}, u32[]{:S(2)}, u32[]{:S(2)}) %collective-permute-start.9) | collective-permute-done | bytes 524320 | tf_op jit(solution)/shard_map/ppermute | solution.py:297
  248.5 15.0 %collective-permute-done.10.refs_2_ = bf16[2,2,2,64,512]{4,3,2,1,0:T(8,128)(2,1)S(1)} collective-permute-done((bf16[2,2,2,64,512]{4,3,2,1,0:T(8,128)(2,1)}, bf16[2,2,2,64,512]{4,3,2,1,0:T(8,128)(2,1)S(1)}, u32[]{:S(2)}, u32[]{:S(2)}) %collective-permute-start.10) | collective-permute-done | bytes 524320 | tf_op jit(solution)/shard_map/ppermute | solution.py:297
  263.5 3.9 collective-permute-start.15
  267.5 5.4 %collective-permute-done.11.refs_3_ = bf16[2,2,2,64,512]{4,3,2,1,0:T(8,128)(2,1)S(1)} collective-permute-done((bf16[2,2,2,64,512]{4,3,2,1,0:T(8,128)(2,1)}, bf16[2,2,2,64,512]{4,3,2,1,0:T(8,128)(2,1)S(1)}, u32[]{:S(2)}, u32[]{:S(2)}) %collective-permute-start.11) | collective-permute-done | bytes 524320 | tf_op jit(solution)/shard_map/ppermute | solution.py:297
  272.8 20.8 %collective-permute-done.12.refs_4_ = bf16[2,2,2,64,512]{4,3,2,1,0:T(8,128)(2,1)S(1)} collective-permute-done((bf16[2,2,2,64,512]{4,3,2,1,0:T(8,128)(2,1)}, bf16[2,2,2,64,512]{4,3,2,1,0:T(8,128)(2,1)S(1)}, u32[]{:S(2)}, u32[]{:S(2)}) %collective-permute-start.12) | collective-permute-done | bytes 524320 | tf_op jit(solution)/shard_map/ppermute | solution.py:297
  293.7 11.9 %collective-permute-done.13.refs_5_ = bf16[2,2,2,64,512]{4,3,2,1,0:T(8,128)(2,1)S(1)} collective-permute-done((bf16[2,2,2,64,512]{4,3,2,1,0:T(8,128)(2,1)}, bf16[2,2,2,64,512]{4,3,2,1,0:T(8,128)(2,1)S(1)}, u32[]{:S(2)}, u32[]{:S(2)}) %collective-permute-start.13) | collective-permute-done | bytes 524320 | tf_op jit(solution)/shard_map/ppermute | solution.py:297
  305.6 7.6 %collective-permute-done.15.refs_7_ = bf16[2,2,2,64,512]{4,3,2,1,0:T(8,128)(2,1)S(1)} collective-permute-done((bf16[2,2,2,64,512]{4,3,2,1,0:T(8,128)(2,1)}, bf16[2,2,2,64,512]{4,3,2,1,0:T(8,128)(2,1)S(1)}, u32[]{:S(2)}, u32[]{:S(2)}) %collective-permute-start.15) | collective-permute-done | bytes 524320 | tf_op jit(solution)/shard_map/ppermute | solution.py:297
  314.0 4.6 %shard_map.130 = bf16[8,2,2,2,32,512]{5,4,3,2,1,0:T(8,128)(2,1)} custom-call(s32[4]{0:T(128)} %fusion.27.quarter_ref.expert_ref, bf16[2,256,256]{2,1,0:T(8,128)(2,1)} %get-tuple-element.25.pick_ref, bf16[2,256,256]{2,1,0:T(8,128)(2,1)} %get-tuple-element.26.high_ref, bf16[2,256,256]{2,1,0:T(8,128)(2,1)} %get-tuple-element.27.low_ref, ...), custom_call_target="tpu_custom_call" | custom-call | tf_op jit(solution)/shard_map/pallas_call | solution.py:344
  318.6 4.4 %collective-permute-done.16.refs_8_ = bf16[8,2,2,2,32,512]{5,4,3,2,1,0:T(8,128)(2,1)S(1)} collective-permute-done((bf16[8,2,2,2,32,512]{5,4,3,2,1,0:T(8,128)(2,1)}, bf16[8,2,2,2,32,512]{5,4,3,2,1,0:T(8,128)(2,1)S(1)}, u32[]{:S(2)}, u32[]{:S(2)}) %collective-permute-start.16) | collective-permute-done | bytes 2097184 | tf_op jit(solution)/shard_map/ppermute | solution.py:354
  324.3 4.8 %shard_map.131 = bf16[8,2,2,2,32,512]{5,4,3,2,1,0:T(8,128)(2,1)} custom-call(s32[4]{0:T(128)} %fusion.27.quarter_ref.expert_ref, bf16[2,256,256]{2,1,0:T(8,128)(2,1)} %get-tuple-element.25.pick_ref, bf16[2,256,256]{2,1,0:T(8,128)(2,1)} %get-tuple-element.26.high_ref, bf16[2,256,256]{2,1,0:T(8,128)(2,1)} %get-tuple-element.27.low_ref, ...), custom_call_target="tpu_custom_call" | custom-call | tf_op jit(solution)/shard_map/pallas_call | solution.py:344
  329.2 45.6 %reduce-scatter.2.cloned.1.call-done = bf16[256,512]{1,0:T(8,128)(2,1)} async-done(((bf16[2048,512]{1,0:T(8,128)(2,1)}), bf16[256,512]{1,0:T(8,128)(2,1)}) %reduce-scatter.2.cloned.1.call-update) | async-done | bytes 262160 | tf_op jit(solution)/shard_map/reduce_scatter | solution.py:355
  377.0 5.3 %collective-permute-done.17 = bf16[128,512]{1,0:T(8,128)(2,1)S(1)} collective-permute-done((bf16[128,512]{1,0:T(8,128)(2,1)S(1)}, bf16[128,512]{1,0:T(8,128)(2,1)S(1)}, u32[]{:S(2)}, u32[]{:S(2)}) %collective-permute-start.17) | collective-permute-done | bytes 131104 | tf_op jit(solution)/shard_map/ppermute | solution.py:357
  384.2 4.7 %slice_bitcast_fusion = (bf16[128,16,384]{2,1,0:T(8,128)(2,1)}, bf16[128,16,384]{2,1,0:T(8,128)(2,1)}, bf16[128,16,384]{2,1,0:T(8,128)(2,1)}) fusion(bf16[128,3,16,384]{3,2,1,0:T(8,128)(2,1)} %all-to-all-done.2), kind=kLoop, calls=%fused_computation.1 | loop fusion | bytes 9437184 | tf_op jit(solution)/shard_map/squeeze | solution.py:358
  (93 shorter events, 46.0 us)
Async XLA Ops:
  7.2 58.7 %all-to-all-start.1 = ((bf16[128,16,384]{2,1,0:T(8,128)(2,1)}), bf16[128,16,384]{2,1,0:T(8,128)(2,1)S(1)}, u32[]{:S(2)}, u32[]{:S(2)}) async-start(bf16[128,16,384]{2,1,0:T(8,128)(2,1)} %param.15), calls=%async_computation.1 | async-start | bytes 3145728 | tf_op jit(solution)/shard_map/all_to_all | solution.py:229
  21.6 71.7 %all-gather.3.cloned.1.call-start = ((), (), s32[]{:S(2)}) async-start(), calls=%async_computation.5 | async-start | bytes 2654208 | tf_op jit(solution)/shard_map/all_gather | solution.py:251
  22.0 9.5 %collective-permute-start = (bf16[128,512]{1,0:T(8,128)(2,1)S(1)}, bf16[128,512]{1,0:T(8,128)(2,1)S(1)}, u32[]{:S(2)}, u32[]{:S(2)}) collective-permute-start(bf16[128,512]{1,0:T(8,128)(2,1)S(1)} %convolution_convert_fusion.1), channel_id=1, source_target_pairs={{0,128},{128,0},{1,129},{129,1},{2,130},{130,2},{3,131},{131,3},{4... | collective-permute-start | bytes 393224 | tf_op jit(solution)/shard_map/ppermute | solution.py:250
  67.1 98.4 %all-to-all-start = ((bf16[128,2,16,384]{3,2,1,0:T(8,128)(2,1)}), bf16[128,2,16,384]{3,2,1,0:T(8,128)(2,1)S(1)}, u32[]{:S(2)}, u32[]{:S(2)}) async-start(bf16[128,2,16,384]{3,2,1,0:T(8,128)(2,1)} %pad_maximum_fusion), calls=%async_computation | async-start | bytes 6291456 | tf_op jit(solution)/shard_map/all_to_all | solution.py:229
  93.3 4.9 %collective-permute-start.1 = (bf16[8,288,512]{2,1,0:T(8,128)(2,1)}, bf16[8,288,512]{2,1,0:T(8,128)(2,1)}, u32[]{:S(2)}, u32[]{:S(2)}) collective-permute-start(bf16[8,288,512]{2,1,0:T(8,128)(2,1)} %bitcast.46), channel_id=1, source_target_pairs={{0,64},{64,0},{1,65},{65,1},{2,66},{66,2},{3,67},{67,3},{4,68},{68... | collective-permute-start | bytes 7077896 | tf_op jit(solution)/shard_map/ppermute | solution.py:254
  105.1 28.2 %collective-permute-start.2 = (bf16[2,2,2,64,512]{4,3,2,1,0:T(8,128)(2,1)}, bf16[2,2,2,64,512]{4,3,2,1,0:T(8,128)(2,1)}, u32[]{:S(2)}, u32[]{:S(2)}) collective-permute-start(bf16[2,2,2,64,512]{4,3,2,1,0:T(8,128)(2,1)} %get-tuple-element.29), channel_id=1, source_target_pairs={{0,48},{8,56},{16,32},{24,40},{32,16},{40,24},{48,0},{56,8},{1,49}... | collective-permute-start | bytes 1572872 | tf_op jit(solution)/shard_map/ppermute | solution.py:297
  108.0 55.3 %collective-permute-start.3 = (bf16[2,2,2,64,512]{4,3,2,1,0:T(8,128)(2,1)}, bf16[2,2,2,64,512]{4,3,2,1,0:T(8,128)(2,1)}, u32[]{:S(2)}, u32[]{:S(2)}) collective-permute-start(bf16[2,2,2,64,512]{4,3,2,1,0:T(8,128)(2,1)} %get-tuple-element.30), channel_id=1, source_target_pairs={{0,16},{8,24},{16,0},{24,8},{32,48},{40,56},{48,32},{56,40},{1,17}... | collective-permute-start | bytes 1572872 | tf_op jit(solution)/shard_map/ppermute | solution.py:297
  108.8 56.7 %collective-permute-start.4 = (bf16[2,2,2,64,512]{4,3,2,1,0:T(8,128)(2,1)}, bf16[2,2,2,64,512]{4,3,2,1,0:T(8,128)(2,1)}, u32[]{:S(2)}, u32[]{:S(2)}) collective-permute-start(bf16[2,2,2,64,512]{4,3,2,1,0:T(8,128)(2,1)} %get-tuple-element.31), channel_id=1, source_target_pairs={{0,40},{8,48},{16,56},{24,32},{32,8},{40,16},{48,24},{56,0},{1,41}... | collective-permute-start | bytes 1572872 | tf_op jit(solution)/shard_map/ppermute | solution.py:297
  111.5 54.0 %collective-permute-start.5 = (bf16[2,2,2,64,512]{4,3,2,1,0:T(8,128)(2,1)}, bf16[2,2,2,64,512]{4,3,2,1,0:T(8,128)(2,1)}, u32[]{:S(2)}, u32[]{:S(2)}) collective-permute-start(bf16[2,2,2,64,512]{4,3,2,1,0:T(8,128)(2,1)} %get-tuple-element.32), channel_id=1, source_target_pairs={{0,56},{8,32},{16,40},{24,48},{32,24},{40,0},{48,8},{56,16},{1,57}... | collective-permute-start | bytes 1572872 | tf_op jit(solution)/shard_map/ppermute | solution.py:297
  112.9 61.2 %collective-permute-start.6 = (bf16[2,2,2,64,512]{4,3,2,1,0:T(8,128)(2,1)}, bf16[2,2,2,64,512]{4,3,2,1,0:T(8,128)(2,1)}, u32[]{:S(2)}, u32[]{:S(2)}) collective-permute-start(bf16[2,2,2,64,512]{4,3,2,1,0:T(8,128)(2,1)} %get-tuple-element.33), channel_id=1, source_target_pairs={{0,8},{8,16},{16,24},{24,0},{32,40},{40,48},{48,56},{56,32},{1,9},... | collective-permute-start | bytes 1572872 | tf_op jit(solution)/shard_map/ppermute | solution.py:297
  133.3 40.8 %collective-permute-start.7 = (bf16[2,2,2,64,512]{4,3,2,1,0:T(8,128)(2,1)}, bf16[2,2,2,64,512]{4,3,2,1,0:T(8,128)(2,1)}, u32[]{:S(2)}, u32[]{:S(2)}) collective-permute-start(bf16[2,2,2,64,512]{4,3,2,1,0:T(8,128)(2,1)} %get-tuple-element.34), channel_id=1, source_target_pairs={{0,24},{8,0},{16,8},{24,16},{32,56},{40,32},{48,40},{56,48},{1,25}... | collective-permute-start | bytes 1572872 | tf_op jit(solution)/shard_map/ppermute | solution.py:297
  163.3 14.1 %collective-permute-start.8 = (bf16[2,2,2,64,512]{4,3,2,1,0:T(8,128)(2,1)}, bf16[2,2,2,64,512]{4,3,2,1,0:T(8,128)(2,1)}, u32[]{:S(2)}, u32[]{:S(2)}) collective-permute-start(bf16[2,2,2,64,512]{4,3,2,1,0:T(8,128)(2,1)} %get-tuple-element.35), channel_id=1, source_target_pairs={{0,32},{8,40},{16,48},{24,56},{32,0},{40,8},{48,16},{56,24},{1,33}... | collective-permute-start | bytes 1572872 | tf_op jit(solution)/shard_map/ppermute | solution.py:297
  194.7 189.5 %all-to-all-start.2 = ((bf16[128,3,16,384]{3,2,1,0:T(8,128)(2,1)}), bf16[128,3,16,384]{3,2,1,0:T(8,128)(2,1)}, u32[]{:S(2)}, u32[]{:S(2)}) async-start(bf16[128,3,16,384]{3,2,1,0:T(8,128)(2,1)} %bitcast.51), calls=%async_computation.3 | async-start | bytes 9437184 | tf_op jit(solution)/shard_map/all_to_all | solution.py:229
  211.4 163.4 %reduce-scatter.2.cloned.1.call-start = ((), (), s32[]{:S(2)}) async-start(), calls=%async_computation.4 | async-start | bytes 2359296 | tf_op jit(solution)/shard_map/reduce_scatter | solution.py:355
  211.5 35.5 %collective-permute-start.9 = (bf16[2,2,2,64,512]{4,3,2,1,0:T(8,128)(2,1)S(1)}, bf16[2,2,2,64,512]{4,3,2,1,0:T(8,128)(2,1)S(1)}, u32[]{:S(2)}, u32[]{:S(2)}) collective-permute-start(bf16[2,2,2,64,512]{4,3,2,1,0:T(8,128)(2,1)S(1)} %copy-done.18), channel_id=1, source_target_pairs={{0,48},{8,56},{16,32},{24,40},{32,16},{40,24},{48,0},{56,8},{1,49}... | collective-permute-start | bytes 1572872 | tf_op jit(solution)/shard_map/ppermute | solution.py:297
  214.3 49.2 %collective-permute-start.10 = (bf16[2,2,2,64,512]{4,3,2,1,0:T(8,128)(2,1)}, bf16[2,2,2,64,512]{4,3,2,1,0:T(8,128)(2,1)S(1)}, u32[]{:S(2)}, u32[]{:S(2)}) collective-permute-start(bf16[2,2,2,64,512]{4,3,2,1,0:T(8,128)(2,1)} %get-tuple-element.38), channel_id=1, source_target_pairs={{0,16},{8,24},{16,0},{24,8},{32,48},{40,56},{48,32},{56,40},{1,17}... | collective-permute-start | bytes 1572872 | tf_op jit(solution)/shard_map/ppermute | solution.py:297
  215.2 57.7 %collective-permute-start.11 = (bf16[2,2,2,64,512]{4,3,2,1,0:T(8,128)(2,1)}, bf16[2,2,2,64,512]{4,3,2,1,0:T(8,128)(2,1)S(1)}, u32[]{:S(2)}, u32[]{:S(2)}) collective-permute-start(bf16[2,2,2,64,512]{4,3,2,1,0:T(8,128)(2,1)} %get-tuple-element.39), channel_id=1, source_target_pairs={{0,56},{8,32},{16,40},{24,48},{32,24},{40,0},{48,8},{56,16},{1,57}... | collective-permute-start | bytes 1572872 | tf_op jit(solution)/shard_map/ppermute | solution.py:297
  219.0 74.7 %collective-permute-start.12 = (bf16[2,2,2,64,512]{4,3,2,1,0:T(8,128)(2,1)}, bf16[2,2,2,64,512]{4,3,2,1,0:T(8,128)(2,1)S(1)}, u32[]{:S(2)}, u32[]{:S(2)}) collective-permute-start(bf16[2,2,2,64,512]{4,3,2,1,0:T(8,128)(2,1)} %get-tuple-element.40), channel_id=1, source_target_pairs={{0,40},{8,48},{16,56},{24,32},{32,8},{40,16},{48,24},{56,0},{1,41}... | collective-permute-start | bytes 1572872 | tf_op jit(solution)/shard_map/ppermute | solution.py:297
  219.0 86.6 %collective-permute-start.13 = (bf16[2,2,2,64,512]{4,3,2,1,0:T(8,128)(2,1)}, bf16[2,2,2,64,512]{4,3,2,1,0:T(8,128)(2,1)S(1)}, u32[]{:S(2)}, u32[]{:S(2)}) collective-permute-start(bf16[2,2,2,64,512]{4,3,2,1,0:T(8,128)(2,1)} %get-tuple-element.41), channel_id=1, source_target_pairs={{0,24},{8,0},{16,8},{24,16},{32,56},{40,32},{48,40},{56,48},{1,25}... | collective-permute-start | bytes 1572872 | tf_op jit(solution)/shard_map/ppermute | solution.py:297
  247.0 66.2 %copy-start.2 = (bf16[2,2,2,64,512]{4,3,2,1,0:T(8,128)(2,1)}, bf16[2,2,2,64,512]{4,3,2,1,0:T(8,128)(2,1)S(1)}, u32[]{:S(2)}) copy-start(bf16[2,2,2,64,512]{4,3,2,1,0:T(8,128)(2,1)S(1)} %collective-permute-done.9.refs_1_) | copy-start | bytes 1572868
  247.0 58.6 %collective-permute-start.14 = (bf16[2,2,2,64,512]{4,3,2,1,0:T(8,128)(2,1)}, bf16[2,2,2,64,512]{4,3,2,1,0:T(8,128)(2,1)S(1)}, u32[]{:S(2)}, u32[]{:S(2)}) collective-permute-start(bf16[2,2,2,64,512]{4,3,2,1,0:T(8,128)(2,1)} %get-tuple-element.42), channel_id=1, source_target_pairs={{0,8},{8,16},{16,24},{24,0},{32,40},{40,48},{48,56},{56,32},{1,9},... | collective-permute-start | bytes 1572872 | tf_op jit(solution)/shard_map/ppermute | solution.py:297
  263.5 49.7 %collective-permute-start.15 = (bf16[2,2,2,64,512]{4,3,2,1,0:T(8,128)(2,1)}, bf16[2,2,2,64,512]{4,3,2,1,0:T(8,128)(2,1)S(1)}, u32[]{:S(2)}, u32[]{:S(2)}) collective-permute-start(bf16[2,2,2,64,512]{4,3,2,1,0:T(8,128)(2,1)} %get-tuple-element.43), channel_id=1, source_target_pairs={{0,32},{8,40},{16,48},{24,56},{32,0},{40,8},{48,16},{56,24},{1,33}... | collective-permute-start | bytes 1572872 | tf_op jit(solution)/shard_map/ppermute | solution.py:297
  318.6 4.4 %collective-permute-start.16 = (bf16[8,2,2,2,32,512]{5,4,3,2,1,0:T(8,128)(2,1)}, bf16[8,2,2,2,32,512]{5,4,3,2,1,0:T(8,128)(2,1)S(1)}, u32[]{:S(2)}, u32[]{:S(2)}) collective-permute-start(bf16[8,2,2,2,32,512]{5,4,3,2,1,0:T(8,128)(2,1)} %shard_map.130), channel_id=1, source_target_pairs={{0,64},{64,0},{1,65},{65,1},{2,66},{66,2},{3,67},{67,3},{4,68},{68... | collective-permute-start | bytes 6291464 | tf_op jit(solution)/shard_map/ppermute | solution.py:354
  375.7 6.6 %collective-permute-start.17 = (bf16[128,512]{1,0:T(8,128)(2,1)S(1)}, bf16[128,512]{1,0:T(8,128)(2,1)S(1)}, u32[]{:S(2)}, u32[]{:S(2)}) collective-permute-start(bf16[128,512]{1,0:T(8,128)(2,1)S(1)} %slice.48), channel_id=1, source_target_pairs={{0,128},{128,0},{1,129},{129,1},{2,130},{130,2},{3,131},{131,3},{4... | collective-permute-start | bytes 393224 | tf_op jit(solution)/shard_map/ppermute | solution.py:357
  (18 other events, 364.8 us)
Sparse Core Ops, SparseCore 0:
  32.4 60.8 all-gather.2
  329.3 45.4 reduce-scatter.1
